TPU v7x, 32 devices: a whole 2x2x4 slice. The times are simulated.
32 devices in a mesh: seq: 8 (over z, y), head: 2 (over x), dp: 2 (over core).
Axes of the slice: x: 2, y: 2, z: 4, core: 2. Of those that a mesh axis runs over, the one named last changes fastest.
Arguments:
- queries: bfloat16 [2048, 4096], P(('dp', 'seq'), 'head'), parts along dimension 0, may hold values from -6 to 6
- key_vectors: bfloat16 [2048, 4096], P(('dp', 'seq'), 'head'), parts along dimension 0, may hold values from -6 to 6
- value_vectors: bfloat16 [2048, 4096], P(('dp', 'seq'), 'head'), parts along dimension 0, may hold values from -6 to 6
- grad_out: bfloat16 [2048, 4096], P(('dp', 'seq'), 'head'), parts along dimension 0, may hold values from -6 to 6
Outputs:
- grad_queries: bfloat16 [2048, 4096], P(('dp', 'seq'), 'head'), parts along dimension 0
- grad_keys: bfloat16 [2048, 4096], P(('dp', 'seq'), 'head'), parts along dimension 0
- grad_values: bfloat16 [2048, 4096], P(('dp', 'seq'), 'head'), parts along dimension 0
There are 2 independent parts, one for each index of `dp`. A program takes and returns all parts, laid end to end along the dimension named above; each array names one. Nothing has to cross between parts.
All inputs are finite; a program needn't handle non-finite values.
Results may differ from a plain program's by a relative error of at most 0.012.
Values may be sent and summed in bfloat16 or wider, within the bound.
No kernel may reach another device: no remote copies, remote signals or barrier semaphores. Data moves between devices by JAX's collectives and lax.ppermute only.
A program may use at most 128 MiB of HBM per device.

v0:
```python
import jax
import jax.numpy as jnp
from jax import lax
from jax.sharding import PartitionSpec as P

E = 128
B = 128


masked_value = -1e30


def passed_along(block, axis, distance):
    devices = range(lax.axis_size(axis))
    route = [(i - distance, i) for i in devices if i - distance in devices]
    return lax.ppermute(block, axis, route)


def prefix(part, axis, combine, identity):
    count = lax.axis_size(axis)
    place = lax.axis_index(axis)
    ahead = count - 1 - place
    gathered = jax.tree.map(lambda a: lax.all_gather(a, axis), part)
    state = jax.tree.map(lambda a, e: jnp.zeros_like(a) + jnp.asarray(e, a.dtype), part, identity)

    def one(turn, state):
        source = count - 1 - turn
        return combine(
            state, jax.tree.map(lambda a: lax.dynamic_index_in_dim(a, source, 0, False), gathered)
        )

    return lax.fori_loop(0, ahead, one, state)


def scores(query_part, key_part, allowed):
    scaling = query_part.shape[2] ** (-0.5)
    logits = (
        jnp.einsum("qhe,khe->hqk", query_part, key_part, preferred_element_type=jnp.float32)
        * scaling
    )
    return jnp.where(allowed[None], logits, masked_value)


def backward_terms(query_part, value_part, grad_part, logits, log_total, inner_term):
    scaling = query_part.shape[2] ** (-0.5)
    probs = jnp.exp(logits - log_total)
    probs_low = probs.astype(jnp.bfloat16)
    grad_probs = jnp.einsum(
        "qhe,khe->hqk", grad_part, value_part, preferred_element_type=jnp.float32
    )
    grad_logits = (probs * (grad_probs - inner_term)).astype(jnp.bfloat16)
    grad_keyset = scaling * jnp.einsum(
        "hqk,qhe->khe", grad_logits, query_part, preferred_element_type=jnp.float32
    )
    grad_valset = jnp.einsum(
        "hqk,qhe->khe", probs_low, grad_part, preferred_element_type=jnp.float32
    )
    return (grad_logits, grad_keyset, grad_valset)


def attend_back(query_part, key_part, value_part, grad_part, allowed):
    scaling = query_part.shape[2] ** (-0.5)
    logits = scores(query_part, key_part, allowed)
    row_max = jnp.max(logits, axis=2, keepdims=True)
    log_total = row_max + jnp.log(jnp.sum(jnp.exp(logits - row_max), axis=2, keepdims=True))
    probs_low = jnp.exp(logits - log_total).astype(jnp.bfloat16)
    output = jnp.einsum("hqk,khe->qhe", probs_low, value_part, preferred_element_type=jnp.float32)
    inner_term = jnp.einsum("qhe,qhe->hq", grad_part.astype(jnp.float32), output)[:, :, None]
    grad_logits, grad_keyset, grad_valset = backward_terms(
        query_part, value_part, grad_part, logits, log_total, inner_term
    )
    grad_query = scaling * jnp.einsum(
        "hqk,khe->qhe", grad_logits, key_part, preferred_element_type=jnp.float32
    )
    return (grad_query, grad_keyset, grad_valset, log_total, inner_term)


def add_pair(earlier, later):
    return (earlier[0] + later[0], earlier[1] + later[1])


def body(queries, key_vectors, value_vectors, grad_out):
    shard_len, feature_count = queries.shape
    head_count = feature_count // E
    block_count = shard_len // B
    offset = lax.axis_index("seq") * shard_len
    query_heads = queries.reshape(shard_len, head_count, E)
    key_heads = key_vectors.reshape(shard_len, head_count, E)
    value_heads = value_vectors.reshape(shard_len, head_count, E)
    grad_heads = grad_out.reshape(shard_len, head_count, E)
    halo_key, halo_value = passed_along((key_heads, value_heads), "seq", 1)
    key_blocks = key_heads.reshape(block_count, B, head_count, E)
    value_blocks = value_heads.reshape(block_count, B, head_count, E)
    query_blocks = query_heads.reshape(block_count, B, head_count, E)
    grad_blocks = grad_heads.reshape(block_count, B, head_count, E)
    strided_key = key_blocks[:, B - 1]
    strided_value = value_blocks[:, B - 1]
    summary_key, summary_value = (
        lax.all_gather(strided_key, "seq", axis=0, tiled=True),
        lax.all_gather(strided_value, "seq", axis=0, tiled=True),
    )
    summary_count = summary_key.shape[0]
    key_before = jnp.concatenate([halo_key[None], key_blocks[:-1]], axis=0)
    value_before = jnp.concatenate([halo_value[None], value_blocks[:-1]], axis=0)
    steps_b = jnp.arange(B, dtype=jnp.int32)
    summary_pos = jnp.arange(summary_count, dtype=jnp.int32) * B + B - 1
    is_local = jnp.arange(2 * B + summary_count, dtype=jnp.int32) < 2 * B

    def one_block(local_index, query_part, key_prev, key_here, value_prev, value_here, grad_part):
        block_start = offset + local_index * B
        key_set = jnp.concatenate([key_prev, key_here, summary_key], axis=0)
        value_set = jnp.concatenate([value_prev, value_here, summary_value], axis=0)
        query_pos = block_start + steps_b
        key_pos = jnp.concatenate([block_start - B + steps_b, block_start + steps_b, summary_pos])
        near = (
            (key_pos[None, :] > query_pos[:, None] - B)
            & (key_pos[None, :] <= query_pos[:, None])
            & (key_pos[None, :] >= 0)
        )
        far_ok = key_pos[None, :] <= query_pos[:, None] - B
        allowed = jnp.where(is_local[None, :], near, far_ok)
        return attend_back(query_part, key_set, value_set, grad_part, allowed)

    grad_query, grad_keyset, grad_valset, log_total, inner_term = jax.vmap(one_block)(
        jnp.arange(block_count, dtype=jnp.int32),
        query_blocks,
        key_before,
        key_blocks,
        value_before,
        value_blocks,
        grad_blocks,
    )
    empty_grad = jnp.zeros((1, B, head_count, E), jnp.float32)
    own_key = grad_keyset[:, B : 2 * B] + jnp.concatenate([grad_keyset[1:, :B], empty_grad], axis=0)
    own_value = grad_valset[:, B : 2 * B] + jnp.concatenate(
        [grad_valset[1:, :B], empty_grad], axis=0
    )
    back_key, back_value = (
        passed_along(grad_keyset[0, :B].astype(jnp.bfloat16), "seq", -1).astype(jnp.float32),
        passed_along(grad_valset[0, :B].astype(jnp.bfloat16), "seq", -1).astype(jnp.float32),
    )
    own_key = own_key.at[block_count - 1].add(back_key)
    own_value = own_value.at[block_count - 1].add(back_value)
    summary_gk = jnp.sum(grad_keyset[:, 2 * B :], axis=0)
    summary_gv = jnp.sum(grad_valset[:, 2 * B :], axis=0)
    empty_sum = jnp.zeros_like(summary_gk)
    later_key, later_value = prefix(
        (summary_gk, summary_gv), "seq", add_pair, (empty_sum, empty_sum)
    )
    start_row = lax.axis_index("seq") * block_count
    mine_key = lax.dynamic_slice_in_dim(later_key + summary_gk, start_row, block_count, 0)
    mine_value = lax.dynamic_slice_in_dim(later_value + summary_gv, start_row, block_count, 0)
    own_key = own_key.at[:, B - 1].add(mine_key)
    own_value = own_value.at[:, B - 1].add(mine_value)
    return (
        grad_query.reshape(shard_len, feature_count).astype(jnp.bfloat16),
        own_key.reshape(shard_len, feature_count).astype(jnp.bfloat16),
        own_value.reshape(shard_len, feature_count).astype(jnp.bfloat16),
    )


def solution(mesh):
    return jax.shard_map(
        body,
        mesh=mesh,
        in_specs=(
            P(("dp", "seq"), "head"),
            P(("dp", "seq"), "head"),
            P(("dp", "seq"), "head"),
            P(("dp", "seq"), "head"),
        ),
        out_specs=(P(("dp", "seq"), "head"), P(("dp", "seq"), "head"), P(("dp", "seq"), "head")),
        check_vma=False,
    )
```

profile of v0, /device:TPU:0, one launch (start us, length us, event | category | flops | bytes accessed | tf_op | source)
XLA Modules:
  0.0 187.8 jit_solution(2531822382661108834)
XLA Ops:
  0.7 1.4 copy.41
  2.3 5.7 %collective-permute-start = (bf16[128,16,128]{2,0,1:T(8,128)(2,1)S(1)}, bf16[128,16,128]{2,0,1:T(8,128)(2,1)}, u32[]{:S(2)}, u32[]{:S(2)}) collective-permute-start(bf16[128,16,128]{2,0,1:T(8,128)(2,1)S(1)} %copy.42), channel_id=1, source_target_pairs={{0,4},{4,8},{8,12},{12,16},{16,20},{20,24},{24,28},{1,5},{5,9},{9,... | collective-permute-start | bytes 1572872 | tf_op jit(solution)/shard_map/ppermute | solution.py:16
  8.3 1.0 copy.49
  9.3 3.4 %collective-permute-start.1 = (bf16[128,16,128]{2,0,1:T(8,128)(2,1)}, bf16[128,16,128]{2,0,1:T(8,128)(2,1)}, u32[]{:S(2)}, u32[]{:S(2)}) collective-permute-start(bf16[128,16,128]{2,0,1:T(8,128)(2,1)} %copy.49), channel_id=1, source_target_pairs={{0,4},{4,8},{8,12},{12,16},{16,20},{20,24},{24,28},{1,5},{5,9},{9,... | collective-permute-start | bytes 1572872 | tf_op jit(solution)/shard_map/ppermute | solution.py:16
  13.0 1.0 copy.46
  14.2 1.0 copy.53
  15.4 40.1 %all-gather = bf16[8,1,16,128]{3,2,1,0:T(8,128)(2,1)S(1)} all-gather(bf16[1,1,16,128]{3,2,1,0:T(8,128)(2,1)S(1)} %copy.44), channel_id=2, replica_groups=mesh['seq'=8,'head'=2,'dp'=2] {'seq'}, dimensions={0}, use_global_device_ids=true | all-gather | bytes 36864 | tf_op jit(solution)/shard_map/all_gather | solution.py:99
  55.8 30.4 %all-gather.1 = bf16[8,1,16,128]{3,2,1,0:T(8,128)(2,1)S(1)} all-gather(bf16[1,1,16,128]{3,2,1,0:T(8,128)(2,1)S(1)} %copy.51), channel_id=3, replica_groups=mesh['seq'=8,'head'=2,'dp'=2] {'seq'}, dimensions={0}, use_global_device_ids=true | all-gather | bytes 36864 | tf_op jit(solution)/shard_map/all_gather | solution.py:100
  86.2 0.9 copy.75
  87.4 1.9 %fusion.24 = (f32[16,128]{1,0:T(8,128)S(1)}, f32[16,128,264]{1,2,0:T(8,128)S(1)}) fusion(bf16[1,8,16,128]{3,1,2,0:T(8,128)(2,1)S(1)} %bitcast.126, bf16[1,128,16,128]{3,1,2,0:T(8,128)(2,1)} %copy.46, bf16[1,128,16,128]{3,1,2,0:T(8,128)(2,1)} %bitcast.5, pred[128,264]{0,1:T(8,128)(4,1)S(1)} %compare_select_fusion, bf16[128,2048]{1,0:T(8,128)(2,1)S(1)} %copy-done), kind=kOutput, calls=%fused_computation.55 | convolution fusion | flops 143276032 | bytes 3810304 | tf_op jit(solution)/shard_map/vmap(qhe,khe->hqk)/dot_general | solution.py:38
  89.7 0.7 copy-done.7
  90.4 2.9 %convolution_bitcast_fusion.1 = f32[16,128,128]{1,2,0:T(8,128)} fusion(bf16[1,8,16,128]{3,1,2,0:T(8,128)(2,1)S(1)} %bitcast.128, bf16[1,128,16,128]{3,1,2,0:T(8,128)(2,1)S(1)} %copy-done.7, bf16[1,128,16,128]{3,1,2,0:T(8,128)(2,1)} %bitcast.11, f32[16,128,264]{1,2,0:T(8,128)S(1)} %get-tuple-element.174, f32[16,128]{1,0:T(8,128)S(1)} %log_add_fusion), kind=kOutput, calls=%fused_computation.11 | convolution fusion | flops 142737408 | bytes 4300800 | tf_op jit(solution)/shard_map/vmap(hqk,khe->qhe)/dot_general | solution.py:67
  93.2 2.6 %copy.71 = f32[16,128,128]{2,0,1:T(8,128)} copy(f32[16,128,128]{1,2,0:T(8,128)} %convolution_bitcast_fusion.1) | data formatting | bytes 2097152
  95.8 1.7 multiply_reduce_fusion
  97.6 1.9 %fusion = bf16[16,128,264]{1,2,0:T(8,128)(2,1)S(1)} fusion(f32[16,128,264]{1,2,0:T(8,128)S(1)} %get-tuple-element.174, f32[16,128]{1,0:T(8,128)S(1)} %copy.72, f32[16,128]{1,0:T(8,128)S(1)} %log_add_fusion, bf16[1,8,16,128]{3,1,2,0:T(8,128)(2,1)S(1)} %bitcast.129, bf16[1,128,16,128]{3,1,2,0:T(8,128)(2,1)} %copy.53, bf16[1,128,16,128]{3,1,2,0:T(8,128)(2,1)} %bitcast.11, ...), kind=kOutput, calls=%fused_computation.3 | convolution fusion | flops 143818752 | bytes 4866048 | tf_op jit(solution)/shard_map/vmap(qhe,khe->hqk)/dot_general | solution.py:48
  99.6 0.7 multiply_bitcast_fusion
  100.3 1.0 fusion.3
  101.3 0.4 copy-done.2
  101.8 0.7 convolution_bitcast_fusion
  102.5 1.3 collective-permute-start.2
  103.9 35.6 %all_gather.16 = f32[8,8,16,128]{3,2,1,0:T(8,128)S(1)} all-gather(f32[1,8,16,128]{3,2,1,0:T(8,128)S(1)} %copy.56), channel_id=1, replica_groups=mesh['seq'=8,'head'=2,'dp'=2] {'seq'}, dimensions={0}, use_global_device_ids=true | all-gather | bytes 589824 | tf_op jit(solution)/shard_map/all_gather | solution.py:23
  139.5 31.6 %all_gather.17 = f32[8,8,16,128]{3,2,1,0:T(8,128)S(1)} all-gather(f32[1,8,16,128]{3,2,1,0:T(8,128)S(1)} %copy.58), channel_id=1, replica_groups=mesh['seq'=8,'head'=2,'dp'=2] {'seq'}, dimensions={0}, use_global_device_ids=true | all-gather | bytes 589824 | tf_op jit(solution)/shard_map/all_gather | solution.py:23
  171.1 0.4 while.18
  171.5 2.1 %fusion.4 = bf16[128,16,128]{2,0,1:T(8,128)(2,1)} fusion(f32[1,264,16,128]{3,1,2,0:T(8,128)} %copy-done.1), kind=kLoop, calls=%fused_computation.21 | loop fusion | bytes 1048576 | tf_op jit(solution)/shard_map/convert_element_type | solution.py:140
  173.7 1.3 collective-permute-start.3
  175.0 2.7 %fusion.2 = bf16[16,128,128]{2,1,0:T(8,128)(2,1)} fusion(bf16[16,128,264]{1,2,0:T(8,128)(2,1)S(1)} %copy-done.5, bf16[1,8,16,128]{3,1,2,0:T(8,128)(2,1)S(1)} %bitcast.127, bf16[1,128,16,128]{3,1,2,0:T(8,128)(2,1)} %copy.46, bf16[1,128,16,128]{3,1,2,0:T(8,128)(2,1)} %bitcast.5), kind=kOutput, calls=%fused_computation.12 | convolution fusion | flops 142180352 | bytes 2686976 | tf_op jit(solution)/shard_map/vmap(hqk,khe->qhe)/dot_general | solution.py:72
  177.6 2.0 %copy.63 = bf16[128,2048]{1,0:T(8,128)(2,1)} copy(bf16[128,2048]{0,1:T(8,128)(2,1)} %bitcast.125) | data formatting | bytes 1048576
  179.7 1.3 slice_add_fusion.1
  181.6 1.0 copy.64
  182.6 2.4 %collective-permute-done.3 = bf16[128,16,128]{2,0,1:T(8,128)(2,1)S(1)} collective-permute-done((bf16[128,16,128]{2,0,1:T(8,128)(2,1)}, bf16[128,16,128]{2,0,1:T(8,128)(2,1)S(1)}, u32[]{:S(2)}, u32[]{:S(2)}) %collective-permute-start.3) | collective-permute-done | bytes 524320 | tf_op jit(solution)/shard_map/ppermute | solution.py:16
  184.9 1.3 slice_add_fusion
  186.7 1.0 copy.65
  (58 shorter events, 3.3 us)
Async XLA Ops:
  0.6 86.7 %copy-start = (bf16[128,2048]{1,0:T(8,128)(2,1)S(1)}, bf16[128,2048]{1,0:T(8,128)(2,1)}, u32[]{:S(2)}) copy-start(bf16[128,2048]{1,0:T(8,128)(2,1)} %param.14) | copy-start | bytes 1572868
  0.6 7.4 %copy-start.6 = (bf16[128,2048]{1,0:T(8,128)(2,1)S(1)}, bf16[128,2048]{1,0:T(8,128)(2,1)}, u32[]{:S(2)}) copy-start(bf16[128,2048]{1,0:T(8,128)(2,1)} %param.16) | copy-start | bytes 1572868
  2.3 85.0 %collective-permute-start = (bf16[128,16,128]{2,0,1:T(8,128)(2,1)S(1)}, bf16[128,16,128]{2,0,1:T(8,128)(2,1)}, u32[]{:S(2)}, u32[]{:S(2)}) collective-permute-start(bf16[128,16,128]{2,0,1:T(8,128)(2,1)S(1)} %copy.42), channel_id=1, source_target_pairs={{0,4},{4,8},{8,12},{12,16},{16,20},{20,24},{24,28},{1,5},{5,9},{9,... | collective-permute-start | bytes 1572872 | tf_op jit(solution)/shard_map/ppermute | solution.py:16
  9.3 80.3 %collective-permute-start.1 = (bf16[128,16,128]{2,0,1:T(8,128)(2,1)}, bf16[128,16,128]{2,0,1:T(8,128)(2,1)}, u32[]{:S(2)}, u32[]{:S(2)}) collective-permute-start(bf16[128,16,128]{2,0,1:T(8,128)(2,1)} %copy.49), channel_id=1, source_target_pairs={{0,4},{4,8},{8,12},{12,16},{16,20},{20,24},{24,28},{1,5},{5,9},{9,... | collective-permute-start | bytes 1572872 | tf_op jit(solution)/shard_map/ppermute | solution.py:16
  13.0 73.3 %copy-start.3 = (bf16[128,2048]{1,0:T(8,128)(2,1)S(1)}, bf16[128,2048]{1,0:T(8,128)(2,1)}, u32[]{:S(2)}) copy-start(bf16[128,2048]{1,0:T(8,128)(2,1)} %param.17) | copy-start | bytes 1572868
  89.3 1.0 copy-start.7
  99.5 1.8 copy-start.4
  100.3 1.5 copy-start.2
  102.5 37.0 %copy-start.1 = (f32[1,264,16,128]{3,1,2,0:T(8,128)}, f32[1,264,16,128]{3,1,2,0:T(8,128)S(1)}, u32[]{:S(2)}) copy-start(f32[1,264,16,128]{3,1,2,0:T(8,128)S(1)} %convolution_bitcast_fusion) | copy-start | bytes 6488068
  102.5 77.2 %collective-permute-start.2 = (bf16[128,16,128]{2,0,1:T(8,128)(2,1)}, bf16[128,16,128]{2,0,1:T(8,128)(2,1)S(1)}, u32[]{:S(2)}, u32[]{:S(2)}) collective-permute-start(bf16[128,16,128]{2,0,1:T(8,128)(2,1)} %fusion.3), channel_id=1, source_target_pairs={{4,0},{8,4},{12,8},{16,12},{20,16},{24,20},{28,24},{5,1},{9,5},{13... | collective-permute-start | bytes 1572872 | tf_op jit(solution)/shard_map/ppermute | solution.py:16
  139.5 35.5 %copy-start.5 = (bf16[16,128,264]{1,2,0:T(8,128)(2,1)S(1)}, bf16[16,128,264]{1,2,0:T(8,128)(2,1)}, u32[]{:S(2)}) copy-start(bf16[16,128,264]{1,2,0:T(8,128)(2,1)} %copy-done.4) | copy-start | bytes 3244036
  173.7 11.3 %collective-permute-start.3 = (bf16[128,16,128]{2,0,1:T(8,128)(2,1)}, bf16[128,16,128]{2,0,1:T(8,128)(2,1)S(1)}, u32[]{:S(2)}, u32[]{:S(2)}) collective-permute-start(bf16[128,16,128]{2,0,1:T(8,128)(2,1)} %fusion.4), channel_id=1, source_target_pairs={{4,0},{8,4},{12,8},{16,12},{20,16},{24,20},{28,24},{5,1},{9,5},{13... | collective-permute-start | bytes 1572872 | tf_op jit(solution)/shard_map/ppermute | solution.py:16
where the time goes:
time: 188 us
  blocking collectives  138 us (73%)
  local copies, waits for them, and re-layouts  18.6 us (10%)
  starting transfers between devices  11.7 us (6%)
  matrix products  10.8 us (6%)
  other arithmetic  5.32 us (3%)
  waiting for transfers between devices  2.37 us (1%)
    all_gather x2, blocking collectives, prefix(): gathered = jax.tree.map(lambda a: lax.all_gather(a, axis), part)  67.2 us
    all_gather x1, blocking collectives, body(): lax.all_gather(strided_key, 'seq', axis=0, tiled=True)  40.1 us
    all_gather x1, blocking collectives, body(): lax.all_gather(strided_value, 'seq', axis=0, tiled=True)  30.4 us
    ppermute x4, starting transfers between devices, passed_along(): return lax.ppermute(block, axis, route)  11.7 us
    unnamed x23, local copies, waits for them, and re-layouts  10.4 us
  transfers between devices with their start and end apart: 4, of which 1 were waited for; matrix products, arithmetic and copies ran while one was open for 9% of the time, Pallas kernels for 0%

commit v1 on v0

v1 whole, which is shorter than its diff:
```python
import functools

import jax
import jax.numpy as jnp
from jax import lax
from jax.experimental import pallas as pl
from jax.experimental.pallas import tpu as pltpu
from jax.sharding import PartitionSpec as P

E = 128
B = 128
STAT_ROWS = 16
MASKED = -1e30
F32 = jnp.float32
BF16 = jnp.bfloat16


def dot(a, b, contract):
    return lax.dot_general(a, b, (contract, ((), ())), preferred_element_type=F32)


def heads_per_step(heads):
    return 4 if heads % 4 == 0 else 1


def passed_along(block, distance):
    count = lax.axis_size("seq")
    route = [(i - distance, i) for i in range(count) if 0 <= i - distance < count]
    return lax.ppermute(block, "seq", route)


def own_stats_kernel(group, heads, q_ref, k_ref, v_ref, g_ref, out_ref):
    key = lax.broadcasted_iota(jnp.int32, (B, B), 0)
    query = lax.broadcasted_iota(jnp.int32, (B, B), 1)
    allowed = key <= query
    first = pl.program_id(0) * group
    for j in range(group):
        cols = slice(j * E, (j + 1) * E)
        q, k, v, g = q_ref[:, cols], k_ref[:, cols], v_ref[:, cols], g_ref[:, cols]
        logits = jnp.where(allowed, dot(k, q, ((1,), (1,))) * E**-0.5, MASKED)
        top = jnp.max(logits, axis=0, keepdims=True)
        weight = jnp.exp(logits - top)
        total = jnp.sum(weight, axis=0, keepdims=True)
        inner = jnp.sum(weight * dot(v, g, ((1,), (1,))), axis=0, keepdims=True)
        out_ref[pl.ds(first + j, 1), :] = top + jnp.log(total)
        out_ref[pl.ds(heads + first + j, 1), :] = inner / total


def in_three(x):
    high = x.astype(BF16).astype(F32)
    middle = (x - high).astype(BF16).astype(F32)
    low = (x - high - middle).astype(BF16).astype(F32)
    return [high, middle, low]


def cross_kernel(
    group, heads, count, place_ref, q_ref, g_ref, k_ref, v_ref, stats_ref, summary_ref,
    gq_ref, gk_ref, gv_ref, gs_ref, rows, sums
):
    place = place_ref[0]
    step = pl.program_id(0)
    padded = sums.shape[0] // (2 * heads)
    scale = E**-0.5

    @pl.when(step == 0)
    def _():
        rows[...] = summary_ref[...].astype(F32).reshape(rows.shape)

    key = lax.broadcasted_iota(jnp.int32, (B + padded, B), 0)
    query = lax.broadcasted_iota(jnp.int32, (B + padded, B), 1)
    allowed = ((key < B) & ((key > query) | (key == B - 1))) | ((key >= B) & (key - B < place))

    def summary(row):
        part = rows[pl.ds(row, count, stride=2 * heads), :]
        if padded > count:
            part = jnp.concatenate([part, jnp.zeros((padded - count, E), F32)], axis=0)
        return part.astype(BF16)

    for j in range(group):
        head = step * group + j
        cols = slice(j * E, (j + 1) * E)
        q, g = q_ref[:, cols], g_ref[:, cols]
        k = jnp.concatenate([k_ref[:, cols], summary(head)], axis=0)
        v = jnp.concatenate([v_ref[:, cols], summary(heads + head)], axis=0)
        logits = jnp.where(allowed, dot(k, q, ((1,), (1,))) * scale, MASKED)
        grad_probs = dot(v, g, ((1,), (1,)))
        own_log = stats_ref[pl.ds(head, 1), :]
        own_inner = stats_ref[pl.ds(heads + head, 1), :]
        top = jnp.maximum(jnp.max(logits, axis=0, keepdims=True), own_log)
        weight = jnp.exp(logits - top)
        own_weight = jnp.exp(own_log - top)
        total = own_weight + jnp.sum(weight, axis=0, keepdims=True)
        part = 1.0 / total
        inner = part * (
            own_weight * own_inner + jnp.sum(weight * grad_probs, axis=0, keepdims=True)
        )
        probs = weight * part
        probs_low = probs.astype(BF16)
        grad_logits = (probs * (grad_probs - inner)).astype(BF16)
        gq_ref[:B, cols] = (scale * dot(grad_logits, k, ((0,), (0,)))).astype(BF16)
        stats = in_three(top + jnp.log(total)) + in_three(inner)
        stats.append(jnp.zeros((STAT_ROWS - len(stats), E), F32))
        gq_ref[B:, cols] = jnp.concatenate(stats, axis=0).astype(BF16)
        grad_k = scale * dot(grad_logits, q, ((1,), (0,)))
        grad_v = dot(probs_low, g, ((1,), (0,)))
        gk_ref[:, cols] = grad_k[:B]
        gv_ref[:, cols] = grad_v[:B]
        sums[pl.ds(pl.multiple_of(head * padded, padded), padded), :] = grad_k[B:]
        sums[pl.ds(pl.multiple_of((heads + head) * padded, padded), padded), :] = grad_v[B:]

    @pl.when(step == pl.num_programs(0) - 1)
    def _():
        for t in range(count):
            gs_ref[t] = sums[pl.ds(t, 2 * heads, stride=padded), :]


def final_kernel(
    group, heads, place_ref, q_ref, g_ref, k_ref, v_ref, own_ref, back_ref, gk_ref, gv_ref,
    gs_ref, out_q_ref, out_k_ref, out_v_ref, sums
):
    place = place_ref[0]
    step = pl.program_id(0)
    scale = E**-0.5

    @pl.when(step == 0)
    def _():
        sums[...] = jnp.sum(gs_ref[...], axis=0)

    key = lax.broadcasted_iota(jnp.int32, (B, B), 0)
    query = lax.broadcasted_iota(jnp.int32, (B, B), 1)
    allowed = key <= query
    last_row = key == B - 1
    for j in range(group):
        head = step * group + j
        cols = slice(j * E, (j + 1) * E)
        q, k, v, g = q_ref[:, cols], k_ref[:, cols], v_ref[:, cols], g_ref[:, cols]
        sent = back_ref[B:, cols].astype(F32)
        log_total = sent[0:1] + sent[1:2] + sent[2:3]
        inner = sent[3:4] + sent[4:5] + sent[5:6]
        log_total = jnp.where(place == 0, own_ref[pl.ds(head, 1), :], log_total)
        inner = jnp.where(place == 0, own_ref[pl.ds(heads + head, 1), :], inner)
        logits = jnp.where(allowed, dot(k, q, ((1,), (1,))) * scale, MASKED)
        probs = jnp.exp(logits - log_total)
        probs_low = probs.astype(BF16)
        grad_logits = (probs * (dot(v, g, ((1,), (1,))) - inner)).astype(BF16)
        grad_q = scale * dot(grad_logits, k, ((0,), (0,))) + back_ref[:B, cols].astype(F32)
        grad_k = scale * dot(grad_logits, q, ((1,), (0,))) + gk_ref[:, cols]
        grad_v = dot(probs_low, g, ((1,), (0,))) + gv_ref[:, cols]
        grad_k += jnp.where(last_row, sums[pl.ds(head, 1), :], 0.0)
        grad_v += jnp.where(last_row, sums[pl.ds(heads + head, 1), :], 0.0)
        out_q_ref[:, cols] = grad_q.astype(BF16)
        out_k_ref[:, cols] = grad_k.astype(BF16)
        out_v_ref[:, cols] = grad_v.astype(BF16)


def body(queries, key_vectors, value_vectors, grad_out):
    shard_len, features = queries.shape
    assert shard_len == B
    heads = features // E
    group = heads_per_step(heads)
    steps = heads // group
    count = lax.axis_size("seq")
    padded = -(-count // 16) * 16
    place = lax.axis_index("seq").astype(jnp.int32).reshape(1)

    def columns(rows):
        return pl.BlockSpec((rows, group * E), lambda i, *_: (0, i))

    def whole(*shape):
        return pl.BlockSpec(shape, lambda i, *_: (0,) * len(shape))

    block = columns(B)
    wide = jax.ShapeDtypeStruct((B, features), BF16)
    wide_f32 = jax.ShapeDtypeStruct((B, features), F32)
    flops = 2 * heads * B * B * E

    next_q = passed_along(queries, -1)
    next_g = passed_along(grad_out, -1)

    own_stats = pl.pallas_call(
        functools.partial(own_stats_kernel, group, heads),
        grid=(steps,),
        in_specs=[block] * 4,
        out_specs=whole(2 * heads, B),
        out_shape=jax.ShapeDtypeStruct((2 * heads, B), F32),
        cost_estimate=pl.CostEstimate(
            flops=2 * flops, bytes_accessed=4 * B * features * 2, transcendentals=heads * B * B
        ),
        name="own_stats",
    )(queries, key_vectors, value_vectors, grad_out)
    next_stats = passed_along(own_stats, -1)

    last_rows = jnp.concatenate(
        [key_vectors[B - 1].reshape(heads, E), value_vectors[B - 1].reshape(heads, E)], axis=0
    )
    summary = lax.all_to_all(
        jnp.broadcast_to(last_rows[None], (count, 2 * heads, E)), "seq", 0, 0, tiled=True
    )

    grad_q_next, grad_k, grad_v, grad_summary = pl.pallas_call(
        functools.partial(cross_kernel, group, heads, count),
        grid_spec=pltpu.PrefetchScalarGridSpec(
            num_scalar_prefetch=1,
            grid=(steps,),
            in_specs=[block] * 4 + [whole(2 * heads, B), whole(count, 2 * heads, E)],
            out_specs=[columns(B + STAT_ROWS), block, block, whole(count, 2 * heads, E)],
            scratch_shapes=[
                pltpu.VMEM((count * 2 * heads, E), F32),
                pltpu.VMEM((padded * 2 * heads, E), F32),
            ],
        ),
        out_shape=[
            jax.ShapeDtypeStruct((B + STAT_ROWS, features), BF16),
            wide_f32,
            wide_f32,
            jax.ShapeDtypeStruct((count, 2 * heads, E), F32),
        ],
        cost_estimate=pl.CostEstimate(
            flops=5 * flops, bytes_accessed=9 * B * features * 2, transcendentals=heads * B * B
        ),
        name="cross",
    )(place, next_q, next_g, key_vectors, value_vectors, next_stats, summary)

    back = passed_along(grad_q_next, 1)
    grad_summary = lax.all_to_all(grad_summary, "seq", 0, 0, tiled=True)

    return pl.pallas_call(
        functools.partial(final_kernel, group, heads),
        grid_spec=pltpu.PrefetchScalarGridSpec(
            num_scalar_prefetch=1,
            grid=(steps,),
            in_specs=[block] * 4
            + [
                whole(2 * heads, B),
                columns(B + STAT_ROWS),
                block,
                block,
                whole(count, 2 * heads, E),
            ],
            out_specs=[block] * 3,
            scratch_shapes=[pltpu.VMEM((2 * heads, E), F32)],
        ),
        out_shape=[wide, wide, wide],
        cost_estimate=pl.CostEstimate(
            flops=5 * flops, bytes_accessed=12 * B * features * 2, transcendentals=heads * B * B
        ),
        name="final",
    )(
        place,
        queries,
        grad_out,
        key_vectors,
        value_vectors,
        own_stats,
        back,
        grad_k,
        grad_v,
        grad_summary,
    )


def solution(mesh):
    spec = P(("dp", "seq"), "head")
    return jax.shard_map(
        body,
        mesh=mesh,
        in_specs=(spec,) * 4,
        out_specs=(spec,) * 3,
        check_vma=False,
    )
```

time: 188 us -> 68 us (0.36)
  the two profiles are of different devices: /device:TPU:0 before, /device:TPU:8 now
where the time goes in v1:
time: 68 us; the launch traced here: 67.3 us
  starting transfers between devices  18.7 us (28%)
  Pallas kernels  18.6 us (27%)
  blocking collectives  16.2 us (24%)
  waiting for transfers between devices  9.06 us (13%)
  local copies, waits for them, and re-layouts  4.01 us (6%)
  between operations  0.7 us (1%)
    all_to_all x1, blocking collectives, body(): grad_summary = lax.all_to_all(grad_summary, 'seq', 0, 0, tiled=True)  16.2 us
    ppermute x4, starting transfers between devices, passed_along(): return lax.ppermute(block, 'seq', route)  11.9 us
    pallas_call x1, Pallas kernels, body(): pl.pallas_call(functools.partial(cross_kernel, group, heads, count), grid...  7.89 us
    pallas_call x1, Pallas kernels, body(): pl.pallas_call(functools.partial(final_kernel, group, heads), grid_spec=p...  6.85 us
    all_to_all x1, starting transfers between devices, body(): lax.all_to_all(jnp.broadcast_to(last_rows[None], (count, 2 * heads, E)),...  6.8 us
    ppermute x4, waiting for transfers between devices, passed_along(): return lax.ppermute(block, 'seq', route)  6.52 us
    pallas_call x1, Pallas kernels, body(): pl.pallas_call(functools.partial(own_stats_kernel, group, heads), grid=(s...  3.88 us
    all_to_all x1, waiting for transfers between devices, body(): lax.all_to_all(jnp.broadcast_to(last_rows[None], (count, 2 * heads, E)),...  2.54 us
  transfers between devices with their start and end apart: 5, of which 2 were waited for; matrix products, arithmetic and copies ran while one was open for 3% of the time, Pallas kernels for 6%

profile of v1, /device:TPU:8, one launch (start us, length us, event | category | flops | bytes accessed | tf_op | source)
XLA Modules:
  0.0 67.3 jit_solution(3959551173196223351)
XLA Ops:
  0.6 3.3 %collective-permute-start = (bf16[128,2048]{1,0:T(8,128)(2,1)}, bf16[128,2048]{1,0:T(8,128)(2,1)S(1)}, u32[]{:S(2)}, u32[]{:S(2)}) collective-permute-start(bf16[128,2048]{1,0:T(8,128)(2,1)} %q_ref.3), channel_id=1, source_target_pairs={{4,0},{8,4},{12,8},{16,12},{20,16},{24,20},{28,24},{5,1},{9,5},{13... | collective-permute-start | bytes 1572872 | tf_op jit(solution)/shard_map/ppermute | solution.py:29
  4.0 1.9 %collective-permute-start.1 = (bf16[128,2048]{1,0:T(8,128)(2,1)}, bf16[128,2048]{1,0:T(8,128)(2,1)S(1)}, u32[]{:S(2)}, u32[]{:S(2)}) collective-permute-start(bf16[128,2048]{1,0:T(8,128)(2,1)} %g_ref.3), channel_id=1, source_target_pairs={{4,0},{8,4},{12,8},{16,12},{20,16},{24,20},{28,24},{5,1},{9,5},{13... | collective-permute-start | bytes 1572872 | tf_op jit(solution)/shard_map/ppermute | solution.py:29
  5.9 0.8 %slice_reduce_fusion.1 = bf16[2048]{0:T(1024)(128)(2,1)S(1)} fusion(bf16[128,2048]{1,0:T(8,128)(2,1)} %k_ref.5), kind=kLoop, calls=%fused_computation.2 | loop fusion | bytes 8192 | tf_op jit(solution)/shard_map/slice | solution.py:194
  6.7 0.8 %slice_reduce_fusion = bf16[2048]{0:T(1024)(128)(2,1)S(1)} fusion(bf16[128,2048]{1,0:T(8,128)(2,1)} %v_ref.5), kind=kLoop, calls=%fused_computation.1 | loop fusion | bytes 8192 | tf_op jit(solution)/shard_map/slice | solution.py:194
  7.5 0.6 broadcast_in_dim.2
  8.1 6.8 %all-to-all-start = ((bf16[8,32,128]{2,1,0:T(8,128)(2,1)}), bf16[8,32,128]{2,1,0:T(8,128)(2,1)S(1)}, u32[]{:S(2)}, u32[]{:S(2)}) async-start(bf16[8,32,128]{2,1,0:T(8,128)(2,1)} %broadcast_in_dim.2), calls=%async_computation | async-start | bytes 131072 | tf_op jit(solution)/shard_map/all_to_all | solution.py:196
  14.9 3.9 %own_stats.1.own_ref = f32[32,128]{1,0:T(8,128)} custom-call(bf16[128,2048]{1,0:T(8,128)(2,1)} %q_ref.3, bf16[128,2048]{1,0:T(8,128)(2,1)} %k_ref.5, bf16[128,2048]{1,0:T(8,128)(2,1)} %v_ref.5, bf16[128,2048]{1,0:T(8,128)(2,1)} %g_ref.3), custom_call_target="tpu_custom_call" | custom-call | flops 134217728 | bytes 2097152 | tf_op jit(solution)/shard_map/own_stats/pallas_call | solution.py:180
  18.8 3.4 %collective-permute-start.2 = (f32[32,128]{1,0:T(8,128)}, f32[32,128]{1,0:T(8,128)S(1)}, u32[]{:S(2)}, u32[]{:S(2)}) collective-permute-start(f32[32,128]{1,0:T(8,128)} %own_stats.1.own_ref), channel_id=1, source_target_pairs={{4,0},{8,4},{12,8},{16,12},{20,16},{24,20},{28,24},{5,1},{9,5},{13... | collective-permute-start | bytes 49160 | tf_op jit(solution)/shard_map/ppermute | solution.py:29
  22.2 6.5 %collective-permute-done.2.stats_ref = f32[32,128]{1,0:T(8,128)S(1)} collective-permute-done((f32[32,128]{1,0:T(8,128)}, f32[32,128]{1,0:T(8,128)S(1)}, u32[]{:S(2)}, u32[]{:S(2)}) %collective-permute-start.2) | collective-permute-done | bytes 16416 | tf_op jit(solution)/shard_map/ppermute | solution.py:29
  28.7 0.0 copy-start.4
  28.7 2.5 %all-to-all-done.summary_ref = bf16[8,32,128]{2,1,0:T(8,128)(2,1)S(1)} async-done(((bf16[8,32,128]{2,1,0:T(8,128)(2,1)}), bf16[8,32,128]{2,1,0:T(8,128)(2,1)S(1)}, u32[]{:S(2)}, u32[]{:S(2)}) %all-to-all-start) | async-done | bytes 65568 | tf_op jit(solution)/shard_map/all_to_all | solution.py:196
  31.2 0.0 copy-start.3
  31.2 0.0 collective-permute-done.q_ref
  31.2 0.0 copy-start.1
  31.2 0.0 collective-permute-done.1.g_ref
  31.2 0.0 copy-start.2
  31.3 0.0 copy-done.4
  31.3 0.6 copy-done.3
  31.9 0.2 copy-done.1
  32.0 0.2 copy-done.2
  32.2 7.9 %cross.1 = (bf16[144,2048]{1,0:T(8,128)(2,1)}, f32[128,2048]{1,0:T(8,128)}, f32[128,2048]{1,0:T(8,128)}, f32[8,32,128]{2,1,0:T(8,128)}) custom-call(s32[1]{0:T(128)} %bitcast.place_ref, bf16[128,2048]{1,0:T(8,128)(2,1)} %copy-done.1, bf16[128,2048]{1,0:T(8,128)(2,1)} %copy-done.2, bf16[128,2048]{1,0:T(8,128)(2,1)} %k_ref.5, bf16[128,2048]{1,0:T(8,128)(2,1)} %v_ref.5, ...), custom_call_target="tpu_custom_call" | custom-call | flops 335544320 | bytes 4718592 | tf_op jit(solution)/shard_map/cross/pallas_call | solution.py:200
  40.1 3.3 %collective-permute-start.3 = (bf16[144,2048]{1,0:T(8,128)(2,1)}, bf16[144,2048]{1,0:T(8,128)(2,1)S(1)}, u32[]{:S(2)}, u32[]{:S(2)}) collective-permute-start(bf16[144,2048]{1,0:T(8,128)(2,1)} %get-tuple-element.7), channel_id=1, source_target_pairs={{0,4},{4,8},{8,12},{12,16},{16,20},{20,24},{24,28},{1,5},{5,9},{9,... | collective-permute-start | bytes 1769480 | tf_op jit(solution)/shard_map/ppermute | solution.py:29
  43.4 16.2 %all_to_all.10.gs_ref = f32[8,32,128]{2,1,0:T(8,128)} all-to-all(f32[8,32,128]{2,1,0:T(8,128)} %get-tuple-element.10), channel_id=1, replica_groups=mesh['seq'=8,'head'=2,'dp'=2] {'seq'}, dimensions={0} | all-to-all | bytes 262144 | tf_op jit(solution)/shard_map/all_to_all | solution.py:225
  59.6 0.0 collective-permute-done.3.back_ref
  59.6 0.0 copy-start
  59.6 0.8 %copy-done = bf16[144,2048]{1,0:T(8,128)(2,1)} copy-done((bf16[144,2048]{1,0:T(8,128)(2,1)}, bf16[144,2048]{1,0:T(8,128)(2,1)S(1)}, u32[]{:S(2)}) %copy-start) | copy-done | bytes 589848
  60.5 6.8 %final.1 = (bf16[128,2048]{1,0:T(8,128)(2,1)}, bf16[128,2048]{1,0:T(8,128)(2,1)}, bf16[128,2048]{1,0:T(8,128)(2,1)}) custom-call(s32[1]{0:T(128)} %bitcast.place_ref, bf16[128,2048]{1,0:T(8,128)(2,1)} %q_ref.3, bf16[128,2048]{1,0:T(8,128)(2,1)} %g_ref.3, bf16[128,2048]{1,0:T(8,128)(2,1)} %k_ref.5, bf16[128,2048]{1,0:T(8,128)(2,1)} %v_ref.5, ...), custom_call_target="tpu_custom_call" | custom-call | flops 335544320 | bytes 6291456 | tf_op jit(solution)/shard_map/final/pallas_call | solution.py:227
  (1 shorter events, 0.0 us)
Async XLA Ops:
  0.6 30.6 %collective-permute-start = (bf16[128,2048]{1,0:T(8,128)(2,1)}, bf16[128,2048]{1,0:T(8,128)(2,1)S(1)}, u32[]{:S(2)}, u32[]{:S(2)}) collective-permute-start(bf16[128,2048]{1,0:T(8,128)(2,1)} %q_ref.3), channel_id=1, source_target_pairs={{4,0},{8,4},{12,8},{16,12},{20,16},{24,20},{28,24},{5,1},{9,5},{13... | collective-permute-start | bytes 1572872 | tf_op jit(solution)/shard_map/ppermute | solution.py:29
  4.0 27.3 %collective-permute-start.1 = (bf16[128,2048]{1,0:T(8,128)(2,1)}, bf16[128,2048]{1,0:T(8,128)(2,1)S(1)}, u32[]{:S(2)}, u32[]{:S(2)}) collective-permute-start(bf16[128,2048]{1,0:T(8,128)(2,1)} %g_ref.3), channel_id=1, source_target_pairs={{4,0},{8,4},{12,8},{16,12},{20,16},{24,20},{28,24},{5,1},{9,5},{13... | collective-permute-start | bytes 1572872 | tf_op jit(solution)/shard_map/ppermute | solution.py:29
  8.1 23.1 %all-to-all-start = ((bf16[8,32,128]{2,1,0:T(8,128)(2,1)}), bf16[8,32,128]{2,1,0:T(8,128)(2,1)S(1)}, u32[]{:S(2)}, u32[]{:S(2)}) async-start(bf16[8,32,128]{2,1,0:T(8,128)(2,1)} %broadcast_in_dim.2), calls=%async_computation | async-start | bytes 131072 | tf_op jit(solution)/shard_map/all_to_all | solution.py:196
  18.8 9.9 %collective-permute-start.2 = (f32[32,128]{1,0:T(8,128)}, f32[32,128]{1,0:T(8,128)S(1)}, u32[]{:S(2)}, u32[]{:S(2)}) collective-permute-start(f32[32,128]{1,0:T(8,128)} %own_stats.1.own_ref), channel_id=1, source_target_pairs={{4,0},{8,4},{12,8},{16,12},{20,16},{24,20},{28,24},{5,1},{9,5},{13... | collective-permute-start | bytes 49160 | tf_op jit(solution)/shard_map/ppermute | solution.py:29
  28.7 2.6 %copy-start.4 = (f32[32,128]{1,0:T(8,128)}, f32[32,128]{1,0:T(8,128)S(1)}, u32[]{:S(2)}) copy-start(f32[32,128]{1,0:T(8,128)S(1)} %collective-permute-done.2.stats_ref) | copy-start | bytes 49156
  31.2 0.6 copy-start.3
  31.2 0.8 %copy-start.1 = (bf16[128,2048]{1,0:T(8,128)(2,1)}, bf16[128,2048]{1,0:T(8,128)(2,1)S(1)}, u32[]{:S(2)}) copy-start(bf16[128,2048]{1,0:T(8,128)(2,1)S(1)} %collective-permute-done.q_ref) | copy-start | bytes 1572868
  31.2 1.0 %copy-start.2 = (bf16[128,2048]{1,0:T(8,128)(2,1)}, bf16[128,2048]{1,0:T(8,128)(2,1)S(1)}, u32[]{:S(2)}) copy-start(bf16[128,2048]{1,0:T(8,128)(2,1)S(1)} %collective-permute-done.1.g_ref) | copy-start | bytes 1572868
  40.1 19.5 %collective-permute-start.3 = (bf16[144,2048]{1,0:T(8,128)(2,1)}, bf16[144,2048]{1,0:T(8,128)(2,1)S(1)}, u32[]{:S(2)}, u32[]{:S(2)}) collective-permute-start(bf16[144,2048]{1,0:T(8,128)(2,1)} %get-tuple-element.7), channel_id=1, source_target_pairs={{0,4},{4,8},{8,12},{12,16},{16,20},{20,24},{24,28},{1,5},{5,9},{9,... | collective-permute-start | bytes 1769480 | tf_op jit(solution)/shard_map/ppermute | solution.py:29
  59.6 0.8 %copy-start = (bf16[144,2048]{1,0:T(8,128)(2,1)}, bf16[144,2048]{1,0:T(8,128)(2,1)S(1)}, u32[]{:S(2)}) copy-start(bf16[144,2048]{1,0:T(8,128)(2,1)S(1)} %collective-permute-done.3.back_ref) | copy-start | bytes 1769476

commit v2 on v1

v2 whole, which is shorter than its diff:
```python
import functools

import jax
import jax.numpy as jnp
from jax import lax
from jax.experimental import pallas as pl
from jax.experimental.pallas import tpu as pltpu
from jax.sharding import PartitionSpec as P

E = 128
B = 128
STAT_ROWS = 16
MASKED = -1e30
F32 = jnp.float32
BF16 = jnp.bfloat16


def dot(a, b, contract):
    return lax.dot_general(a, b, (contract, ((), ())), preferred_element_type=F32)


def passed_along(block, distance):
    count = lax.axis_size("seq")
    route = [(i - distance, i) for i in range(count) if 0 <= i - distance < count]
    return lax.ppermute(block, "seq", route)


def own_stats_kernel(heads, q_ref, k_ref, v_ref, g_ref, out_ref):
    key = lax.broadcasted_iota(jnp.int32, (B, B), 0)
    query = lax.broadcasted_iota(jnp.int32, (B, B), 1)
    allowed = key <= query
    for h in range(heads):
        cols = slice(h * E, (h + 1) * E)
        q, k, v, g = q_ref[:, cols], k_ref[:, cols], v_ref[:, cols], g_ref[:, cols]
        logits = jnp.where(allowed, dot(k, q, ((1,), (1,))) * E**-0.5, MASKED)
        top = jnp.max(logits, axis=0, keepdims=True)
        weight = jnp.exp(logits - top)
        total = jnp.sum(weight, axis=0, keepdims=True)
        inner = jnp.sum(weight * dot(v, g, ((1,), (1,))), axis=0, keepdims=True)
        out_ref[h : h + 1, :] = top + jnp.log(total)
        out_ref[heads + h : heads + h + 1, :] = inner / total


def in_three(x):
    high = x.astype(BF16).astype(F32)
    middle = (x - high).astype(BF16).astype(F32)
    low = (x - high - middle).astype(BF16).astype(F32)
    return [high, middle, low]


def cross_kernel(
    heads, count, place_ref, q_ref, g_ref, k_ref, v_ref, stats_ref, summary_ref,
    gq_ref, gk_ref, gv_ref, gs_ref, rows, sums
):
    place = place_ref[0]
    padded = sums.shape[0] // (2 * heads)
    scale = E**-0.5
    rows[...] = summary_ref[...].astype(F32).reshape(rows.shape)
    key = lax.broadcasted_iota(jnp.int32, (B + padded, B), 0)
    query = lax.broadcasted_iota(jnp.int32, (B + padded, B), 1)
    allowed = ((key < B) & ((key > query) | (key == B - 1))) | ((key >= B) & (key - B < place))

    def summary(row):
        part = rows[pl.ds(row, count, stride=2 * heads), :]
        if padded > count:
            part = jnp.concatenate([part, jnp.zeros((padded - count, E), F32)], axis=0)
        return part.astype(BF16)

    for h in range(heads):
        cols = slice(h * E, (h + 1) * E)
        q, g = q_ref[:, cols], g_ref[:, cols]
        k = jnp.concatenate([k_ref[:, cols], summary(h)], axis=0)
        v = jnp.concatenate([v_ref[:, cols], summary(heads + h)], axis=0)
        logits = jnp.where(allowed, dot(k, q, ((1,), (1,))) * scale, MASKED)
        grad_probs = dot(v, g, ((1,), (1,)))
        own_log = stats_ref[h : h + 1, :]
        own_inner = stats_ref[heads + h : heads + h + 1, :]
        top = jnp.maximum(jnp.max(logits, axis=0, keepdims=True), own_log)
        weight = jnp.exp(logits - top)
        own_weight = jnp.exp(own_log - top)
        total = own_weight + jnp.sum(weight, axis=0, keepdims=True)
        part = 1.0 / total
        inner = part * (
            own_weight * own_inner + jnp.sum(weight * grad_probs, axis=0, keepdims=True)
        )
        probs = weight * part
        probs_low = probs.astype(BF16)
        grad_logits = (probs * (grad_probs - inner)).astype(BF16)
        gq_ref[:B, cols] = (scale * dot(grad_logits, k, ((0,), (0,)))).astype(BF16)
        stats = in_three(top + jnp.log(total)) + in_three(inner)
        stats.append(jnp.zeros((STAT_ROWS - len(stats), E), F32))
        gq_ref[B:, cols] = jnp.concatenate(stats, axis=0).astype(BF16)
        grad_k = scale * dot(grad_logits, q, ((1,), (0,)))
        grad_v = dot(probs_low, g, ((1,), (0,)))
        gk_ref[:, cols] = grad_k[:B]
        gv_ref[:, cols] = grad_v[:B]
        sums[h * padded : (h + 1) * padded, :] = grad_k[B:]
        sums[(heads + h) * padded : (heads + h + 1) * padded, :] = grad_v[B:]

    for t in range(count):
        gs_ref[t] = sums[pl.ds(t, 2 * heads, stride=padded), :]


def final_kernel(
    heads, place_ref, q_ref, g_ref, k_ref, v_ref, own_ref, back_ref, gk_ref, gv_ref,
    gs_ref, out_q_ref, out_k_ref, out_v_ref
):
    first = place_ref[0] == 0
    scale = E**-0.5
    sums = jnp.sum(gs_ref[...], axis=0)
    key = lax.broadcasted_iota(jnp.int32, (B, B), 0)
    query = lax.broadcasted_iota(jnp.int32, (B, B), 1)
    allowed = key <= query
    last_row = key == B - 1
    for h in range(heads):
        cols = slice(h * E, (h + 1) * E)
        q, k, v, g = q_ref[:, cols], k_ref[:, cols], v_ref[:, cols], g_ref[:, cols]
        sent = back_ref[B:, cols].astype(F32)
        log_total = sent[0:1] + sent[1:2] + sent[2:3]
        inner = sent[3:4] + sent[4:5] + sent[5:6]
        log_total = jnp.where(first, own_ref[h : h + 1, :], log_total)
        inner = jnp.where(first, own_ref[heads + h : heads + h + 1, :], inner)
        logits = jnp.where(allowed, dot(k, q, ((1,), (1,))) * scale, MASKED)
        probs = jnp.exp(logits - log_total)
        probs_low = probs.astype(BF16)
        grad_logits = (probs * (dot(v, g, ((1,), (1,))) - inner)).astype(BF16)
        grad_q = scale * dot(grad_logits, k, ((0,), (0,))) + back_ref[:B, cols].astype(F32)
        grad_k = scale * dot(grad_logits, q, ((1,), (0,))) + gk_ref[:, cols]
        grad_v = dot(probs_low, g, ((1,), (0,))) + gv_ref[:, cols]
        grad_k += jnp.where(last_row, sums[h : h + 1, :], 0.0)
        grad_v += jnp.where(last_row, sums[heads + h : heads + h + 1, :], 0.0)
        out_q_ref[:, cols] = grad_q.astype(BF16)
        out_k_ref[:, cols] = grad_k.astype(BF16)
        out_v_ref[:, cols] = grad_v.astype(BF16)


def body(queries, key_vectors, value_vectors, grad_out):
    shard_len, features = queries.shape
    assert shard_len == B
    heads = features // E
    count = lax.axis_size("seq")
    padded = -(-count // 16) * 16
    place = lax.axis_index("seq").astype(jnp.int32).reshape(1)
    vmem = pl.BlockSpec(memory_space=pltpu.VMEM)
    smem = pl.BlockSpec(memory_space=pltpu.SMEM)
    wide = jax.ShapeDtypeStruct((B, features), BF16)
    wide_f32 = jax.ShapeDtypeStruct((B, features), F32)
    flops = 2 * heads * B * B * E
    limit = pltpu.CompilerParams(vmem_limit_bytes=24 << 20)

    next_q = passed_along(queries, -1)
    next_g = passed_along(grad_out, -1)

    own_stats = pl.pallas_call(
        functools.partial(own_stats_kernel, heads),
        in_specs=[vmem] * 4,
        out_specs=vmem,
        out_shape=jax.ShapeDtypeStruct((2 * heads, B), F32),
        compiler_params=limit,
        cost_estimate=pl.CostEstimate(
            flops=2 * flops, bytes_accessed=4 * B * features * 2, transcendentals=heads * B * B
        ),
        name="own_stats",
    )(queries, key_vectors, value_vectors, grad_out)
    next_stats = passed_along(own_stats, -1)

    last_rows = jnp.concatenate(
        [key_vectors[B - 1].reshape(heads, E), value_vectors[B - 1].reshape(heads, E)], axis=0
    )
    summary = lax.all_to_all(
        jnp.broadcast_to(last_rows[None], (count, 2 * heads, E)), "seq", 0, 0, tiled=True
    )

    grad_q_next, grad_k, grad_v, grad_summary = pl.pallas_call(
        functools.partial(cross_kernel, heads, count),
        in_specs=[smem] + [vmem] * 6,
        out_specs=[vmem] * 4,
        scratch_shapes=[
            pltpu.VMEM((count * 2 * heads, E), F32),
            pltpu.VMEM((padded * 2 * heads, E), F32),
        ],
        out_shape=[
            jax.ShapeDtypeStruct((B + STAT_ROWS, features), BF16),
            wide_f32,
            wide_f32,
            jax.ShapeDtypeStruct((count, 2 * heads, E), F32),
        ],
        compiler_params=limit,
        cost_estimate=pl.CostEstimate(
            flops=5 * flops, bytes_accessed=9 * B * features * 2, transcendentals=heads * B * B
        ),
        name="cross",
    )(place, next_q, next_g, key_vectors, value_vectors, next_stats, summary)

    back = passed_along(grad_q_next, 1)
    grad_summary = lax.all_to_all(grad_summary, "seq", 0, 0, tiled=True)

    return pl.pallas_call(
        functools.partial(final_kernel, heads),
        in_specs=[smem] + [vmem] * 9,
        out_specs=[vmem] * 3,
        out_shape=[wide, wide, wide],
        compiler_params=limit,
        cost_estimate=pl.CostEstimate(
            flops=5 * flops, bytes_accessed=12 * B * features * 2, transcendentals=heads * B * B
        ),
        name="final",
    )(
        place,
        queries,
        grad_out,
        key_vectors,
        value_vectors,
        own_stats,
        back,
        grad_k,
        grad_v,
        grad_summary,
    )


def solution(mesh):
    spec = P(("dp", "seq"), "head")
    return jax.shard_map(
        body,
        mesh=mesh,
        in_specs=(spec,) * 4,
        out_specs=(spec,) * 3,
        check_vma=False,
    )
```

time: 68 us -> 61.2 us (0.900)
  Pallas kernels: 18.6 us -> 11 us
  local copies, waits for them, and re-layouts: 4.01 us -> 6.41 us
  waiting for transfers between devices: 9.06 us -> 7.86 us
    pallas_call x3, Pallas kernels: 18.6 us -> 11 us  [the longest x1 5.16 us: body(): pl.pallas_call(functools.partial(cross_kernel, heads, count), in_specs=[s...]
    unnamed x10 -> x16, local copies, waits for them, and re-layouts: 1.79 us -> 4.18 us
    ppermute x4, waiting for transfers between devices: 6.52 us -> 5.33 us  [passed_along(): return lax.ppermute(block, 'seq', route)]
  transfers between devices with their start and end apart: 5 -> 5, of which waited for: 2 -> 2; matrix products, arithmetic and copies ran while one was open for 3% -> 4% of each run, Pallas kernels for 6% -> 1%
where the time goes in v2:
time: 61.2 us; the launch traced here: 60.6 us
  starting transfers between devices  18.7 us (31%)
  blocking collectives  15.9 us (26%)
  Pallas kernels  11 us (18%)
  waiting for transfers between devices  7.86 us (13%)
  local copies, waits for them, and re-layouts  6.41 us (10%)
  between operations  0.72 us (1%)
    all_to_all x1, blocking collectives, body(): grad_summary = lax.all_to_all(grad_summary, 'seq', 0, 0, tiled=True)  15.9 us
    ppermute x4, starting transfers between devices, passed_along(): return lax.ppermute(block, 'seq', route)  11.9 us
    all_to_all x1, starting transfers between devices, body(): lax.all_to_all(jnp.broadcast_to(last_rows[None], (count, 2 * heads, E)),...  6.8 us
    ppermute x4, waiting for transfers between devices, passed_along(): return lax.ppermute(block, 'seq', route)  5.33 us
    pallas_call x1, Pallas kernels, body(): pl.pallas_call(functools.partial(cross_kernel, heads, count), in_specs=[s...  5.16 us
    pallas_call x1, Pallas kernels, body(): pl.pallas_call(functools.partial(final_kernel, heads), in_specs=[smem] +...  4.92 us
    unnamed x16, local copies, waits for them, and re-layouts  4.18 us
    all_to_all x1, waiting for transfers between devices, body(): lax.all_to_all(jnp.broadcast_to(last_rows[None], (count, 2 * heads, E)),...  2.54 us
  transfers between devices with their start and end apart: 5, of which 2 were waited for; matrix products, arithmetic and copies ran while one was open for 4% of the time, Pallas kernels for 1%

profile of v2, /device:TPU:8, one launch (start us, length us, event | category | flops | bytes accessed | tf_op | source)
XLA Modules:
  0.0 60.6 jit_solution(15118896057069983519)
XLA Ops:
  0.6 3.3 %collective-permute-start = (bf16[128,2048]{1,0:T(8,128)(2,1)}, bf16[128,2048]{1,0:T(8,128)(2,1)S(1)}, u32[]{:S(2)}, u32[]{:S(2)}) collective-permute-start(bf16[128,2048]{1,0:T(8,128)(2,1)} %q_ref.3), channel_id=1, source_target_pairs={{4,0},{8,4},{12,8},{16,12},{20,16},{24,20},{28,24},{5,1},{9,5},{13... | collective-permute-start | bytes 1572872 | tf_op jit(solution)/shard_map/ppermute | solution.py:25
  4.0 1.9 %collective-permute-start.1 = (bf16[128,2048]{1,0:T(8,128)(2,1)}, bf16[128,2048]{1,0:T(8,128)(2,1)S(1)}, u32[]{:S(2)}, u32[]{:S(2)}) collective-permute-start(bf16[128,2048]{1,0:T(8,128)(2,1)} %g_ref.3), channel_id=1, source_target_pairs={{4,0},{8,4},{12,8},{16,12},{20,16},{24,20},{28,24},{5,1},{9,5},{13... | collective-permute-start | bytes 1572872 | tf_op jit(solution)/shard_map/ppermute | solution.py:25
  5.9 0.8 %slice_reduce_fusion.1 = bf16[2048]{0:T(1024)(128)(2,1)S(1)} fusion(bf16[128,2048]{1,0:T(8,128)(2,1)} %k_ref.5), kind=kLoop, calls=%fused_computation.2 | loop fusion | bytes 8192 | tf_op jit(solution)/shard_map/slice | solution.py:168
  6.7 0.8 %slice_reduce_fusion = bf16[2048]{0:T(1024)(128)(2,1)S(1)} fusion(bf16[128,2048]{1,0:T(8,128)(2,1)} %v_ref.5), kind=kLoop, calls=%fused_computation.1 | loop fusion | bytes 8192 | tf_op jit(solution)/shard_map/slice | solution.py:168
  7.5 0.6 %broadcast_in_dim.2 = bf16[8,32,128]{2,1,0:T(8,128)(2,1)} broadcast(bf16[32,128]{1,0:T(8,128)(2,1)S(1)} %pad_maximum_fusion), dimensions={1,2} | broadcast | bytes 73728 | tf_op jit(solution)/shard_map/broadcast_in_dim | solution.py:171
  8.1 6.8 %all-to-all-start = ((bf16[8,32,128]{2,1,0:T(8,128)(2,1)}), bf16[8,32,128]{2,1,0:T(8,128)(2,1)S(1)}, u32[]{:S(2)}, u32[]{:S(2)}) async-start(bf16[8,32,128]{2,1,0:T(8,128)(2,1)} %broadcast_in_dim.2), calls=%async_computation | async-start | bytes 131072 | tf_op jit(solution)/shard_map/all_to_all | solution.py:170
  14.9 0.0 copy-start
  14.9 1.0 %copy-done = bf16[128,2048]{1,0:T(8,128)(2,1)S(1)} copy-done((bf16[128,2048]{1,0:T(8,128)(2,1)S(1)}, bf16[128,2048]{1,0:T(8,128)(2,1)}, u32[]{:S(2)}) %copy-start) | copy-done | bytes 524312
  16.0 0.0 copy-start.2
  16.0 1.0 %copy-done.2 = bf16[128,2048]{1,0:T(8,128)(2,1)S(1)} copy-done((bf16[128,2048]{1,0:T(8,128)(2,1)S(1)}, bf16[128,2048]{1,0:T(8,128)(2,1)}, u32[]{:S(2)}) %copy-start.2) | copy-done | bytes 524312
  17.0 0.0 copy-start.4
  17.0 1.0 %copy-done.4 = bf16[128,2048]{1,0:T(8,128)(2,1)S(1)} copy-done((bf16[128,2048]{1,0:T(8,128)(2,1)S(1)}, bf16[128,2048]{1,0:T(8,128)(2,1)}, u32[]{:S(2)}) %copy-start.4) | copy-done | bytes 524312
  18.0 0.0 copy-start.6
  18.1 1.0 %copy-done.6 = bf16[128,2048]{1,0:T(8,128)(2,1)S(1)} copy-done((bf16[128,2048]{1,0:T(8,128)(2,1)S(1)}, bf16[128,2048]{1,0:T(8,128)(2,1)}, u32[]{:S(2)}) %copy-start.6) | copy-done | bytes 524312
  19.1 0.0 copy-start.1
  19.1 0.9 %own_stats.1.own_ref = f32[32,128]{1,0:T(8,128)S(1)} custom-call(bf16[128,2048]{1,0:T(8,128)(2,1)S(1)} %copy-done.4, bf16[128,2048]{1,0:T(8,128)(2,1)S(1)} %copy-done, bf16[128,2048]{1,0:T(8,128)(2,1)S(1)} %copy-done.2, bf16[128,2048]{1,0:T(8,128)(2,1)S(1)} %copy-done.6), custom_call_target="tpu_custom_call" | custom-call | flops 134217728 | bytes 2097152 | tf_op jit(solution)/shard_map/own_stats/pallas_call | solution.py:154
  20.0 3.4 %collective-permute-start.2 = (f32[32,128]{1,0:T(8,128)S(1)}, f32[32,128]{1,0:T(8,128)S(1)}, u32[]{:S(2)}, u32[]{:S(2)}) collective-permute-start(f32[32,128]{1,0:T(8,128)S(1)} %own_stats.1.own_ref), channel_id=1, source_target_pairs={{4,0},{8,4},{12,8},{16,12},{20,16},{24,20},{28,24},{5,1},{9,5},{13... | collective-permute-start | bytes 49160 | tf_op jit(solution)/shard_map/ppermute | solution.py:25
  23.4 5.3 %collective-permute-done.2.stats_ref = f32[32,128]{1,0:T(8,128)S(1)} collective-permute-done((f32[32,128]{1,0:T(8,128)S(1)}, f32[32,128]{1,0:T(8,128)S(1)}, u32[]{:S(2)}, u32[]{:S(2)}) %collective-permute-start.2) | collective-permute-done | bytes 16416 | tf_op jit(solution)/shard_map/ppermute | solution.py:25
  28.7 2.5 %all-to-all-done.summary_ref = bf16[8,32,128]{2,1,0:T(8,128)(2,1)S(1)} async-done(((bf16[8,32,128]{2,1,0:T(8,128)(2,1)}), bf16[8,32,128]{2,1,0:T(8,128)(2,1)S(1)}, u32[]{:S(2)}, u32[]{:S(2)}) %all-to-all-start) | async-done | bytes 65568 | tf_op jit(solution)/shard_map/all_to_all | solution.py:170
  31.2 0.0 collective-permute-done.q_ref
  31.2 0.0 collective-permute-done.1.g_ref
  31.2 0.0 copy-done.1
  31.2 0.0 copy-done.3
  31.2 0.0 copy-start.5
  31.3 0.0 copy-start.7
  31.3 5.2 %cross.1 = (bf16[144,2048]{1,0:T(8,128)(2,1)S(1)}, f32[128,2048]{1,0:T(8,128)S(1)}, f32[128,2048]{1,0:T(8,128)S(1)}, f32[8,32,128]{2,1,0:T(8,128)S(1)}) custom-call(s32[1]{0:T(128)} %bitcast.place_ref, bf16[128,2048]{1,0:T(8,128)(2,1)S(1)} %collective-permute-done.q_ref, bf16[128,2048]{1,0:T(8,128)(2,1)S(1)} %collective-permute-done.1.g_ref, ...), custom_call_target="tpu_custom_call" | custom-call | flops 335544320 | bytes 4718592 | tf_op jit(solution)/shard_map/cross/pallas_call | solution.py:174
  36.4 3.3 %collective-permute-start.3 = (bf16[144,2048]{1,0:T(8,128)(2,1)S(1)}, bf16[144,2048]{1,0:T(8,128)(2,1)S(1)}, u32[]{:S(2)}, u32[]{:S(2)}) collective-permute-start(bf16[144,2048]{1,0:T(8,128)(2,1)S(1)} %get-tuple-element.7), channel_id=1, source_target_pairs={{0,4},{4,8},{8,12},{12,16},{16,20},{20,24},{24,28},{1,5},{5,9},{9,... | collective-permute-start | bytes 1769480 | tf_op jit(solution)/shard_map/ppermute | solution.py:25
  39.7 15.9 %all_to_all.10.gs_ref = f32[8,32,128]{2,1,0:T(8,128)S(1)} all-to-all(f32[8,32,128]{2,1,0:T(8,128)S(1)} %get-tuple-element.10), channel_id=1, replica_groups=mesh['seq'=8,'head'=2,'dp'=2] {'seq'}, dimensions={0} | all-to-all | bytes 262144 | tf_op jit(solution)/shard_map/all_to_all | solution.py:196
  55.6 0.0 collective-permute-done.3.back_ref
  55.6 0.0 copy-done.5
  55.6 0.0 copy-done.7
  55.6 4.9 %final.1 = (bf16[128,2048]{1,0:T(8,128)(2,1)}, bf16[128,2048]{1,0:T(8,128)(2,1)}, bf16[128,2048]{1,0:T(8,128)(2,1)}) custom-call(s32[1]{0:T(128)} %bitcast.place_ref, bf16[128,2048]{1,0:T(8,128)(2,1)S(1)} %copy-done.5, bf16[128,2048]{1,0:T(8,128)(2,1)S(1)} %copy-done.7, bf16[128,2048]{1,0:T(8,128)(2,1)S(1)} %copy-done.1, bf16[128,2048]{1,0:T(8,128)(2,1)S(1)} %copy-done.3, ...), custom_call_target="tpu_custom_call" | custom-call | flops 335544320 | bytes 6291456 | tf_op jit(solution)/shard_map/final/pallas_call | solution.py:198
  (2 shorter events, 0.0 us)
Async XLA Ops:
  0.6 30.6 %collective-permute-start = (bf16[128,2048]{1,0:T(8,128)(2,1)}, bf16[128,2048]{1,0:T(8,128)(2,1)S(1)}, u32[]{:S(2)}, u32[]{:S(2)}) collective-permute-start(bf16[128,2048]{1,0:T(8,128)(2,1)} %q_ref.3), channel_id=1, source_target_pairs={{4,0},{8,4},{12,8},{16,12},{20,16},{24,20},{28,24},{5,1},{9,5},{13... | collective-permute-start | bytes 1572872 | tf_op jit(solution)/shard_map/ppermute | solution.py:25
  4.0 27.3 %collective-permute-start.1 = (bf16[128,2048]{1,0:T(8,128)(2,1)}, bf16[128,2048]{1,0:T(8,128)(2,1)S(1)}, u32[]{:S(2)}, u32[]{:S(2)}) collective-permute-start(bf16[128,2048]{1,0:T(8,128)(2,1)} %g_ref.3), channel_id=1, source_target_pairs={{4,0},{8,4},{12,8},{16,12},{20,16},{24,20},{28,24},{5,1},{9,5},{13... | collective-permute-start | bytes 1572872 | tf_op jit(solution)/shard_map/ppermute | solution.py:25
  8.1 23.1 %all-to-all-start = ((bf16[8,32,128]{2,1,0:T(8,128)(2,1)}), bf16[8,32,128]{2,1,0:T(8,128)(2,1)S(1)}, u32[]{:S(2)}, u32[]{:S(2)}) async-start(bf16[8,32,128]{2,1,0:T(8,128)(2,1)} %broadcast_in_dim.2), calls=%async_computation | async-start | bytes 131072 | tf_op jit(solution)/shard_map/all_to_all | solution.py:170
  14.9 1.0 %copy-start = (bf16[128,2048]{1,0:T(8,128)(2,1)S(1)}, bf16[128,2048]{1,0:T(8,128)(2,1)}, u32[]{:S(2)}) copy-start(bf16[128,2048]{1,0:T(8,128)(2,1)} %k_ref.5) | copy-start | bytes 1572868
  16.0 1.0 %copy-start.2 = (bf16[128,2048]{1,0:T(8,128)(2,1)S(1)}, bf16[128,2048]{1,0:T(8,128)(2,1)}, u32[]{:S(2)}) copy-start(bf16[128,2048]{1,0:T(8,128)(2,1)} %v_ref.5) | copy-start | bytes 1572868
  17.0 1.0 %copy-start.4 = (bf16[128,2048]{1,0:T(8,128)(2,1)S(1)}, bf16[128,2048]{1,0:T(8,128)(2,1)}, u32[]{:S(2)}) copy-start(bf16[128,2048]{1,0:T(8,128)(2,1)} %q_ref.3) | copy-start | bytes 1572868
  18.0 1.0 %copy-start.6 = (bf16[128,2048]{1,0:T(8,128)(2,1)S(1)}, bf16[128,2048]{1,0:T(8,128)(2,1)}, u32[]{:S(2)}) copy-start(bf16[128,2048]{1,0:T(8,128)(2,1)} %g_ref.3) | copy-start | bytes 1572868
  19.1 12.1 %copy-start.1 = (bf16[128,2048]{1,0:T(8,128)(2,1)S(1)}, bf16[128,2048]{1,0:T(8,128)(2,1)}, u32[]{:S(2)}) copy-start(bf16[128,2048]{1,0:T(8,128)(2,1)} %k_ref.5) | copy-start | bytes 1572868
  19.1 12.1 %copy-start.3 = (bf16[128,2048]{1,0:T(8,128)(2,1)S(1)}, bf16[128,2048]{1,0:T(8,128)(2,1)}, u32[]{:S(2)}) copy-start(bf16[128,2048]{1,0:T(8,128)(2,1)} %v_ref.5) | copy-start | bytes 1572868
  20.0 8.7 %collective-permute-start.2 = (f32[32,128]{1,0:T(8,128)S(1)}, f32[32,128]{1,0:T(8,128)S(1)}, u32[]{:S(2)}, u32[]{:S(2)}) collective-permute-start(f32[32,128]{1,0:T(8,128)S(1)} %own_stats.1.own_ref), channel_id=1, source_target_pairs={{4,0},{8,4},{12,8},{16,12},{20,16},{24,20},{28,24},{5,1},{9,5},{13... | collective-permute-start | bytes 49160 | tf_op jit(solution)/shard_map/ppermute | solution.py:25
  31.2 24.4 %copy-start.5 = (bf16[128,2048]{1,0:T(8,128)(2,1)S(1)}, bf16[128,2048]{1,0:T(8,128)(2,1)}, u32[]{:S(2)}) copy-start(bf16[128,2048]{1,0:T(8,128)(2,1)} %q_ref.3) | copy-start | bytes 1572868
  31.3 24.4 %copy-start.7 = (bf16[128,2048]{1,0:T(8,128)(2,1)S(1)}, bf16[128,2048]{1,0:T(8,128)(2,1)}, u32[]{:S(2)}) copy-start(bf16[128,2048]{1,0:T(8,128)(2,1)} %g_ref.3) | copy-start | bytes 1572868
  36.4 19.2 %collective-permute-start.3 = (bf16[144,2048]{1,0:T(8,128)(2,1)S(1)}, bf16[144,2048]{1,0:T(8,128)(2,1)S(1)}, u32[]{:S(2)}, u32[]{:S(2)}) collective-permute-start(bf16[144,2048]{1,0:T(8,128)(2,1)S(1)} %get-tuple-element.7), channel_id=1, source_target_pairs={{0,4},{4,8},{8,12},{12,16},{16,20},{20,24},{24,28},{1,5},{5,9},{9,... | collective-permute-start | bytes 1769480 | tf_op jit(solution)/shard_map/ppermute | solution.py:25

commit v3 on v2

v3 whole, which is shorter than its diff:
```python
import functools

import jax
import jax.numpy as jnp
from jax import lax
from jax.experimental import pallas as pl
from jax.experimental.pallas import tpu as pltpu
from jax.sharding import PartitionSpec as P

E = 128
B = 128
STAT_ROWS = 8
MASKED = -1e30
F32 = jnp.float32
BF16 = jnp.bfloat16


def dot(a, b, contract):
    return lax.dot_general(a, b, (contract, ((), ())), preferred_element_type=F32)


def passed_along(block, distance):
    count = lax.axis_size("seq")
    route = [(i - distance, i) for i in range(count) if 0 <= i - distance < count]
    return lax.ppermute(block, "seq", route)


def in_three(x):
    high = x.astype(BF16).astype(F32)
    middle = (x - high).astype(BF16).astype(F32)
    low = (x - high - middle).astype(BF16).astype(F32)
    return [high, middle, low]


def stat_rows(log_total, inner):
    rows = in_three(log_total) + in_three(inner)
    rows.append(jnp.zeros((STAT_ROWS - len(rows), E), F32))
    return jnp.concatenate(rows, axis=0).astype(BF16)


def stats_of(rows):
    rows = rows.astype(F32)
    return rows[0:1] + rows[1:2] + rows[2:3], rows[3:4] + rows[4:5] + rows[5:6]


def head_columns(head):
    return slice(head * E, (head + 1) * E)


def own_stats_kernel(heads, q_ref, k_ref, v_ref, g_ref, out_ref):
    key = lax.broadcasted_iota(jnp.int32, (B, B), 0)
    query = lax.broadcasted_iota(jnp.int32, (B, B), 1)
    allowed = key <= query
    for h in range(heads):
        cols = head_columns(h)
        q, k, v, g = q_ref[:, cols], k_ref[:, cols], v_ref[:, cols], g_ref[:, cols]
        logits = jnp.where(allowed, dot(k, q, ((1,), (1,))) * E**-0.5, MASKED)
        top = jnp.max(logits, axis=0, keepdims=True)
        weight = jnp.exp(logits - top)
        total = jnp.sum(weight, axis=0, keepdims=True)
        inner = jnp.sum(weight * dot(v, g, ((1,), (1,))), axis=0, keepdims=True)
        out_ref[:B, cols] = g
        out_ref[B:, cols] = stat_rows(top + jnp.log(total), inner / total)


def cross_kernel(
    heads, count, place_ref, q_ref, g_ref, k_ref, v_ref, summary_ref,
    gq_ref, gk_ref, gv_ref, gs_ref, sums, low, grads
):
    place = place_ref[0]
    pairs = summary_ref.shape[2]
    padded = low.shape[1] - B
    scale = E**-0.5
    key = lax.broadcasted_iota(jnp.int32, (B + padded, B), 0)
    query = lax.broadcasted_iota(jnp.int32, (B + padded, B), 1)
    same, other = key - B, key - B - pairs
    pair = lax.shift_right_logical(place, 1)
    allowed = (key < B) & ((key > query) | (key == B - 1))
    allowed |= (same >= 1) & (same < pairs) & (same <= pair)
    allowed |= (other >= 1 - (place & 1)) & (other < pairs) & (other <= pair)

    def with_summary(block, which, cols):
        parts = [summary_ref[i, which, :, cols].astype(F32) for i in range(2)]
        if padded > 2 * pairs:
            parts.append(jnp.zeros((padded - 2 * pairs, E), F32))
        return jnp.concatenate([block, jnp.concatenate(parts, axis=0).astype(BF16)], axis=0)

    for h in range(heads):
        cols = head_columns(h)
        k = with_summary(k_ref[:, cols], 0, cols)
        v = with_summary(v_ref[:, cols], 1, cols)
        logits = jnp.where(allowed, dot(k, q_ref[:, cols], ((1,), (1,))) * scale, MASKED)
        grad_probs = dot(v, g_ref[:B, cols], ((1,), (1,)))
        own_log, own_inner = stats_of(g_ref[B:, cols])
        top = jnp.maximum(jnp.max(logits, axis=0, keepdims=True), own_log)
        weight = jnp.exp(logits - top)
        own_weight = jnp.exp(own_log - top)
        total = own_weight + jnp.sum(weight, axis=0, keepdims=True)
        part = 1.0 / total
        inner = part * (
            own_weight * own_inner + jnp.sum(weight * grad_probs, axis=0, keepdims=True)
        )
        probs = weight * part
        low[h] = probs.astype(BF16)
        grads[h] = (probs * (grad_probs - inner)).astype(BF16)
        gq_ref[B:, cols] = stat_rows(top + jnp.log(total), inner)

    for h in range(heads):
        cols = head_columns(h)
        grad_logits = grads[h]
        k = with_summary(k_ref[:, cols], 0, cols)
        gq_ref[:B, cols] = (scale * dot(grad_logits, k, ((0,), (0,)))).astype(BF16)
        grad_k = scale * dot(grad_logits, q_ref[:, cols], ((1,), (0,)))
        grad_v = dot(low[h], g_ref[:B, cols], ((1,), (0,)))
        gk_ref[:, cols] = grad_k[:B]
        gv_ref[:, cols] = grad_v[:B]
        sums[h * padded : (h + 1) * padded, :] = grad_k[B:]
        sums[(heads + h) * padded : (heads + h + 1) * padded, :] = grad_v[B:]

    for t in range(count):
        row = ((place ^ t) & 1) * pairs + pair - t // 2
        row = jnp.where(t < place, row, 0)
        gs_ref[t] = sums[pl.ds(row, 2 * heads, stride=padded), :]


def final_kernel(
    heads, place_ref, q_ref, g_ref, k_ref, v_ref, own_ref, back_ref, gk_ref, gv_ref,
    gs_ref, out_q_ref, out_k_ref, out_v_ref, low, grads, done_q, done_k, done_v, sems
):
    first = place_ref[0] == 0
    scale = E**-0.5
    group = heads // 4 if heads % 4 == 0 else heads
    sums = jnp.sum(gs_ref[...], axis=0)
    key = lax.broadcasted_iota(jnp.int32, (B, B), 0)
    query = lax.broadcasted_iota(jnp.int32, (B, B), 1)
    allowed = key <= query
    last_row = key == B - 1
    for h in range(heads):
        cols = head_columns(h)
        log_total, inner = stats_of(jnp.where(first, own_ref[B:, cols], back_ref[B:, cols]))
        logits = dot(k_ref[:, cols], q_ref[:, cols], ((1,), (1,))) * scale
        probs = jnp.exp(jnp.where(allowed, logits, MASKED) - log_total)
        low[h] = probs.astype(BF16)
        grad_probs = dot(v_ref[:, cols], g_ref[:, cols], ((1,), (1,)))
        grads[h] = (probs * (grad_probs - inner)).astype(BF16)

    copies = []
    for h in range(heads):
        cols = head_columns(h)
        grad_logits = grads[h]
        grad_q = scale * dot(grad_logits, k_ref[:, cols], ((0,), (0,)))
        grad_k = scale * dot(grad_logits, q_ref[:, cols], ((1,), (0,)))
        grad_v = dot(low[h], g_ref[:, cols], ((1,), (0,)))
        grad_k += gk_ref[:, cols] + jnp.where(last_row, sums[h : h + 1, :], 0.0)
        grad_v += gv_ref[:, cols] + jnp.where(last_row, sums[heads + h : heads + h + 1, :], 0.0)
        done_q[:, cols] = (grad_q + back_ref[:B, cols].astype(F32)).astype(BF16)
        done_k[:, cols] = grad_k.astype(BF16)
        done_v[:, cols] = grad_v.astype(BF16)
        if (h + 1) % group == 0:
            part = slice((h + 1 - group) * E, (h + 1) * E)
            for done, out in (done_q, out_q_ref), (done_k, out_k_ref), (done_v, out_v_ref):
                copies.append(
                    pltpu.make_async_copy(
                        done.at[:, part], out.at[:, part], sems.at[len(copies)]
                    )
                )
                copies[-1].start()
    for copy in copies:
        copy.wait()


def body(queries, key_vectors, value_vectors, grad_out):
    shard_len, features = queries.shape
    assert shard_len == B and lax.axis_size("seq") % 2 == 0
    heads = features // E
    count = lax.axis_size("seq")
    place = lax.axis_index("seq").astype(jnp.int32).reshape(1)
    vmem = pl.BlockSpec(memory_space=pltpu.VMEM)
    smem = pl.BlockSpec(memory_space=pltpu.SMEM)
    anywhere = pl.BlockSpec(memory_space=pl.ANY)
    wide = jax.ShapeDtypeStruct((B, features), BF16)
    wide_stats = jax.ShapeDtypeStruct((B + STAT_ROWS, features), BF16)
    wide_f32 = jax.ShapeDtypeStruct((B, features), F32)
    flops = 2 * heads * B * B * E
    limit = pltpu.CompilerParams(vmem_limit_bytes=24 << 20)

    next_q = passed_along(queries, -1)

    rows = jnp.stack([key_vectors[B - 1 :], value_vectors[B - 1 :]])
    swap = lax.ppermute(rows, "seq", [(i, i ^ 1) for i in range(count)])
    summary = jnp.stack([rows, swap])
    while 2 * summary.shape[2] < count:
        earlier = passed_along(summary, 2 * summary.shape[2])
        summary = jnp.concatenate([summary, earlier], axis=2)
    padded = -(-2 * summary.shape[2] // 16) * 16
    _, grad_out = lax.optimization_barrier((swap, grad_out))

    grad_stats = pl.pallas_call(
        functools.partial(own_stats_kernel, heads),
        in_specs=[vmem] * 4,
        out_specs=vmem,
        out_shape=wide_stats,
        compiler_params=limit,
        cost_estimate=pl.CostEstimate(
            flops=2 * flops, bytes_accessed=4 * B * features * 2, transcendentals=heads * B * B
        ),
        name="own_stats",
    )(queries, key_vectors, value_vectors, grad_out)
    next_g = passed_along(grad_stats, -1)

    grad_q_next, grad_k, grad_v, grad_summary = pl.pallas_call(
        functools.partial(cross_kernel, heads, count),
        in_specs=[smem] + [vmem] * 5,
        out_specs=[vmem] * 4,
        scratch_shapes=[
            pltpu.VMEM((padded * 2 * heads, E), F32),
            pltpu.VMEM((heads, B + padded, B), BF16),
            pltpu.VMEM((heads, B + padded, B), BF16),
        ],
        out_shape=[
            wide_stats,
            wide_f32,
            wide_f32,
            jax.ShapeDtypeStruct((count, 2 * heads, E), F32),
        ],
        compiler_params=limit,
        cost_estimate=pl.CostEstimate(
            flops=5 * flops, bytes_accessed=9 * B * features * 2, transcendentals=heads * B * B
        ),
        name="cross",
    )(place, next_q, next_g, key_vectors, value_vectors, summary)

    back = passed_along(grad_q_next, 1)
    grad_summary = lax.all_to_all(grad_summary, "seq", 0, 0, tiled=True)

    return pl.pallas_call(
        functools.partial(final_kernel, heads),
        in_specs=[smem] + [vmem] * 9,
        out_specs=[anywhere] * 3,
        out_shape=[wide, wide, wide],
        scratch_shapes=[
            pltpu.VMEM((heads, B, B), BF16),
            pltpu.VMEM((heads, B, B), BF16),
            pltpu.VMEM((B, features), BF16),
            pltpu.VMEM((B, features), BF16),
            pltpu.VMEM((B, features), BF16),
            pltpu.SemaphoreType.DMA((12,)),
        ],
        compiler_params=limit,
        cost_estimate=pl.CostEstimate(
            flops=5 * flops, bytes_accessed=12 * B * features * 2, transcendentals=heads * B * B
        ),
        name="final",
    )(
        place,
        queries,
        grad_out,
        key_vectors,
        value_vectors,
        grad_stats,
        back,
        grad_k,
        grad_v,
        grad_summary,
    )


def solution(mesh):
    spec = P(("dp", "seq"), "head")
    return jax.shard_map(
        body,
        mesh=mesh,
        in_specs=(spec,) * 4,
        out_specs=(spec,) * 3,
        check_vma=False,
    )
```

time: 61.2 us -> 54.3 us (0.89)
  Pallas kernels: 11 us -> 5.39 us
  local copies, waits for them, and re-layouts: 6.41 us -> 5.01 us
  blocking collectives: 15.9 us -> 15 us
    all_to_all x1 -> x0, starting transfers between devices: 6.8 us -> none  [body(): lax.all_to_all(jnp.broadcast_to(last_rows[None], (count, 2 * heads, E)),...]
    ppermute x4 -> x5, starting transfers between devices: 11.9 us -> 16.9 us  [passed_along(): return lax.ppermute(block, 'seq', route)]
    pallas_call x1, Pallas kernels: 5.16 us -> 2.11 us  [body(): pl.pallas_call(functools.partial(cross_kernel, heads, count), in_specs=[s...]
    ppermute x4 -> x5, waiting for transfers between devices: 5.33 us -> 8.29 us  [passed_along(): return lax.ppermute(block, 'seq', route)]
    pallas_call x1, Pallas kernels: 4.92 us -> 2.37 us  [body(): pl.pallas_call(functools.partial(final_kernel, heads), in_specs=[smem] +...]
    all_to_all x1 -> x0, waiting for transfers between devices: 2.54 us -> none  [body(): lax.all_to_all(jnp.broadcast_to(last_rows[None], (count, 2 * heads, E)),...]
    slice x2 -> x0, local copies, waits for them, and re-layouts: 1.59 us -> none  [the longest x1 0.79 us: body(): key_vectors[B - 1].reshape(heads, E)]
    ppermute x0 -> x1, starting transfers between devices: none -> 1.58 us  [body(): swap = lax.ppermute(rows, 'seq', [(i, i ^ 1) for i in range(count)])]
  transfers between devices with their start and end apart: 5 -> 6, of which waited for: 2 -> 4; matrix products, arithmetic and copies ran while one was open for 4% -> 0% of each run, Pallas kernels for 1% -> 2%
where the time goes in v3:
time: 54.3 us; the launch traced here: 53.3 us
  starting transfers between devices  18.4 us (34%)
  blocking collectives  15 us (28%)
  waiting for transfers between devices  8.45 us (16%)
  Pallas kernels  5.39 us (10%)
  local copies, waits for them, and re-layouts  5.01 us (9%)
  between operations  0.75 us (1%)
    ppermute x5, starting transfers between devices, passed_along(): return lax.ppermute(block, 'seq', route)  16.9 us
    all_to_all x1, blocking collectives, body(): grad_summary = lax.all_to_all(grad_summary, 'seq', 0, 0, tiled=True)  15 us
    ppermute x5, waiting for transfers between devices, passed_along(): return lax.ppermute(block, 'seq', route)  8.29 us
    unnamed x17, local copies, waits for them, and re-layouts  4.19 us
    pallas_call x1, Pallas kernels, body(): pl.pallas_call(functools.partial(final_kernel, heads), in_specs=[smem] +...  2.37 us
    pallas_call x1, Pallas kernels, body(): pl.pallas_call(functools.partial(cross_kernel, heads, count), in_specs=[s...  2.11 us
    ppermute x1, starting transfers between devices, body(): swap = lax.ppermute(rows, 'seq', [(i, i ^ 1) for i in range(count)])  1.58 us
  transfers between devices with their start and end apart: 6, of which 4 were waited for; matrix products, arithmetic and copies ran while one was open for 0% of the time, Pallas kernels for 2%

profile of v3, /device:TPU:8, one launch (start us, length us, event | category | flops | bytes accessed | tf_op | source)
XLA Modules:
  0.0 53.3 jit_solution(14584640317318784756)
XLA Ops:
  0.6 0.8 %slice_bitcast_fusion = (bf16[1,1,2048]{2,0,1:T(2,128)(2,1)S(1)}, bf16[1,1,2048]{2,0,1:T(2,128)(2,1)S(1)}) fusion(bf16[128,2048]{1,0:T(8,128)(2,1)} %v_ref.5, bf16[128,2048]{1,0:T(8,128)(2,1)} %k_ref.5), kind=kLoop, calls=%fused_computation.5 | loop fusion | bytes 16384 | tf_op jit(solution)/shard_map/stack | solution.py:189
  1.5 1.6 %collective-permute-start = (bf16[2,1,2048]{2,0,1:T(2,128)(2,1)S(1)}, bf16[2,1,2048]{2,0,1:T(2,128)(2,1)S(1)}, u32[]{:S(2)}, u32[]{:S(2)}) collective-permute-start(bf16[2,1,2048]{2,0,1:T(2,128)(2,1)S(1)} %pad_maximum_fusion.2), channel_id=1, source_target_pairs={{0,4},{4,0},{8,12},{12,8},{16,20},{20,16},{24,28},{28,24},{1,5},{5... | collective-permute-start | bytes 24584 | tf_op jit(solution)/shard_map/ppermute | solution.py:190
  3.0 1.9 %collective-permute-start.1 = (bf16[128,2048]{1,0:T(8,128)(2,1)}, bf16[128,2048]{1,0:T(8,128)(2,1)S(1)}, u32[]{:S(2)}, u32[]{:S(2)}) collective-permute-start(bf16[128,2048]{1,0:T(8,128)(2,1)} %q_ref.3), channel_id=1, source_target_pairs={{4,0},{8,4},{12,8},{16,12},{20,16},{24,20},{28,24},{5,1},{9,5},{13... | collective-permute-start | bytes 1572872 | tf_op jit(solution)/shard_map/ppermute | solution.py:25
  5.0 0.2 collective-permute-done
  5.2 0.0 copy-start
  5.2 1.0 %copy-done = bf16[128,2048]{1,0:T(8,128)(2,1)S(1)} copy-done((bf16[128,2048]{1,0:T(8,128)(2,1)S(1)}, bf16[128,2048]{1,0:T(8,128)(2,1)}, u32[]{:S(2)}) %copy-start) | copy-done | bytes 524312
  6.2 0.0 copy-start.2
  6.2 1.0 %copy-done.2 = bf16[128,2048]{1,0:T(8,128)(2,1)S(1)} copy-done((bf16[128,2048]{1,0:T(8,128)(2,1)S(1)}, bf16[128,2048]{1,0:T(8,128)(2,1)}, u32[]{:S(2)}) %copy-start.2) | copy-done | bytes 524312
  7.3 0.0 copy-start.4
  7.3 1.0 %copy-done.4 = bf16[128,2048]{1,0:T(8,128)(2,1)S(1)} copy-done((bf16[128,2048]{1,0:T(8,128)(2,1)S(1)}, bf16[128,2048]{1,0:T(8,128)(2,1)}, u32[]{:S(2)}) %copy-start.4) | copy-done | bytes 524312
  8.3 0.0 copy-start.6
  8.3 1.0 %copy-done.6 = bf16[128,2048]{1,0:T(8,128)(2,1)S(1)} copy-done((bf16[128,2048]{1,0:T(8,128)(2,1)S(1)}, bf16[128,2048]{1,0:T(8,128)(2,1)}, u32[]{:S(2)}) %copy-start.6) | copy-done | bytes 524312
  9.3 0.0 copy-start.1
  9.4 0.9 %own_stats.1.own_ref = bf16[136,2048]{1,0:T(8,128)(2,1)S(1)} custom-call(bf16[128,2048]{1,0:T(8,128)(2,1)S(1)} %copy-done.4, bf16[128,2048]{1,0:T(8,128)(2,1)S(1)} %copy-done, bf16[128,2048]{1,0:T(8,128)(2,1)S(1)} %copy-done.2, bf16[128,2048]{1,0:T(8,128)(2,1)S(1)} %copy-done.6), custom_call_target="tpu_custom_call" | custom-call | flops 134217728 | bytes 2097152 | tf_op jit(solution)/shard_map/own_stats/pallas_call | solution.py:198
  10.3 3.7 %collective-permute-start.2 = (bf16[136,2048]{1,0:T(8,128)(2,1)S(1)}, bf16[136,2048]{1,0:T(8,128)(2,1)S(1)}, u32[]{:S(2)}, u32[]{:S(2)}) collective-permute-start(bf16[136,2048]{1,0:T(8,128)(2,1)S(1)} %own_stats.1.own_ref), channel_id=1, source_target_pairs={{4,0},{8,4},{12,8},{16,12},{20,16},{24,20},{28,24},{5,1},{9,5},{13... | collective-permute-start | bytes 1671176 | tf_op jit(solution)/shard_map/ppermute | solution.py:25
  14.0 3.5 %collective-permute-start.3 = (bf16[2,2,1,2048]{3,2,1,0:T(2,128)(2,1)S(1)}, bf16[2,2,1,2048]{3,2,1,0:T(2,128)(2,1)S(1)}, u32[]{:S(2)}, u32[]{:S(2)}) collective-permute-start(bf16[2,2,1,2048]{3,2,1,0:T(2,128)(2,1)S(1)} %copy_dynamic-update-slice_fusion), channel_id=1, source_target_pairs={{0,8},{4,12},{8,16},{12,20},{16,24},{20,28},{1,9},{5,13},{9,17},{1... | collective-permute-start | bytes 49160 | tf_op jit(solution)/shard_map/ppermute | solution.py:25
  17.5 2.3 %collective-permute-done.3 = bf16[2,2,1,2048]{3,2,1,0:T(2,128)(2,1)S(1)} collective-permute-done((bf16[2,2,1,2048]{3,2,1,0:T(2,128)(2,1)S(1)}, bf16[2,2,1,2048]{3,2,1,0:T(2,128)(2,1)S(1)}, u32[]{:S(2)}, u32[]{:S(2)}) %collective-permute-start.3) | collective-permute-done | bytes 16416 | tf_op jit(solution)/shard_map/ppermute | solution.py:25
  19.8 0.1 pad_maximum_fusion.1
  19.9 4.5 %collective-permute-start.4 = (bf16[2,2,2,2048]{3,2,1,0:T(2,128)(2,1)S(1)}, bf16[2,2,2,2048]{3,2,1,0:T(2,128)(2,1)S(1)}, u32[]{:S(2)}, u32[]{:S(2)}) collective-permute-start(bf16[2,2,2,2048]{3,2,1,0:T(2,128)(2,1)S(1)} %pad_maximum_fusion.1), channel_id=1, source_target_pairs={{0,16},{4,20},{8,24},{12,28},{1,17},{5,21},{9,25},{13,29},{2,18},{... | collective-permute-start | bytes 98312 | tf_op jit(solution)/shard_map/ppermute | solution.py:25
  24.4 1.7 %collective-permute-done.4 = bf16[2,2,2,2048]{3,2,1,0:T(2,128)(2,1)S(1)} collective-permute-done((bf16[2,2,2,2048]{3,2,1,0:T(2,128)(2,1)S(1)}, bf16[2,2,2,2048]{3,2,1,0:T(2,128)(2,1)S(1)}, u32[]{:S(2)}, u32[]{:S(2)}) %collective-permute-start.4) | collective-permute-done | bytes 32800 | tf_op jit(solution)/shard_map/ppermute | solution.py:25
  26.0 0.1 pad_maximum_fusion.summary_ref
  26.2 0.0 collective-permute-done.1.q_ref
  26.2 4.3 %collective-permute-done.2.g_ref = bf16[136,2048]{1,0:T(8,128)(2,1)S(1)} collective-permute-done((bf16[136,2048]{1,0:T(8,128)(2,1)S(1)}, bf16[136,2048]{1,0:T(8,128)(2,1)S(1)}, u32[]{:S(2)}, u32[]{:S(2)}) %collective-permute-start.2) | collective-permute-done | bytes 557088 | tf_op jit(solution)/shard_map/ppermute | solution.py:25
  30.5 0.0 copy-done.1
  30.5 0.0 copy-done.3
  30.5 2.1 %cross.1 = (bf16[136,2048]{1,0:T(8,128)(2,1)S(1)}, f32[128,2048]{1,0:T(8,128)S(1)}, f32[128,2048]{1,0:T(8,128)S(1)}, f32[8,32,128]{2,1,0:T(8,128)S(1)}) custom-call(s32[1]{0:T(128)} %bitcast.place_ref, bf16[128,2048]{1,0:T(8,128)(2,1)S(1)} %collective-permute-done.1.q_ref, bf16[136,2048]{1,0:T(8,128)(2,1)S(1)} %collective-permute-done.2.g_ref, ...), custom_call_target="tpu_custom_call" | custom-call | flops 335544320 | bytes 4718592 | tf_op jit(solution)/shard_map/cross/pallas_call | solution.py:211
  32.6 3.3 %collective-permute-start.5 = (bf16[136,2048]{1,0:T(8,128)(2,1)S(1)}, bf16[136,2048]{1,0:T(8,128)(2,1)S(1)}, u32[]{:S(2)}, u32[]{:S(2)}) collective-permute-start(bf16[136,2048]{1,0:T(8,128)(2,1)S(1)} %get-tuple-element.9), channel_id=1, source_target_pairs={{0,4},{4,8},{8,12},{12,16},{16,20},{20,24},{24,28},{1,5},{5,9},{9,... | collective-permute-start | bytes 1671176 | tf_op jit(solution)/shard_map/ppermute | solution.py:25
  35.9 15.0 %all_to_all.5.gs_ref = f32[8,32,128]{2,1,0:T(8,128)S(1)} all-to-all(f32[8,32,128]{2,1,0:T(8,128)S(1)} %get-tuple-element.12), channel_id=1, replica_groups=mesh['seq'=8,'head'=2,'dp'=2] {'seq'}, dimensions={0} | all-to-all | bytes 262144 | tf_op jit(solution)/shard_map/all_to_all | solution.py:234
  50.9 0.0 collective-permute-done.5.back_ref
  50.9 0.0 copy-done.5
  50.9 0.0 copy-done.7
  50.9 2.4 %final.1 = (bf16[128,2048]{1,0:T(8,128)(2,1)}, bf16[128,2048]{1,0:T(8,128)(2,1)}, bf16[128,2048]{1,0:T(8,128)(2,1)}) custom-call(s32[1]{0:T(128)} %bitcast.place_ref, bf16[128,2048]{1,0:T(8,128)(2,1)S(1)} %copy-done.5, bf16[128,2048]{1,0:T(8,128)(2,1)S(1)} %copy-done.7, bf16[128,2048]{1,0:T(8,128)(2,1)S(1)} %copy-done.1, bf16[128,2048]{1,0:T(8,128)(2,1)S(1)} %copy-done.3, ...), custom_call_target="tpu_custom_call" | custom-call | flops 335544320 | bytes 6291456 | tf_op jit(solution)/shard_map/final/pallas_call | solution.py:236
  (7 shorter events, 0.1 us)
Async XLA Ops:
  1.5 3.7 %collective-permute-start = (bf16[2,1,2048]{2,0,1:T(2,128)(2,1)S(1)}, bf16[2,1,2048]{2,0,1:T(2,128)(2,1)S(1)}, u32[]{:S(2)}, u32[]{:S(2)}) collective-permute-start(bf16[2,1,2048]{2,0,1:T(2,128)(2,1)S(1)} %pad_maximum_fusion.2), channel_id=1, source_target_pairs={{0,4},{4,0},{8,12},{12,8},{16,20},{20,16},{24,28},{28,24},{1,5},{5... | collective-permute-start | bytes 24584 | tf_op jit(solution)/shard_map/ppermute | solution.py:190
  3.0 23.1 %collective-permute-start.1 = (bf16[128,2048]{1,0:T(8,128)(2,1)}, bf16[128,2048]{1,0:T(8,128)(2,1)S(1)}, u32[]{:S(2)}, u32[]{:S(2)}) collective-permute-start(bf16[128,2048]{1,0:T(8,128)(2,1)} %q_ref.3), channel_id=1, source_target_pairs={{4,0},{8,4},{12,8},{16,12},{20,16},{24,20},{28,24},{5,1},{9,5},{13... | collective-permute-start | bytes 1572872 | tf_op jit(solution)/shard_map/ppermute | solution.py:25
  5.2 1.0 %copy-start = (bf16[128,2048]{1,0:T(8,128)(2,1)S(1)}, bf16[128,2048]{1,0:T(8,128)(2,1)}, u32[]{:S(2)}) copy-start(bf16[128,2048]{1,0:T(8,128)(2,1)} %k_ref.5) | copy-start | bytes 1572868
  6.2 1.0 %copy-start.2 = (bf16[128,2048]{1,0:T(8,128)(2,1)S(1)}, bf16[128,2048]{1,0:T(8,128)(2,1)}, u32[]{:S(2)}) copy-start(bf16[128,2048]{1,0:T(8,128)(2,1)} %v_ref.5) | copy-start | bytes 1572868
  7.3 1.0 %copy-start.4 = (bf16[128,2048]{1,0:T(8,128)(2,1)S(1)}, bf16[128,2048]{1,0:T(8,128)(2,1)}, u32[]{:S(2)}) copy-start(bf16[128,2048]{1,0:T(8,128)(2,1)} %q_ref.3) | copy-start | bytes 1572868
  8.3 1.0 %copy-start.6 = (bf16[128,2048]{1,0:T(8,128)(2,1)S(1)}, bf16[128,2048]{1,0:T(8,128)(2,1)}, u32[]{:S(2)}) copy-start(bf16[128,2048]{1,0:T(8,128)(2,1)} %g_ref.1) | copy-start | bytes 1572868
  9.3 21.1 %copy-start.1 = (bf16[128,2048]{1,0:T(8,128)(2,1)S(1)}, bf16[128,2048]{1,0:T(8,128)(2,1)}, u32[]{:S(2)}) copy-start(bf16[128,2048]{1,0:T(8,128)(2,1)} %k_ref.5) | copy-start | bytes 1572868
  9.4 21.1 %copy-start.3 = (bf16[128,2048]{1,0:T(8,128)(2,1)S(1)}, bf16[128,2048]{1,0:T(8,128)(2,1)}, u32[]{:S(2)}) copy-start(bf16[128,2048]{1,0:T(8,128)(2,1)} %v_ref.5) | copy-start | bytes 1572868
  10.3 20.2 %collective-permute-start.2 = (bf16[136,2048]{1,0:T(8,128)(2,1)S(1)}, bf16[136,2048]{1,0:T(8,128)(2,1)S(1)}, u32[]{:S(2)}, u32[]{:S(2)}) collective-permute-start(bf16[136,2048]{1,0:T(8,128)(2,1)S(1)} %own_stats.1.own_ref), channel_id=1, source_target_pairs={{4,0},{8,4},{12,8},{16,12},{20,16},{24,20},{28,24},{5,1},{9,5},{13... | collective-permute-start | bytes 1671176 | tf_op jit(solution)/shard_map/ppermute | solution.py:25
  14.0 5.8 %collective-permute-start.3 = (bf16[2,2,1,2048]{3,2,1,0:T(2,128)(2,1)S(1)}, bf16[2,2,1,2048]{3,2,1,0:T(2,128)(2,1)S(1)}, u32[]{:S(2)}, u32[]{:S(2)}) collective-permute-start(bf16[2,2,1,2048]{3,2,1,0:T(2,128)(2,1)S(1)} %copy_dynamic-update-slice_fusion), channel_id=1, source_target_pairs={{0,8},{4,12},{8,16},{12,20},{16,24},{20,28},{1,9},{5,13},{9,17},{1... | collective-permute-start | bytes 49160 | tf_op jit(solution)/shard_map/ppermute | solution.py:25
  19.9 6.2 %collective-permute-start.4 = (bf16[2,2,2,2048]{3,2,1,0:T(2,128)(2,1)S(1)}, bf16[2,2,2,2048]{3,2,1,0:T(2,128)(2,1)S(1)}, u32[]{:S(2)}, u32[]{:S(2)}) collective-permute-start(bf16[2,2,2,2048]{3,2,1,0:T(2,128)(2,1)S(1)} %pad_maximum_fusion.1), channel_id=1, source_target_pairs={{0,16},{4,20},{8,24},{12,28},{1,17},{5,21},{9,25},{13,29},{2,18},{... | collective-permute-start | bytes 98312 | tf_op jit(solution)/shard_map/ppermute | solution.py:25
  30.5 20.5 %copy-start.5 = (bf16[128,2048]{1,0:T(8,128)(2,1)S(1)}, bf16[128,2048]{1,0:T(8,128)(2,1)}, u32[]{:S(2)}) copy-start(bf16[128,2048]{1,0:T(8,128)(2,1)} %q_ref.3) | copy-start | bytes 1572868
  30.5 20.5 %copy-start.7 = (bf16[128,2048]{1,0:T(8,128)(2,1)S(1)}, bf16[128,2048]{1,0:T(8,128)(2,1)}, u32[]{:S(2)}) copy-start(bf16[128,2048]{1,0:T(8,128)(2,1)} %g_ref.1) | copy-start | bytes 1572868
  32.6 18.3 %collective-permute-start.5 = (bf16[136,2048]{1,0:T(8,128)(2,1)S(1)}, bf16[136,2048]{1,0:T(8,128)(2,1)S(1)}, u32[]{:S(2)}, u32[]{:S(2)}) collective-permute-start(bf16[136,2048]{1,0:T(8,128)(2,1)S(1)} %get-tuple-element.9), channel_id=1, source_target_pairs={{0,4},{4,8},{8,12},{12,16},{16,20},{20,24},{24,28},{1,5},{5,9},{9,... | collective-permute-start | bytes 1671176 | tf_op jit(solution)/shard_map/ppermute | solution.py:25

commit v4 on v3

v4 whole, which is shorter than its diff:
```python
import functools

import jax
import jax.numpy as jnp
from jax import lax
from jax.experimental import pallas as pl
from jax.experimental.pallas import tpu as pltpu
from jax.sharding import PartitionSpec as P

E = 128
B = 128
STAT_ROWS = 8
MASKED = -1e30
F32 = jnp.float32
BF16 = jnp.bfloat16


def dot(a, b, contract):
    return lax.dot_general(a, b, (contract, ((), ())), preferred_element_type=F32)


def passed_along(block, distance):
    count = lax.axis_size("seq")
    route = [(i - distance, i) for i in range(count) if 0 <= i - distance < count]
    return lax.ppermute(block, "seq", route)


def in_three(x):
    high = x.astype(BF16).astype(F32)
    middle = (x - high).astype(BF16).astype(F32)
    low = (x - high - middle).astype(BF16).astype(F32)
    return [high, middle, low]


def stat_rows(log_total, inner):
    rows = in_three(log_total) + in_three(inner)
    rows.append(jnp.zeros((STAT_ROWS - len(rows), E), F32))
    return jnp.concatenate(rows, axis=0).astype(BF16)


def stats_of(rows):
    rows = rows.astype(F32)
    return rows[0:1] + rows[1:2] + rows[2:3], rows[3:4] + rows[4:5] + rows[5:6]


def head_columns(head):
    return slice(head * E, (head + 1) * E)


def own_kernel(
    heads, q_ref, k_ref, v_ref, g_ref, out_ref, stats_ref, weight_ref, gp_ref, top_ref
):
    key = lax.broadcasted_iota(jnp.int32, (B, B), 0)
    query = lax.broadcasted_iota(jnp.int32, (B, B), 1)
    allowed = key <= query
    for h in range(heads):
        cols = head_columns(h)
        q, k, v, g = q_ref[:, cols], k_ref[:, cols], v_ref[:, cols], g_ref[:, cols]
        logits = jnp.where(allowed, dot(k, q, ((1,), (1,))) * E**-0.5, MASKED)
        top = jnp.max(logits, axis=0, keepdims=True)
        weight = jnp.exp(logits - top)
        grad_probs = dot(v, g, ((1,), (1,)))
        total = jnp.sum(weight, axis=0, keepdims=True)
        inner = jnp.sum(weight * grad_probs, axis=0, keepdims=True)
        out_ref[:B, cols] = g
        stats = stat_rows(top + jnp.log(total), inner / total)
        out_ref[B:, cols] = stats
        stats_ref[:, cols] = stats
        weight_ref[h] = weight
        gp_ref[h] = grad_probs
        top_ref[h : h + 1, :] = top


def with_summary(block, summary_ref, which, cols, padded):
    pairs = summary_ref.shape[2]
    parts = [summary_ref[i, which, :, cols].astype(F32) for i in range(2)]
    if padded > 2 * pairs:
        parts.append(jnp.zeros((padded - 2 * pairs, E), F32))
    return jnp.concatenate([block, jnp.concatenate(parts, axis=0).astype(BF16)], axis=0)


def cross_weights_kernel(heads, padded, place_ref, q_ref, k_ref, summary_ref, weight_ref, sums_ref):
    place = place_ref[0]
    pairs = summary_ref.shape[2]
    key = lax.broadcasted_iota(jnp.int32, (B + padded, B), 0)
    query = lax.broadcasted_iota(jnp.int32, (B + padded, B), 1)
    same, other = key - B, key - B - pairs
    pair = lax.shift_right_logical(place, 1)
    allowed = (key < B) & ((key > query) | (key == B - 1))
    allowed |= (same >= 1) & (same < pairs) & (same <= pair)
    allowed |= (other >= 1 - (place & 1)) & (other < pairs) & (other <= pair)
    for h in range(heads):
        cols = head_columns(h)
        k = with_summary(k_ref[:, cols], summary_ref, 0, cols, padded)
        logits = jnp.where(allowed, dot(k, q_ref[:, cols], ((1,), (1,))) * E**-0.5, MASKED)
        top = jnp.max(logits, axis=0, keepdims=True)
        weight = jnp.exp(logits - top)
        weight_ref[h] = weight
        sums_ref[h : h + 1, :] = top
        sums_ref[heads + h : heads + h + 1, :] = jnp.sum(weight, axis=0, keepdims=True)


def cross_scores_kernel(
    heads, padded, q_ref, g_ref, v_ref, summary_ref, weight_ref, sums_ref,
    low_ref, grads_ref, stats_ref, same_ref, other_ref
):
    pairs = summary_ref.shape[2]
    scale = E**-0.5
    for h in range(heads):
        cols = head_columns(h)
        v = with_summary(v_ref[:, cols], summary_ref, 1, cols, padded)
        grad_probs = dot(v, g_ref[:B, cols], ((1,), (1,)))
        own_log, own_inner = stats_of(g_ref[B:, cols])
        cross_top = sums_ref[h : h + 1, :]
        weight = weight_ref[h]
        top = jnp.maximum(cross_top, own_log)
        own_weight = jnp.exp(own_log - top)
        cross_weight = jnp.exp(cross_top - top)
        total = own_weight + cross_weight * sums_ref[heads + h : heads + h + 1, :]
        own_part = own_weight / total
        cross_part = cross_weight / total
        inner = own_part * own_inner + cross_part * jnp.sum(
            weight * grad_probs, axis=0, keepdims=True
        )
        probs = weight * cross_part
        low_ref[h] = probs.astype(BF16)
        grads_ref[h] = (probs * (grad_probs - inner)).astype(BF16)
        stats_ref[:, cols] = stat_rows(top + jnp.log(total), inner)
    for h in range(heads):
        cols = head_columns(h)
        grad_k = scale * dot(grads_ref[h, B:, :], q_ref[:, cols], ((1,), (0,)))
        grad_v = dot(low_ref[h, B:, :], g_ref[:B, cols], ((1,), (0,)))
        for i, grad in enumerate((grad_k, grad_v)):
            same_ref[i, :, cols] = grad[:pairs]
            other_ref[i, :, cols] = grad[pairs : 2 * pairs]


def cross_queries_kernel(heads, padded, k_ref, summary_ref, grads_ref, stats_ref, gq_ref):
    gq_ref[B:, :] = stats_ref[...]
    for h in range(heads):
        cols = head_columns(h)
        k = with_summary(k_ref[:, cols], summary_ref, 0, cols, padded)
        gq_ref[:B, cols] = (E**-0.5 * dot(grads_ref[h], k, ((0,), (0,)))).astype(BF16)


def cross_keys_kernel(heads, q_ref, g_ref, low_ref, grads_ref, gk_ref, gv_ref):
    for h in range(heads):
        cols = head_columns(h)
        gk_ref[:, cols] = E**-0.5 * dot(grads_ref[h, :B, :], q_ref[:, cols], ((1,), (0,)))
        gv_ref[:, cols] = dot(low_ref[h, :B, :], g_ref[:B, cols], ((1,), (0,)))


def final_kernel(
    heads, place_ref, q_ref, g_ref, k_ref, own_ref, weight_ref, gp_ref, top_ref, back_ref,
    gk_ref, gv_ref, gs_ref, out_q_ref, out_k_ref, out_v_ref,
    low, grads, done_q, done_k, done_v, sems
):
    first = place_ref[0] == 0
    scale = E**-0.5
    group = heads // 4 if heads % 4 == 0 else heads
    last_row = lax.broadcasted_iota(jnp.int32, (B, B), 0) == B - 1
    for h in range(heads):
        cols = head_columns(h)
        log_total, inner = stats_of(jnp.where(first, own_ref[:, cols], back_ref[B:, cols]))
        probs = weight_ref[h] * jnp.exp(top_ref[h : h + 1, :] - log_total)
        low[h] = probs.astype(BF16)
        grads[h] = (probs * (gp_ref[h] - inner)).astype(BF16)

    copies = []
    for h in range(heads):
        cols = head_columns(h)
        grad_logits = grads[h]
        grad_q = scale * dot(grad_logits, k_ref[:, cols], ((0,), (0,)))
        grad_k = scale * dot(grad_logits, q_ref[:, cols], ((1,), (0,)))
        grad_v = dot(low[h], g_ref[:, cols], ((1,), (0,)))
        grad_k += gk_ref[:, cols] + jnp.where(last_row, gs_ref[0, :, cols], 0.0)
        grad_v += gv_ref[:, cols] + jnp.where(last_row, gs_ref[1, :, cols], 0.0)
        done_q[:, cols] = (grad_q + back_ref[:B, cols].astype(F32)).astype(BF16)
        done_k[:, cols] = grad_k.astype(BF16)
        done_v[:, cols] = grad_v.astype(BF16)
        if (h + 1) % group == 0:
            part = slice((h + 1 - group) * E, (h + 1) * E)
            for done, out in (done_q, out_q_ref), (done_k, out_k_ref), (done_v, out_v_ref):
                copies.append(
                    pltpu.make_async_copy(
                        done.at[:, part], out.at[:, part], sems.at[len(copies)]
                    )
                )
                copies[-1].start()
    for copy in copies:
        copy.wait()


def body(queries, key_vectors, value_vectors, grad_out):
    shard_len, features = queries.shape
    count = lax.axis_size("seq")
    assert shard_len == B and count % 2 == 0
    heads = features // E
    place = lax.axis_index("seq").astype(jnp.int32).reshape(1)
    vmem = pl.BlockSpec(memory_space=pltpu.VMEM)
    smem = pl.BlockSpec(memory_space=pltpu.SMEM)
    anywhere = pl.BlockSpec(memory_space=pl.ANY)

    def kernel(function, name, products, inputs, outputs, spec=vmem, scratch=(), scalar=False):
        out_shape = [jax.ShapeDtypeStruct(shape, kind) for shape, kind in outputs]
        moved = sum(x.size * x.dtype.itemsize for x in (*inputs, *out_shape))
        return pl.pallas_call(
            function,
            in_specs=[smem] * scalar + [vmem] * (len(inputs) - scalar),
            out_specs=[spec] * len(out_shape),
            out_shape=out_shape,
            scratch_shapes=scratch,
            compiler_params=pltpu.CompilerParams(vmem_limit_bytes=16 << 20),
            cost_estimate=pl.CostEstimate(
                flops=products * 2 * heads * B * B * E,
                bytes_accessed=moved,
                transcendentals=heads * B * B,
            ),
            name=name,
        )(*inputs)

    rows = jnp.stack([key_vectors[B - 1 :], value_vectors[B - 1 :]])
    grad_stats, own_stats, weight, grad_probs, top = kernel(
        functools.partial(own_kernel, heads),
        "own",
        2,
        (queries, key_vectors, value_vectors, grad_out),
        [
            ((B + STAT_ROWS, features), BF16),
            ((STAT_ROWS, features), BF16),
            ((heads, B, B), F32),
            ((heads, B, B), F32),
            ((heads, B), F32),
        ],
    )

    across = [(i, i ^ 1) for i in range(count)]
    swap = lax.ppermute(rows, "seq", across)
    rows, queries = lax.optimization_barrier((rows, queries))
    next_q = passed_along(queries, -1)
    summary = jnp.stack([rows, swap])
    _, grad_stats = lax.optimization_barrier((swap, grad_stats))
    while 2 * summary.shape[2] < count:
        earlier = passed_along(summary, 2 * summary.shape[2])
        summary = jnp.concatenate([summary, earlier], axis=2)
    pairs = summary.shape[2]
    padded = -(-2 * pairs // 16) * 16
    next_g = passed_along(grad_stats, -1)

    wide = heads, B + padded, B
    cross_weight, cross_sums = kernel(
        functools.partial(cross_weights_kernel, heads, padded),
        "cross_weights",
        1,
        (place, next_q, key_vectors, summary),
        [(wide, F32), ((2 * heads, B), F32)],
        scalar=True,
    )
    low, grads, stats, same, other = kernel(
        functools.partial(cross_scores_kernel, heads, padded),
        "cross_scores",
        2,
        (next_q, next_g, value_vectors, summary, cross_weight, cross_sums),
        [
            (wide, BF16),
            (wide, BF16),
            ((STAT_ROWS, features), BF16),
            ((2, pairs, features), F32),
            ((2, pairs, features), F32),
        ],
    )
    other = lax.ppermute(other, "seq", across)
    (grad_q_next,) = kernel(
        functools.partial(cross_queries_kernel, heads, padded),
        "cross_queries",
        1,
        (key_vectors, summary, grads, stats),
        [((B + STAT_ROWS, features), BF16)],
    )
    back = passed_along(grad_q_next, 1)
    grad_k, grad_v = kernel(
        functools.partial(cross_keys_kernel, heads),
        "cross_keys",
        2,
        (next_q, next_g, low, grads),
        [((B, features), F32)] * 2,
    )
    grad_summary = same + other
    while pairs > 1:
        ways = 4 if pairs % 4 == 0 else 2
        pairs //= ways
        parts = [grad_summary[:, i * pairs : (i + 1) * pairs] for i in range(ways)]
        sent = [passed_along(parts[i], -2 * pairs * i) for i in range(1, ways)]
        grad_summary = sum(sent, parts[0])

    return kernel(
        functools.partial(final_kernel, heads),
        "final",
        3,
        (
            place,
            queries,
            grad_out,
            key_vectors,
            own_stats,
            weight,
            grad_probs,
            top,
            back,
            grad_k,
            grad_v,
            grad_summary,
        ),
        [((B, features), BF16)] * 3,
        spec=anywhere,
        scratch=[
            pltpu.VMEM((heads, B, B), BF16),
            pltpu.VMEM((heads, B, B), BF16),
            pltpu.VMEM((B, features), BF16),
            pltpu.VMEM((B, features), BF16),
            pltpu.VMEM((B, features), BF16),
            pltpu.SemaphoreType.DMA((12,)),
        ],
        scalar=True,
    )


def solution(mesh):
    spec = P(("dp", "seq"), "head")
    return jax.shard_map(
        body,
        mesh=mesh,
        in_specs=(spec,) * 4,
        out_specs=(spec,) * 3,
        check_vma=False,
    )
```

time: 54.3 us -> 51.9 us (0.956)
  blocking collectives: 15 us -> 0 us
  waiting for transfers between devices: 8.45 us -> 14.3 us
  starting transfers between devices: 18.4 us -> 23.9 us
  local copies, waits for them, and re-layouts: 5.01 us -> 6.06 us
  Pallas kernels: 5.39 us -> 6.02 us
    all_to_all x1 -> x0, blocking collectives: 15 us -> none  [body(): grad_summary = lax.all_to_all(grad_summary, 'seq', 0, 0, tiled=True)]
    ppermute x5 -> x8, waiting for transfers between devices: 8.29 us -> 14.3 us  [passed_along(): return lax.ppermute(block, 'seq', route)]
    ppermute x5 -> x8, starting transfers between devices: 16.9 us -> 20.8 us  [passed_along(): return lax.ppermute(block, 'seq', route)]
    ppermute x1 -> x2, starting transfers between devices: 1.58 us -> 3.04 us  [the longest x1 1.58 us: body(): swap = lax.ppermute(rows, 'seq', across)]
    unnamed x17 -> x21, local copies, waits for them, and re-layouts: 4.19 us -> 5.2 us
    pallas_call x3 -> x6, Pallas kernels: 5.39 us -> 6.02 us  [kernel(): pl.pallas_call(function, in_specs=[smem] * scalar + [vmem] * (len(inputs)...]
  transfers between devices with their start and end apart: 6 -> 10, of which waited for: 4 -> 6; matrix products, arithmetic and copies ran while one was open for 0% -> 1% of each run, Pallas kernels for 2% -> 6%
where the time goes in v4:
time: 51.9 us; the launch traced here: 51.4 us
  starting transfers between devices  23.9 us (46%)
  waiting for transfers between devices  14.3 us (28%)
  local copies, waits for them, and re-layouts  6.06 us (12%)
  Pallas kernels  6.02 us (12%)
  between operations  0.82 us (2%)
    ppermute x8, starting transfers between devices, passed_along(): return lax.ppermute(block, 'seq', route)  20.8 us
    ppermute x8, waiting for transfers between devices, passed_along(): return lax.ppermute(block, 'seq', route)  14.3 us
    pallas_call x6, Pallas kernels, kernel(): pl.pallas_call(function, in_specs=[smem] * scalar + [vmem] * (len(inputs)...  6.02 us
    unnamed x21, local copies, waits for them, and re-layouts  5.2 us
    ppermute x1, starting transfers between devices, body(): swap = lax.ppermute(rows, 'seq', across)  1.58 us
    ppermute x1, starting transfers between devices, body(): other = lax.ppermute(other, 'seq', across)  1.45 us
  transfers between devices with their start and end apart: 10, of which 6 were waited for; matrix products, arithmetic and copies ran while one was open for 1% of the time, Pallas kernels for 6%

profile of v4, /device:TPU:8, one launch (start us, length us, event | category | flops | bytes accessed | tf_op | source)
XLA Modules:
  0.0 51.4 jit_solution(3130913702287221690)
XLA Ops:
  0.6 0.8 %slice_bitcast_fusion = (bf16[1,1,2048]{2,0,1:T(2,128)(2,1)S(1)}, bf16[1,1,2048]{2,0,1:T(2,128)(2,1)S(1)}) fusion(bf16[128,2048]{1,0:T(8,128)(2,1)} %v_ref.3, bf16[128,2048]{1,0:T(8,128)(2,1)} %k_ref.7), kind=kLoop, calls=%fused_computation.8 | loop fusion | bytes 16384 | tf_op jit(solution)/shard_map/stack | solution.py:222
  1.5 1.6 %collective-permute-start = (bf16[2,1,2048]{2,0,1:T(2,128)(2,1)S(1)}, bf16[2,1,2048]{2,0,1:T(2,128)(2,1)S(1)}, u32[]{:S(2)}, u32[]{:S(2)}) collective-permute-start(bf16[2,1,2048]{2,0,1:T(2,128)(2,1)S(1)} %pad_maximum_fusion.2), channel_id=1, source_target_pairs={{0,4},{4,0},{8,12},{12,8},{16,20},{20,16},{24,28},{28,24},{1,5},{5... | collective-permute-start | bytes 24584 | tf_op jit(solution)/shard_map/ppermute | solution.py:238
  3.0 1.9 %collective-permute-start.3 = (bf16[128,2048]{1,0:T(8,128)(2,1)}, bf16[128,2048]{1,0:T(8,128)(2,1)S(1)}, u32[]{:S(2)}, u32[]{:S(2)}) collective-permute-start(bf16[128,2048]{1,0:T(8,128)(2,1)} %q_ref.2), channel_id=1, source_target_pairs={{4,0},{8,4},{12,8},{16,12},{20,16},{24,20},{28,24},{5,1},{9,5},{13... | collective-permute-start | bytes 1572872 | tf_op jit(solution)/shard_map/ppermute | solution.py:25
  5.0 0.0 copy-start
  5.0 1.0 %copy-done = bf16[128,2048]{1,0:T(8,128)(2,1)S(1)} copy-done((bf16[128,2048]{1,0:T(8,128)(2,1)S(1)}, bf16[128,2048]{1,0:T(8,128)(2,1)}, u32[]{:S(2)}) %copy-start) | copy-done | bytes 524312
  6.0 1.0 %copy-done.2 = bf16[128,2048]{1,0:T(8,128)(2,1)S(1)} copy-done((bf16[128,2048]{1,0:T(8,128)(2,1)S(1)}, bf16[128,2048]{1,0:T(8,128)(2,1)}, u32[]{:S(2)}) %copy-start.2) | copy-done | bytes 524312
  7.1 1.0 %copy-done.4 = bf16[128,2048]{1,0:T(8,128)(2,1)S(1)} copy-done((bf16[128,2048]{1,0:T(8,128)(2,1)S(1)}, bf16[128,2048]{1,0:T(8,128)(2,1)}, u32[]{:S(2)}) %copy-start.4) | copy-done | bytes 524312
  8.1 1.0 %copy-done.6 = bf16[128,2048]{1,0:T(8,128)(2,1)S(1)} copy-done((bf16[128,2048]{1,0:T(8,128)(2,1)S(1)}, bf16[128,2048]{1,0:T(8,128)(2,1)}, u32[]{:S(2)}) %copy-start.6) | copy-done | bytes 524312
  9.2 1.7 %own.1 = (bf16[136,2048]{1,0:T(8,128)(2,1)}, bf16[8,2048]{1,0:T(8,128)(2,1)S(1)}, f32[16,128,128]{2,1,0:T(8,128)S(1)}, f32[16,128,128]{2,1,0:T(8,128)S(1)}, f32[16,128]{1,0:T(8,128)S(1)}) custom-call(bf16[128,2048]{1,0:T(8,128)(2,1)S(1)} %copy-done.4, bf16[128,2048]{1,0:T(8,128)(2,1)S(1)} %copy-done, bf16[128,2048]{1,0:T(8,128)(2,1)S(1)} %copy-done.2, ...), custom_call_target="tpu_custom_call" | custom-call | flops 134217728 | bytes 4792320 | tf_op jit(solution)/shard_map/own/pallas_call | solution.py:207
  10.9 1.0 %copy-done.8 = f32[16,128,128]{2,1,0:T(8,128)} copy-done((f32[16,128,128]{2,1,0:T(8,128)}, f32[16,128,128]{2,1,0:T(8,128)S(1)}, u32[]{:S(2)}) %copy-start.8) | copy-done | bytes 1048600
  11.9 3.9 %collective-permute-start.4 = (bf16[136,2048]{1,0:T(8,128)(2,1)}, bf16[136,2048]{1,0:T(8,128)(2,1)S(1)}, u32[]{:S(2)}, u32[]{:S(2)}) collective-permute-start(bf16[136,2048]{1,0:T(8,128)(2,1)} %get-tuple-element.27), channel_id=1, source_target_pairs={{4,0},{8,4},{12,8},{16,12},{20,16},{24,20},{28,24},{5,1},{9,5},{13... | collective-permute-start | bytes 1671176 | tf_op jit(solution)/shard_map/ppermute | solution.py:25
  15.9 3.5 %collective-permute-start.1 = (bf16[2,2,1,2048]{3,2,1,0:T(2,128)(2,1)S(1)}, bf16[2,2,1,2048]{3,2,1,0:T(2,128)(2,1)S(1)}, u32[]{:S(2)}, u32[]{:S(2)}) collective-permute-start(bf16[2,2,1,2048]{3,2,1,0:T(2,128)(2,1)S(1)} %copy_dynamic-update-slice_fusion), channel_id=1, source_target_pairs={{0,8},{4,12},{8,16},{12,20},{16,24},{20,28},{1,9},{5,13},{9,17},{1... | collective-permute-start | bytes 49160 | tf_op jit(solution)/shard_map/ppermute | solution.py:25
  19.4 2.3 %collective-permute-done.1 = bf16[2,2,1,2048]{3,2,1,0:T(2,128)(2,1)S(1)} collective-permute-done((bf16[2,2,1,2048]{3,2,1,0:T(2,128)(2,1)S(1)}, bf16[2,2,1,2048]{3,2,1,0:T(2,128)(2,1)S(1)}, u32[]{:S(2)}, u32[]{:S(2)}) %collective-permute-start.1) | collective-permute-done | bytes 16416 | tf_op jit(solution)/shard_map/ppermute | solution.py:25
  21.7 0.1 pad_maximum_fusion.1
  21.8 4.5 %collective-permute-start.2 = (bf16[2,2,2,2048]{3,2,1,0:T(2,128)(2,1)S(1)}, bf16[2,2,2,2048]{3,2,1,0:T(2,128)(2,1)S(1)}, u32[]{:S(2)}, u32[]{:S(2)}) collective-permute-start(bf16[2,2,2,2048]{3,2,1,0:T(2,128)(2,1)S(1)} %pad_maximum_fusion.1), channel_id=1, source_target_pairs={{0,16},{4,20},{8,24},{12,28},{1,17},{5,21},{9,25},{13,29},{2,18},{... | collective-permute-start | bytes 98312 | tf_op jit(solution)/shard_map/ppermute | solution.py:25
  26.3 1.7 %collective-permute-done.2 = bf16[2,2,2,2048]{3,2,1,0:T(2,128)(2,1)S(1)} collective-permute-done((bf16[2,2,2,2048]{3,2,1,0:T(2,128)(2,1)S(1)}, bf16[2,2,2,2048]{3,2,1,0:T(2,128)(2,1)S(1)}, u32[]{:S(2)}, u32[]{:S(2)}) %collective-permute-start.2) | collective-permute-done | bytes 32800 | tf_op jit(solution)/shard_map/ppermute | solution.py:25
  28.0 0.1 pad_maximum_fusion.summary_ref
  28.1 0.6 %cross_weights.1 = (f32[16,144,128]{2,1,0:T(8,128)S(1)}, f32[32,128]{1,0:T(8,128)S(1)}) custom-call(s32[1]{0:T(128)} %bitcast.place_ref, bf16[128,2048]{1,0:T(8,128)(2,1)S(1)} %collective-permute-done.3.q_ref, bf16[128,2048]{1,0:T(8,128)(2,1)S(1)} %copy-done.1, bf16[2,2,4,2048]{3,2,1,0:T(4,128)(2,1)S(1)} %pad_maximum_fusion.summary_ref), custom_call_target="tpu_custom_call" | custom-call | flops 67108864 | bytes 2310148 | tf_op jit(solution)/shard_map/cross_weights/pallas_call | solution.py:207
  28.7 1.7 %collective-permute-done.4.g_ref = bf16[136,2048]{1,0:T(8,128)(2,1)S(1)} collective-permute-done((bf16[136,2048]{1,0:T(8,128)(2,1)}, bf16[136,2048]{1,0:T(8,128)(2,1)S(1)}, u32[]{:S(2)}, u32[]{:S(2)}) %collective-permute-start.4) | collective-permute-done | bytes 557088 | tf_op jit(solution)/shard_map/ppermute | solution.py:25
  30.5 0.9 %cross_scores.1 = (bf16[16,144,128]{2,1,0:T(8,128)(2,1)S(1)}, bf16[16,144,128]{2,1,0:T(8,128)(2,1)S(1)}, bf16[8,2048]{1,0:T(8,128)(2,1)S(1)}, f32[2,4,2048]{2,1,0:T(4,128)S(1)}, f32[2,4,2048]{2,1,0:T(4,128)S(1)}) custom-call(bf16[128,2048]{1,0:T(8,128)(2,1)S(1)} %collective-permute-done.3.q_ref, bf16[136,2048]{1,0:T(8,128)(2,1)S(1)} %collective-permute-done.4.g_ref, ...), custom_call_target="tpu_custom_call" | custom-call | flops 134217728 | bytes 4210688 | tf_op jit(solution)/shard_map/cross_scores/pallas_call | solution.py:207
  31.4 1.5 %collective-permute-start.6 = (f32[2,4,2048]{2,1,0:T(4,128)S(1)}, f32[2,4,2048]{2,1,0:T(4,128)S(1)}, u32[]{:S(2)}, u32[]{:S(2)}) collective-permute-start(f32[2,4,2048]{2,1,0:T(4,128)S(1)} %get-tuple-element.36), channel_id=1, source_target_pairs={{0,4},{4,0},{8,12},{12,8},{16,20},{20,16},{24,28},{28,24},{1,5},{5... | collective-permute-start | bytes 196616 | tf_op jit(solution)/shard_map/ppermute | solution.py:272
  32.8 0.5 cross_queries.1
  33.3 2.5 %collective-permute-start.5 = (bf16[136,2048]{1,0:T(8,128)(2,1)S(1)}, bf16[136,2048]{1,0:T(8,128)(2,1)S(1)}, u32[]{:S(2)}, u32[]{:S(2)}) collective-permute-start(bf16[136,2048]{1,0:T(8,128)(2,1)S(1)} %cross_queries.1), channel_id=1, source_target_pairs={{0,4},{4,8},{8,12},{12,16},{16,20},{20,24},{24,28},{1,5},{5,9},{9,... | collective-permute-start | bytes 1671176 | tf_op jit(solution)/shard_map/ppermute | solution.py:25
  36.0 2.4 %collective-permute-start.7 = (f32[2,1,2048]{2,1,0:T(1,128)S(1)}, f32[2,1,2048]{2,1,0:T(1,128)S(1)}, u32[]{:S(2)}, u32[]{:S(2)}) collective-permute-start(f32[2,1,2048]{2,1,0:T(1,128)S(1)} %get-tuple-element.37), channel_id=1, source_target_pairs={{8,0},{12,4},{16,8},{20,12},{24,16},{28,20},{9,1},{13,5},{17,9},{2... | collective-permute-start | bytes 49160 | tf_op jit(solution)/shard_map/ppermute | solution.py:25
  38.4 0.0 copy-start.5
  38.4 1.4 %collective-permute-start.8 = (f32[2,1,2048]{2,1,0:T(1,128)S(1)}, f32[2,1,2048]{2,1,0:T(1,128)S(1)}, u32[]{:S(2)}, u32[]{:S(2)}) collective-permute-start(f32[2,1,2048]{2,1,0:T(1,128)S(1)} %get-tuple-element.39), channel_id=1, source_target_pairs={{16,0},{20,4},{24,8},{28,12},{17,1},{21,5},{25,9},{29,13},{18,2},{... | collective-permute-start | bytes 49160 | tf_op jit(solution)/shard_map/ppermute | solution.py:25
  39.8 0.7 %collective-permute-start.9 = (f32[2,1,2048]{2,1,0:T(1,128)S(1)}, f32[2,1,2048]{2,1,0:T(1,128)S(1)}, u32[]{:S(2)}, u32[]{:S(2)}) collective-permute-start(f32[2,1,2048]{2,1,0:T(1,128)S(1)} %get-tuple-element.38), channel_id=1, source_target_pairs={{24,0},{28,4},{25,1},{29,5},{26,2},{30,6},{27,3},{31,7}} | collective-permute-start | bytes 49160 | tf_op jit(solution)/shard_map/ppermute | solution.py:25
  40.5 0.4 cross_keys.1
  40.9 0.7 %collective-permute-done.7 = f32[2,1,2048]{2,1,0:T(1,128)S(1)} collective-permute-done((f32[2,1,2048]{2,1,0:T(1,128)S(1)}, f32[2,1,2048]{2,1,0:T(1,128)S(1)}, u32[]{:S(2)}, u32[]{:S(2)}) %collective-permute-start.7) | collective-permute-done | bytes 16416 | tf_op jit(solution)/shard_map/ppermute | solution.py:25
  41.6 3.5 %collective-permute-done.8 = f32[2,1,2048]{2,1,0:T(1,128)S(1)} collective-permute-done((f32[2,1,2048]{2,1,0:T(1,128)S(1)}, f32[2,1,2048]{2,1,0:T(1,128)S(1)}, u32[]{:S(2)}, u32[]{:S(2)}) %collective-permute-start.8) | collective-permute-done | bytes 16416 | tf_op jit(solution)/shard_map/ppermute | solution.py:25
  45.1 4.5 %collective-permute-done.5.back_ref = bf16[136,2048]{1,0:T(8,128)(2,1)S(1)} collective-permute-done((bf16[136,2048]{1,0:T(8,128)(2,1)S(1)}, bf16[136,2048]{1,0:T(8,128)(2,1)S(1)}, u32[]{:S(2)}, u32[]{:S(2)}) %collective-permute-start.5) | collective-permute-done | bytes 557088 | tf_op jit(solution)/shard_map/ppermute | solution.py:25
  49.6 1.8 %final.1 = (bf16[128,2048]{1,0:T(8,128)(2,1)}, bf16[128,2048]{1,0:T(8,128)(2,1)}, bf16[128,2048]{1,0:T(8,128)(2,1)}) custom-call(s32[1]{0:T(128)} %bitcast.place_ref, bf16[128,2048]{1,0:T(8,128)(2,1)S(1)} %copy-done.5, bf16[128,2048]{1,0:T(8,128)(2,1)S(1)} %copy-done.7, bf16[128,2048]{1,0:T(8,128)(2,1)S(1)} %copy-done.1, ...), custom_call_target="tpu_custom_call" | custom-call | flops 201326592 | bytes 7954436 | tf_op jit(solution)/shard_map/final/pallas_call | solution.py:207
  (23 shorter events, 0.2 us)
Async XLA Ops:
  1.5 10.5 %collective-permute-start = (bf16[2,1,2048]{2,0,1:T(2,128)(2,1)S(1)}, bf16[2,1,2048]{2,0,1:T(2,128)(2,1)S(1)}, u32[]{:S(2)}, u32[]{:S(2)}) collective-permute-start(bf16[2,1,2048]{2,0,1:T(2,128)(2,1)S(1)} %pad_maximum_fusion.2), channel_id=1, source_target_pairs={{0,4},{4,0},{8,12},{12,8},{16,20},{20,16},{24,28},{28,24},{1,5},{5... | collective-permute-start | bytes 24584 | tf_op jit(solution)/shard_map/ppermute | solution.py:238
  3.0 25.0 %collective-permute-start.3 = (bf16[128,2048]{1,0:T(8,128)(2,1)}, bf16[128,2048]{1,0:T(8,128)(2,1)S(1)}, u32[]{:S(2)}, u32[]{:S(2)}) collective-permute-start(bf16[128,2048]{1,0:T(8,128)(2,1)} %q_ref.2), channel_id=1, source_target_pairs={{4,0},{8,4},{12,8},{16,12},{20,16},{24,20},{28,24},{5,1},{9,5},{13... | collective-permute-start | bytes 1572872 | tf_op jit(solution)/shard_map/ppermute | solution.py:25
  5.0 1.0 %copy-start = (bf16[128,2048]{1,0:T(8,128)(2,1)S(1)}, bf16[128,2048]{1,0:T(8,128)(2,1)}, u32[]{:S(2)}) copy-start(bf16[128,2048]{1,0:T(8,128)(2,1)} %k_ref.7) | copy-start | bytes 1572868
  6.0 1.0 %copy-start.2 = (bf16[128,2048]{1,0:T(8,128)(2,1)S(1)}, bf16[128,2048]{1,0:T(8,128)(2,1)}, u32[]{:S(2)}) copy-start(bf16[128,2048]{1,0:T(8,128)(2,1)} %v_ref.3) | copy-start | bytes 1572868
  7.1 1.0 %copy-start.4 = (bf16[128,2048]{1,0:T(8,128)(2,1)S(1)}, bf16[128,2048]{1,0:T(8,128)(2,1)}, u32[]{:S(2)}) copy-start(bf16[128,2048]{1,0:T(8,128)(2,1)} %q_ref.2) | copy-start | bytes 1572868
  8.1 1.0 %copy-start.6 = (bf16[128,2048]{1,0:T(8,128)(2,1)S(1)}, bf16[128,2048]{1,0:T(8,128)(2,1)}, u32[]{:S(2)}) copy-start(bf16[128,2048]{1,0:T(8,128)(2,1)} %g_ref.3) | copy-start | bytes 1572868
  9.2 18.9 %copy-start.1 = (bf16[128,2048]{1,0:T(8,128)(2,1)S(1)}, bf16[128,2048]{1,0:T(8,128)(2,1)}, u32[]{:S(2)}) copy-start(bf16[128,2048]{1,0:T(8,128)(2,1)} %k_ref.7) | copy-start | bytes 1572868
  10.9 1.0 %copy-start.8 = (f32[16,128,128]{2,1,0:T(8,128)}, f32[16,128,128]{2,1,0:T(8,128)S(1)}, u32[]{:S(2)}) copy-start(f32[16,128,128]{2,1,0:T(8,128)S(1)} %get-tuple-element.23.gp_ref) | copy-start | bytes 3145732
  11.9 18.6 %copy-start.3 = (bf16[128,2048]{1,0:T(8,128)(2,1)S(1)}, bf16[128,2048]{1,0:T(8,128)(2,1)}, u32[]{:S(2)}) copy-start(bf16[128,2048]{1,0:T(8,128)(2,1)} %v_ref.3) | copy-start | bytes 1572868
  11.9 18.5 %collective-permute-start.4 = (bf16[136,2048]{1,0:T(8,128)(2,1)}, bf16[136,2048]{1,0:T(8,128)(2,1)S(1)}, u32[]{:S(2)}, u32[]{:S(2)}) collective-permute-start(bf16[136,2048]{1,0:T(8,128)(2,1)} %get-tuple-element.27), channel_id=1, source_target_pairs={{4,0},{8,4},{12,8},{16,12},{20,16},{24,20},{28,24},{5,1},{9,5},{13... | collective-permute-start | bytes 1671176 | tf_op jit(solution)/shard_map/ppermute | solution.py:25
  15.9 5.8 %collective-permute-start.1 = (bf16[2,2,1,2048]{3,2,1,0:T(2,128)(2,1)S(1)}, bf16[2,2,1,2048]{3,2,1,0:T(2,128)(2,1)S(1)}, u32[]{:S(2)}, u32[]{:S(2)}) collective-permute-start(bf16[2,2,1,2048]{3,2,1,0:T(2,128)(2,1)S(1)} %copy_dynamic-update-slice_fusion), channel_id=1, source_target_pairs={{0,8},{4,12},{8,16},{12,20},{16,24},{20,28},{1,9},{5,13},{9,17},{1... | collective-permute-start | bytes 49160 | tf_op jit(solution)/shard_map/ppermute | solution.py:25
  21.8 6.2 %collective-permute-start.2 = (bf16[2,2,2,2048]{3,2,1,0:T(2,128)(2,1)S(1)}, bf16[2,2,2,2048]{3,2,1,0:T(2,128)(2,1)S(1)}, u32[]{:S(2)}, u32[]{:S(2)}) collective-permute-start(bf16[2,2,2,2048]{3,2,1,0:T(2,128)(2,1)S(1)} %pad_maximum_fusion.1), channel_id=1, source_target_pairs={{0,16},{4,20},{8,24},{12,28},{1,17},{5,21},{9,25},{13,29},{2,18},{... | collective-permute-start | bytes 98312 | tf_op jit(solution)/shard_map/ppermute | solution.py:25
  31.4 4.5 %collective-permute-start.6 = (f32[2,4,2048]{2,1,0:T(4,128)S(1)}, f32[2,4,2048]{2,1,0:T(4,128)S(1)}, u32[]{:S(2)}, u32[]{:S(2)}) collective-permute-start(f32[2,4,2048]{2,1,0:T(4,128)S(1)} %get-tuple-element.36), channel_id=1, source_target_pairs={{0,4},{4,0},{8,12},{12,8},{16,20},{20,16},{24,28},{28,24},{1,5},{5... | collective-permute-start | bytes 196616 | tf_op jit(solution)/shard_map/ppermute | solution.py:272
  33.3 16.2 %collective-permute-start.5 = (bf16[136,2048]{1,0:T(8,128)(2,1)S(1)}, bf16[136,2048]{1,0:T(8,128)(2,1)S(1)}, u32[]{:S(2)}, u32[]{:S(2)}) collective-permute-start(bf16[136,2048]{1,0:T(8,128)(2,1)S(1)} %cross_queries.1), channel_id=1, source_target_pairs={{0,4},{4,8},{8,12},{12,16},{16,20},{20,24},{24,28},{1,5},{5,9},{9,... | collective-permute-start | bytes 1671176 | tf_op jit(solution)/shard_map/ppermute | solution.py:25
  36.0 5.6 %collective-permute-start.7 = (f32[2,1,2048]{2,1,0:T(1,128)S(1)}, f32[2,1,2048]{2,1,0:T(1,128)S(1)}, u32[]{:S(2)}, u32[]{:S(2)}) collective-permute-start(f32[2,1,2048]{2,1,0:T(1,128)S(1)} %get-tuple-element.37), channel_id=1, source_target_pairs={{8,0},{12,4},{16,8},{20,12},{24,16},{28,20},{9,1},{13,5},{17,9},{2... | collective-permute-start | bytes 49160 | tf_op jit(solution)/shard_map/ppermute | solution.py:25
  38.4 11.2 %copy-start.5 = (bf16[128,2048]{1,0:T(8,128)(2,1)S(1)}, bf16[128,2048]{1,0:T(8,128)(2,1)}, u32[]{:S(2)}) copy-start(bf16[128,2048]{1,0:T(8,128)(2,1)} %q_ref.2) | copy-start | bytes 1572868
  38.4 11.2 %copy-start.7 = (bf16[128,2048]{1,0:T(8,128)(2,1)S(1)}, bf16[128,2048]{1,0:T(8,128)(2,1)}, u32[]{:S(2)}) copy-start(bf16[128,2048]{1,0:T(8,128)(2,1)} %g_ref.3) | copy-start | bytes 1572868
  38.4 11.2 %copy-start.9 = (f32[16,128,128]{2,1,0:T(8,128)S(1)}, f32[16,128,128]{2,1,0:T(8,128)}, u32[]{:S(2)}) copy-start(f32[16,128,128]{2,1,0:T(8,128)} %copy-done.8) | copy-start | bytes 3145732
  38.4 6.7 %collective-permute-start.8 = (f32[2,1,2048]{2,1,0:T(1,128)S(1)}, f32[2,1,2048]{2,1,0:T(1,128)S(1)}, u32[]{:S(2)}, u32[]{:S(2)}) collective-permute-start(f32[2,1,2048]{2,1,0:T(1,128)S(1)} %get-tuple-element.39), channel_id=1, source_target_pairs={{16,0},{20,4},{24,8},{28,12},{17,1},{21,5},{25,9},{29,13},{18,2},{... | collective-permute-start | bytes 49160 | tf_op jit(solution)/shard_map/ppermute | solution.py:25
  39.8 5.2 %collective-permute-start.9 = (f32[2,1,2048]{2,1,0:T(1,128)S(1)}, f32[2,1,2048]{2,1,0:T(1,128)S(1)}, u32[]{:S(2)}, u32[]{:S(2)}) collective-permute-start(f32[2,1,2048]{2,1,0:T(1,128)S(1)} %get-tuple-element.38), channel_id=1, source_target_pairs={{24,0},{28,4},{25,1},{29,5},{26,2},{30,6},{27,3},{31,7}} | collective-permute-start | bytes 49160 | tf_op jit(solution)/shard_map/ppermute | solution.py:25

commit v5 on v4

--- a/solution.py
+++ b/solution.py
@@ -25,6 +25,11 @@
     return lax.ppermute(block, "seq", route)
 
 
+def passed_round(block, distance):
+    count = lax.axis_size("seq")
+    return lax.ppermute(block, "seq", [(i, (i + distance) % count) for i in range(count)])
+
+
 def in_three(x):
     high = x.astype(BF16).astype(F32)
     middle = (x - high).astype(BF16).astype(F32)
@@ -48,12 +53,27 @@
 
 
 def own_kernel(
-    heads, q_ref, k_ref, v_ref, g_ref, out_ref, stats_ref, weight_ref, gp_ref, top_ref
+    heads, q_hbm, k_hbm, v_hbm, g_hbm, out_ref, stats_ref, q_ref, k_ref, v_ref, g_ref, sems
 ):
+    group = heads // 4 if heads % 4 == 0 else heads
+    pairs = (q_hbm, q_ref), (k_hbm, k_ref), (v_hbm, v_ref), (g_hbm, g_ref)
+    copies = []
+    for start in range(0, heads, group):
+        part = slice(start * E, (start + group) * E)
+        for source, target in pairs:
+            copies.append(
+                pltpu.make_async_copy(
+                    source.at[:, part], target.at[:, part], sems.at[len(copies)]
+                )
+            )
+            copies[-1].start()
     key = lax.broadcasted_iota(jnp.int32, (B, B), 0)
     query = lax.broadcasted_iota(jnp.int32, (B, B), 1)
     allowed = key <= query
     for h in range(heads):
+        if h % group == 0:
+            for copy in copies[h // group * 4 : h // group * 4 + 4]:
+                copy.wait()
         cols = head_columns(h)
         q, k, v, g = q_ref[:, cols], k_ref[:, cols], v_ref[:, cols], g_ref[:, cols]
         logits = jnp.where(allowed, dot(k, q, ((1,), (1,))) * E**-0.5, MASKED)
@@ -66,8 +86,19 @@
         stats = stat_rows(top + jnp.log(total), inner / total)
         out_ref[B:, cols] = stats
         stats_ref[:, cols] = stats
-        weight_ref[h] = weight
-        gp_ref[h] = grad_probs
+
+
+def own_weights_kernel(heads, q_ref, k_ref, v_ref, g_ref, weight_ref, gp_ref, top_ref):
+    key = lax.broadcasted_iota(jnp.int32, (B, B), 0)
+    query = lax.broadcasted_iota(jnp.int32, (B, B), 1)
+    allowed = key <= query
+    for h in range(heads):
+        cols = head_columns(h)
+        logits = dot(k_ref[:, cols], q_ref[:, cols], ((1,), (1,))) * E**-0.5
+        logits = jnp.where(allowed, logits, MASKED)
+        top = jnp.max(logits, axis=0, keepdims=True)
+        weight_ref[h] = jnp.exp(logits - top)
+        gp_ref[h] = dot(v_ref[:, cols], g_ref[:, cols], ((1,), (1,)))
         top_ref[h : h + 1, :] = top
 
 
@@ -201,16 +232,27 @@
     smem = pl.BlockSpec(memory_space=pltpu.SMEM)
     anywhere = pl.BlockSpec(memory_space=pl.ANY)
 
-    def kernel(function, name, products, inputs, outputs, spec=vmem, scratch=(), scalar=False):
+    def kernel(
+        function,
+        name,
+        products,
+        inputs,
+        outputs,
+        spec=vmem,
+        scratch=(),
+        scalar=False,
+        source=vmem,
+        limit=16 << 20,
+    ):
         out_shape = [jax.ShapeDtypeStruct(shape, kind) for shape, kind in outputs]
         moved = sum(x.size * x.dtype.itemsize for x in (*inputs, *out_shape))
         return pl.pallas_call(
             function,
-            in_specs=[smem] * scalar + [vmem] * (len(inputs) - scalar),
+            in_specs=[smem] * scalar + [source] * (len(inputs) - scalar),
             out_specs=[spec] * len(out_shape),
             out_shape=out_shape,
             scratch_shapes=scratch,
-            compiler_params=pltpu.CompilerParams(vmem_limit_bytes=16 << 20),
+            compiler_params=pltpu.CompilerParams(vmem_limit_bytes=limit),
             cost_estimate=pl.CostEstimate(
                 flops=products * 2 * heads * B * B * E,
                 bytes_accessed=moved,
@@ -220,7 +262,18 @@
         )(*inputs)
 
     rows = jnp.stack([key_vectors[B - 1 :], value_vectors[B - 1 :]])
-    grad_stats, own_stats, weight, grad_probs, top = kernel(
+    across = [(i, i ^ 1) for i in range(count)]
+    swap = lax.ppermute(rows, "seq", across)
+    rows, queries = lax.optimization_barrier((rows, queries))
+    next_q = passed_round(queries, -1)
+    summary = jnp.stack([rows, swap])
+    while 2 * summary.shape[2] < count:
+        earlier = passed_along(summary, 2 * summary.shape[2])
+        summary = jnp.concatenate([summary, earlier], axis=2)
+    pairs = summary.shape[2]
+    padded = -(-2 * pairs // 16) * 16
+    _, grad_out = lax.optimization_barrier((swap, grad_out))
+    grad_stats, own_stats = kernel(
         functools.partial(own_kernel, heads),
         "own",
         2,
@@ -228,24 +281,21 @@
         [
             ((B + STAT_ROWS, features), BF16),
             ((STAT_ROWS, features), BF16),
-            ((heads, B, B), F32),
-            ((heads, B, B), F32),
-            ((heads, B), F32),
         ],
-    )
-
-    across = [(i, i ^ 1) for i in range(count)]
-    swap = lax.ppermute(rows, "seq", across)
-    rows, queries = lax.optimization_barrier((rows, queries))
-    next_q = passed_along(queries, -1)
-    summary = jnp.stack([rows, swap])
-    _, grad_stats = lax.optimization_barrier((swap, grad_stats))
-    while 2 * summary.shape[2] < count:
-        earlier = passed_along(summary, 2 * summary.shape[2])
-        summary = jnp.concatenate([summary, earlier], axis=2)
-    pairs = summary.shape[2]
-    padded = -(-2 * pairs // 16) * 16
+        source=anywhere,
+        limit=None,
+        scratch=[pltpu.VMEM((B, features), BF16)] * 4 + [pltpu.SemaphoreType.DMA((16,))],
+    )
+
     next_g = passed_along(grad_stats, -1)
+    grad_out, next_q = lax.optimization_barrier((grad_out, next_q))
+    weight, grad_probs, top = kernel(
+        functools.partial(own_weights_kernel, heads),
+        "own_weights",
+        2,
+        (queries, key_vectors, value_vectors, grad_out),
+        [((heads, B, B), F32)] * 2 + [((heads, B), F32)],
+    )
 
     wide = heads, B + padded, B
     cross_weight, cross_sums = kernel(

time: 51.9 us -> 49.3 us (0.950)
  local copies, waits for them, and re-layouts: 6.06 us -> 0.9 us
  waiting for transfers between devices: 14.3 us -> 17.1 us
  starting transfers between devices: 23.9 us -> 21.1 us
  Pallas kernels: 6.02 us -> 8.74 us
    unnamed x21 -> x11, local copies, waits for them, and re-layouts: 5.2 us -> 0.04 us
    ppermute x8 -> x7, starting transfers between devices: 20.8 us -> 18.1 us  [passed_along(): return lax.ppermute(block, 'seq', route)]
    pallas_call x6 -> x7, Pallas kernels: 6.02 us -> 8.74 us  [kernel(): pl.pallas_call(function, in_specs=[smem] * scalar + [source] * (len(input...]
    ppermute x1, waiting for transfers between devices: 0.01 us -> 2.1 us  [body(): swap = lax.ppermute(rows, 'seq', across)]
    ppermute x8 -> x7, waiting for transfers between devices: 14.3 us -> 15 us  [passed_along(): return lax.ppermute(block, 'seq', route)]
  transfers between devices with their start and end apart: 10 -> 10, of which waited for: 6 -> 6; matrix products, arithmetic and copies ran while one was open for 1% -> 1% of each run, Pallas kernels for 6% -> 12%
where the time goes in v5:
time: 49.3 us; the launch traced here: 49 us
  starting transfers between devices  21.1 us (43%)
  waiting for transfers between devices  17.1 us (35%)
  Pallas kernels  8.74 us (18%)
  local copies, waits for them, and re-layouts  0.9 us (2%)
  between operations  0.84 us (2%)
    ppermute x7, starting transfers between devices, passed_along(): return lax.ppermute(block, 'seq', route)  18.1 us
    ppermute x7, waiting for transfers between devices, passed_along(): return lax.ppermute(block, 'seq', route)  15 us
    pallas_call x7, Pallas kernels, kernel(): pl.pallas_call(function, in_specs=[smem] * scalar + [source] * (len(input...  8.74 us
    ppermute x1, waiting for transfers between devices, body(): swap = lax.ppermute(rows, 'seq', across)  2.1 us
    ppermute x1, starting transfers between devices, body(): swap = lax.ppermute(rows, 'seq', across)  1.58 us
    ppermute x1, starting transfers between devices, body(): other = lax.ppermute(other, 'seq', across)  1.45 us
  transfers between devices with their start and end apart: 10, of which 6 were waited for; matrix products, arithmetic and copies ran while one was open for 1% of the time, Pallas kernels for 12%

profile of v5, /device:TPU:8, one launch (start us, length us, event | category | flops | bytes accessed | tf_op | source)
XLA Modules:
  0.0 49.0 jit_solution(14476438636436545000)
XLA Ops:
  0.6 0.8 %slice_bitcast_fusion = (bf16[1,1,2048]{2,0,1:T(2,128)(2,1)S(1)}, bf16[1,1,2048]{2,0,1:T(2,128)(2,1)S(1)}) fusion(bf16[128,2048]{1,0:T(8,128)(2,1)} %v_ref.3, bf16[128,2048]{1,0:T(8,128)(2,1)} %k_ref.7), kind=kLoop, calls=%fused_computation.8 | loop fusion | bytes 16384 | tf_op jit(solution)/shard_map/stack | solution.py:264
  1.5 1.6 %collective-permute-start = (bf16[2,1,2048]{2,0,1:T(2,128)(2,1)S(1)}, bf16[2,1,2048]{2,0,1:T(2,128)(2,1)S(1)}, u32[]{:S(2)}, u32[]{:S(2)}) collective-permute-start(bf16[2,1,2048]{2,0,1:T(2,128)(2,1)S(1)} %pad_maximum_fusion.2), channel_id=1, source_target_pairs={{0,4},{4,0},{8,12},{12,8},{16,20},{20,16},{24,28},{28,24},{1,5},{5... | collective-permute-start | bytes 24584 | tf_op jit(solution)/shard_map/ppermute | solution.py:266
  3.0 0.0 collective-permute-start.1
  3.1 0.0 copy-start
  3.1 2.1 %collective-permute-done = bf16[2,1,2048]{2,0,1:T(2,128)(2,1)S(1)} collective-permute-done((bf16[2,1,2048]{2,0,1:T(2,128)(2,1)S(1)}, bf16[2,1,2048]{2,0,1:T(2,128)(2,1)S(1)}, u32[]{:S(2)}, u32[]{:S(2)}) %collective-permute-start) | collective-permute-done | bytes 8224 | tf_op jit(solution)/shard_map/ppermute | solution.py:266
  5.2 3.6 %own.1 = (bf16[136,2048]{1,0:T(8,128)(2,1)}, bf16[8,2048]{1,0:T(8,128)(2,1)}) custom-call(bf16[128,2048]{1,0:T(8,128)(2,1)} %q_ref.1, bf16[128,2048]{1,0:T(8,128)(2,1)} %k_ref.7, bf16[128,2048]{1,0:T(8,128)(2,1)} %v_ref.3, bf16[128,2048]{1,0:T(8,128)(2,1)} %g_ref.1), custom_call_target="tpu_custom_call" | custom-call | flops 134217728 | bytes 2686976 | tf_op jit(solution)/shard_map/own/pallas_call | solution.py:249
  8.8 0.0 copy-start.1
  8.8 3.4 %collective-permute-start.4 = (bf16[136,2048]{1,0:T(8,128)(2,1)}, bf16[136,2048]{1,0:T(8,128)(2,1)S(1)}, u32[]{:S(2)}, u32[]{:S(2)}) collective-permute-start(bf16[136,2048]{1,0:T(8,128)(2,1)} %get-tuple-element.31), channel_id=1, source_target_pairs={{4,0},{8,4},{12,8},{16,12},{20,16},{24,20},{28,24},{5,1},{9,5},{13... | collective-permute-start | bytes 1671176 | tf_op jit(solution)/shard_map/ppermute | solution.py:25
  12.3 3.5 %collective-permute-start.2 = (bf16[2,2,1,2048]{3,2,1,0:T(2,128)(2,1)S(1)}, bf16[2,2,1,2048]{3,2,1,0:T(2,128)(2,1)S(1)}, u32[]{:S(2)}, u32[]{:S(2)}) collective-permute-start(bf16[2,2,1,2048]{3,2,1,0:T(2,128)(2,1)S(1)} %copy_dynamic-update-slice_fusion), channel_id=1, source_target_pairs={{0,8},{4,12},{8,16},{12,20},{16,24},{20,28},{1,9},{5,13},{9,17},{1... | collective-permute-start | bytes 49160 | tf_op jit(solution)/shard_map/ppermute | solution.py:25
  15.8 3.6 %collective-permute-done.2 = bf16[2,2,1,2048]{3,2,1,0:T(2,128)(2,1)S(1)} collective-permute-done((bf16[2,2,1,2048]{3,2,1,0:T(2,128)(2,1)S(1)}, bf16[2,2,1,2048]{3,2,1,0:T(2,128)(2,1)S(1)}, u32[]{:S(2)}, u32[]{:S(2)}) %collective-permute-start.2) | collective-permute-done | bytes 16416 | tf_op jit(solution)/shard_map/ppermute | solution.py:25
  19.4 0.1 pad_maximum_fusion.1
  19.4 4.3 %collective-permute-start.3 = (bf16[2,2,2,2048]{3,2,1,0:T(2,128)(2,1)S(1)}, bf16[2,2,2,2048]{3,2,1,0:T(2,128)(2,1)S(1)}, u32[]{:S(2)}, u32[]{:S(2)}) collective-permute-start(bf16[2,2,2,2048]{3,2,1,0:T(2,128)(2,1)S(1)} %pad_maximum_fusion.1), channel_id=1, source_target_pairs={{0,16},{4,20},{8,24},{12,28},{1,17},{5,21},{9,25},{13,29},{2,18},{... | collective-permute-start | bytes 98312 | tf_op jit(solution)/shard_map/ppermute | solution.py:25
  23.7 1.8 %collective-permute-done.3 = bf16[2,2,2,2048]{3,2,1,0:T(2,128)(2,1)S(1)} collective-permute-done((bf16[2,2,2,2048]{3,2,1,0:T(2,128)(2,1)S(1)}, bf16[2,2,2,2048]{3,2,1,0:T(2,128)(2,1)S(1)}, u32[]{:S(2)}, u32[]{:S(2)}) %collective-permute-start.3) | collective-permute-done | bytes 32800 | tf_op jit(solution)/shard_map/ppermute | solution.py:25
  25.5 0.1 pad_maximum_fusion.summary_ref
  25.6 0.0 collective-permute-done.1.q_ref
  25.6 0.6 %cross_weights.1 = (f32[16,144,128]{2,1,0:T(8,128)S(1)}, f32[32,128]{1,0:T(8,128)S(1)}) custom-call(s32[1]{0:T(128)} %bitcast.place_ref, bf16[128,2048]{1,0:T(8,128)(2,1)S(1)} %collective-permute-done.1.q_ref, bf16[128,2048]{1,0:T(8,128)(2,1)S(1)} %copy-done, bf16[2,2,4,2048]{3,2,1,0:T(4,128)(2,1)S(1)} %pad_maximum_fusion.summary_ref), custom_call_target="tpu_custom_call" | custom-call | flops 67108864 | bytes 2310148 | tf_op jit(solution)/shard_map/cross_weights/pallas_call | solution.py:249
  26.2 2.4 %collective-permute-done.4.g_ref = bf16[136,2048]{1,0:T(8,128)(2,1)S(1)} collective-permute-done((bf16[136,2048]{1,0:T(8,128)(2,1)}, bf16[136,2048]{1,0:T(8,128)(2,1)S(1)}, u32[]{:S(2)}, u32[]{:S(2)}) %collective-permute-start.4) | collective-permute-done | bytes 557088 | tf_op jit(solution)/shard_map/ppermute | solution.py:25
  28.6 0.9 %cross_scores.1 = (bf16[16,144,128]{2,1,0:T(8,128)(2,1)S(1)}, bf16[16,144,128]{2,1,0:T(8,128)(2,1)S(1)}, bf16[8,2048]{1,0:T(8,128)(2,1)S(1)}, f32[2,4,2048]{2,1,0:T(4,128)S(1)}, f32[2,4,2048]{2,1,0:T(4,128)S(1)}) custom-call(bf16[128,2048]{1,0:T(8,128)(2,1)S(1)} %collective-permute-done.1.q_ref, bf16[136,2048]{1,0:T(8,128)(2,1)S(1)} %collective-permute-done.4.g_ref, ...), custom_call_target="tpu_custom_call" | custom-call | flops 134217728 | bytes 4210688 | tf_op jit(solution)/shard_map/cross_scores/pallas_call | solution.py:249
  29.5 1.5 %collective-permute-start.6 = (f32[2,4,2048]{2,1,0:T(4,128)S(1)}, f32[2,4,2048]{2,1,0:T(4,128)S(1)}, u32[]{:S(2)}, u32[]{:S(2)}) collective-permute-start(f32[2,4,2048]{2,1,0:T(4,128)S(1)} %get-tuple-element.40), channel_id=1, source_target_pairs={{0,4},{4,0},{8,12},{12,8},{16,20},{20,16},{24,28},{28,24},{1,5},{5... | collective-permute-start | bytes 196616 | tf_op jit(solution)/shard_map/ppermute | solution.py:322
  31.0 0.5 %cross_queries.1 = bf16[136,2048]{1,0:T(8,128)(2,1)S(1)} custom-call(bf16[128,2048]{1,0:T(8,128)(2,1)S(1)} %copy-done, bf16[2,2,4,2048]{3,2,1,0:T(4,128)(2,1)S(1)} %pad_maximum_fusion.summary_ref, bf16[16,144,128]{2,1,0:T(8,128)(2,1)S(1)} %get-tuple-element.34.grads_ref, bf16[8,2048]{1,0:T(8,128)(2,1)S(1)} %get-tuple-element.35.stats_ref), custom_call_target="tpu_custom_call" | custom-call | flops 67108864 | bytes 1769472 | tf_op jit(solution)/shard_map/cross_queries/pallas_call | solution.py:249
  31.5 2.5 %collective-permute-start.5 = (bf16[136,2048]{1,0:T(8,128)(2,1)S(1)}, bf16[136,2048]{1,0:T(8,128)(2,1)S(1)}, u32[]{:S(2)}, u32[]{:S(2)}) collective-permute-start(bf16[136,2048]{1,0:T(8,128)(2,1)S(1)} %cross_queries.1), channel_id=1, source_target_pairs={{0,4},{4,8},{8,12},{12,16},{16,20},{20,24},{24,28},{1,5},{5,9},{9,... | collective-permute-start | bytes 1671176 | tf_op jit(solution)/shard_map/ppermute | solution.py:25
  34.0 0.0 collective-permute-done.6
  34.1 2.4 %collective-permute-start.7 = (f32[2,1,2048]{2,1,0:T(1,128)S(1)}, f32[2,1,2048]{2,1,0:T(1,128)S(1)}, u32[]{:S(2)}, u32[]{:S(2)}) collective-permute-start(f32[2,1,2048]{2,1,0:T(1,128)S(1)} %get-tuple-element.41), channel_id=1, source_target_pairs={{8,0},{12,4},{16,8},{20,12},{24,16},{28,20},{9,1},{13,5},{17,9},{2... | collective-permute-start | bytes 49160 | tf_op jit(solution)/shard_map/ppermute | solution.py:25
  36.5 0.7 %collective-permute-start.9 = (f32[2,1,2048]{2,1,0:T(1,128)S(1)}, f32[2,1,2048]{2,1,0:T(1,128)S(1)}, u32[]{:S(2)}, u32[]{:S(2)}) collective-permute-start(f32[2,1,2048]{2,1,0:T(1,128)S(1)} %get-tuple-element.42), channel_id=1, source_target_pairs={{24,0},{28,4},{25,1},{29,5},{26,2},{30,6},{27,3},{31,7}} | collective-permute-start | bytes 49160 | tf_op jit(solution)/shard_map/ppermute | solution.py:25
  37.2 1.3 %collective-permute-start.8 = (f32[2,1,2048]{2,1,0:T(1,128)S(1)}, f32[2,1,2048]{2,1,0:T(1,128)S(1)}, u32[]{:S(2)}, u32[]{:S(2)}) collective-permute-start(f32[2,1,2048]{2,1,0:T(1,128)S(1)} %get-tuple-element.43), channel_id=1, source_target_pairs={{16,0},{20,4},{24,8},{28,12},{17,1},{21,5},{25,9},{29,13},{18,2},{... | collective-permute-start | bytes 49160 | tf_op jit(solution)/shard_map/ppermute | solution.py:25
  38.5 0.9 %own_weights.1 = (f32[16,128,128]{2,1,0:T(8,128)S(1)}, f32[16,128,128]{2,1,0:T(8,128)S(1)}, f32[16,128]{1,0:T(8,128)S(1)}) custom-call(bf16[128,2048]{1,0:T(8,128)(2,1)S(1)} %copy-done.2, bf16[128,2048]{1,0:T(8,128)(2,1)S(1)} %copy-done, bf16[128,2048]{1,0:T(8,128)(2,1)S(1)} %copy-done.1, bf16[128,2048]{1,0:T(8,128)(2,1)S(1)} %copy-done.3), custom_call_target="tpu_custom_call" | custom-call | flops 134217728 | bytes 4202496 | tf_op jit(solution)/shard_map/own_weights/pallas_call | solution.py:249
  39.4 0.0 copy-start.4
  39.4 0.4 cross_keys.1
  39.9 0.0 collective-permute-done.9
  39.9 3.8 %collective-permute-done.8 = f32[2,1,2048]{2,1,0:T(1,128)S(1)} collective-permute-done((f32[2,1,2048]{2,1,0:T(1,128)S(1)}, f32[2,1,2048]{2,1,0:T(1,128)S(1)}, u32[]{:S(2)}, u32[]{:S(2)}) %collective-permute-start.8) | collective-permute-done | bytes 16416 | tf_op jit(solution)/shard_map/ppermute | solution.py:25
  43.7 3.4 %collective-permute-done.5.back_ref = bf16[136,2048]{1,0:T(8,128)(2,1)S(1)} collective-permute-done((bf16[136,2048]{1,0:T(8,128)(2,1)S(1)}, bf16[136,2048]{1,0:T(8,128)(2,1)S(1)}, u32[]{:S(2)}, u32[]{:S(2)}) %collective-permute-start.5) | collective-permute-done | bytes 557088 | tf_op jit(solution)/shard_map/ppermute | solution.py:25
  47.2 1.8 %final.1 = (bf16[128,2048]{1,0:T(8,128)(2,1)}, bf16[128,2048]{1,0:T(8,128)(2,1)}, bf16[128,2048]{1,0:T(8,128)(2,1)}) custom-call(s32[1]{0:T(128)} %bitcast.place_ref, bf16[128,2048]{1,0:T(8,128)(2,1)S(1)} %copy-done.2, bf16[128,2048]{1,0:T(8,128)(2,1)S(1)} %copy-done.3, bf16[128,2048]{1,0:T(8,128)(2,1)S(1)} %copy-done, bf16[8,2048]{1,0:T(8,128)(2,1)S(1)} %copy-done.4, ...), custom_call_target="tpu_custom_call" | custom-call | flops 201326592 | bytes 7954436 | tf_op jit(solution)/shard_map/final/pallas_call | solution.py:249
  (14 shorter events, 0.2 us)
Async XLA Ops:
  1.5 3.7 %collective-permute-start = (bf16[2,1,2048]{2,0,1:T(2,128)(2,1)S(1)}, bf16[2,1,2048]{2,0,1:T(2,128)(2,1)S(1)}, u32[]{:S(2)}, u32[]{:S(2)}) collective-permute-start(bf16[2,1,2048]{2,0,1:T(2,128)(2,1)S(1)} %pad_maximum_fusion.2), channel_id=1, source_target_pairs={{0,4},{4,0},{8,12},{12,8},{16,20},{20,16},{24,28},{28,24},{1,5},{5... | collective-permute-start | bytes 24584 | tf_op jit(solution)/shard_map/ppermute | solution.py:266
  3.0 22.6 %collective-permute-start.1 = (bf16[128,2048]{1,0:T(8,128)(2,1)}, bf16[128,2048]{1,0:T(8,128)(2,1)S(1)}, u32[]{:S(2)}, u32[]{:S(2)}) collective-permute-start(bf16[128,2048]{1,0:T(8,128)(2,1)} %q_ref.1), channel_id=1, source_target_pairs={{0,28},{4,0},{8,4},{12,8},{16,12},{20,16},{24,20},{28,24},{1,29},{... | collective-permute-start | bytes 1572872 | tf_op jit(solution)/shard_map/ppermute | solution.py:30
  3.1 22.5 %copy-start = (bf16[128,2048]{1,0:T(8,128)(2,1)S(1)}, bf16[128,2048]{1,0:T(8,128)(2,1)}, u32[]{:S(2)}) copy-start(bf16[128,2048]{1,0:T(8,128)(2,1)} %k_ref.7) | copy-start | bytes 1572868
  8.8 19.8 %copy-start.1 = (bf16[128,2048]{1,0:T(8,128)(2,1)S(1)}, bf16[128,2048]{1,0:T(8,128)(2,1)}, u32[]{:S(2)}) copy-start(bf16[128,2048]{1,0:T(8,128)(2,1)} %v_ref.3) | copy-start | bytes 1572868
  8.8 19.8 %collective-permute-start.4 = (bf16[136,2048]{1,0:T(8,128)(2,1)}, bf16[136,2048]{1,0:T(8,128)(2,1)S(1)}, u32[]{:S(2)}, u32[]{:S(2)}) collective-permute-start(bf16[136,2048]{1,0:T(8,128)(2,1)} %get-tuple-element.31), channel_id=1, source_target_pairs={{4,0},{8,4},{12,8},{16,12},{20,16},{24,20},{28,24},{5,1},{9,5},{13... | collective-permute-start | bytes 1671176 | tf_op jit(solution)/shard_map/ppermute | solution.py:25
  12.3 7.1 %collective-permute-start.2 = (bf16[2,2,1,2048]{3,2,1,0:T(2,128)(2,1)S(1)}, bf16[2,2,1,2048]{3,2,1,0:T(2,128)(2,1)S(1)}, u32[]{:S(2)}, u32[]{:S(2)}) collective-permute-start(bf16[2,2,1,2048]{3,2,1,0:T(2,128)(2,1)S(1)} %copy_dynamic-update-slice_fusion), channel_id=1, source_target_pairs={{0,8},{4,12},{8,16},{12,20},{16,24},{20,28},{1,9},{5,13},{9,17},{1... | collective-permute-start | bytes 49160 | tf_op jit(solution)/shard_map/ppermute | solution.py:25
  19.4 6.0 %collective-permute-start.3 = (bf16[2,2,2,2048]{3,2,1,0:T(2,128)(2,1)S(1)}, bf16[2,2,2,2048]{3,2,1,0:T(2,128)(2,1)S(1)}, u32[]{:S(2)}, u32[]{:S(2)}) collective-permute-start(bf16[2,2,2,2048]{3,2,1,0:T(2,128)(2,1)S(1)} %pad_maximum_fusion.1), channel_id=1, source_target_pairs={{0,16},{4,20},{8,24},{12,28},{1,17},{5,21},{9,25},{13,29},{2,18},{... | collective-permute-start | bytes 98312 | tf_op jit(solution)/shard_map/ppermute | solution.py:25
  29.5 9.0 %copy-start.2 = (bf16[128,2048]{1,0:T(8,128)(2,1)S(1)}, bf16[128,2048]{1,0:T(8,128)(2,1)}, u32[]{:S(2)}) copy-start(bf16[128,2048]{1,0:T(8,128)(2,1)} %q_ref.1) | copy-start | bytes 1572868
  29.5 9.0 %copy-start.3 = (bf16[128,2048]{1,0:T(8,128)(2,1)S(1)}, bf16[128,2048]{1,0:T(8,128)(2,1)}, u32[]{:S(2)}) copy-start(bf16[128,2048]{1,0:T(8,128)(2,1)} %g_ref.1) | copy-start | bytes 1572868
  29.5 4.5 %collective-permute-start.6 = (f32[2,4,2048]{2,1,0:T(4,128)S(1)}, f32[2,4,2048]{2,1,0:T(4,128)S(1)}, u32[]{:S(2)}, u32[]{:S(2)}) collective-permute-start(f32[2,4,2048]{2,1,0:T(4,128)S(1)} %get-tuple-element.40), channel_id=1, source_target_pairs={{0,4},{4,0},{8,12},{12,8},{16,20},{20,16},{24,28},{28,24},{1,5},{5... | collective-permute-start | bytes 196616 | tf_op jit(solution)/shard_map/ppermute | solution.py:322
  31.5 15.7 %collective-permute-start.5 = (bf16[136,2048]{1,0:T(8,128)(2,1)S(1)}, bf16[136,2048]{1,0:T(8,128)(2,1)S(1)}, u32[]{:S(2)}, u32[]{:S(2)}) collective-permute-start(bf16[136,2048]{1,0:T(8,128)(2,1)S(1)} %cross_queries.1), channel_id=1, source_target_pairs={{0,4},{4,8},{8,12},{12,16},{16,20},{20,24},{24,28},{1,5},{5,9},{9,... | collective-permute-start | bytes 1671176 | tf_op jit(solution)/shard_map/ppermute | solution.py:25
  34.1 5.7 %collective-permute-start.7 = (f32[2,1,2048]{2,1,0:T(1,128)S(1)}, f32[2,1,2048]{2,1,0:T(1,128)S(1)}, u32[]{:S(2)}, u32[]{:S(2)}) collective-permute-start(f32[2,1,2048]{2,1,0:T(1,128)S(1)} %get-tuple-element.41), channel_id=1, source_target_pairs={{8,0},{12,4},{16,8},{20,12},{24,16},{28,20},{9,1},{13,5},{17,9},{2... | collective-permute-start | bytes 49160 | tf_op jit(solution)/shard_map/ppermute | solution.py:25
  36.5 3.4 %collective-permute-start.9 = (f32[2,1,2048]{2,1,0:T(1,128)S(1)}, f32[2,1,2048]{2,1,0:T(1,128)S(1)}, u32[]{:S(2)}, u32[]{:S(2)}) collective-permute-start(f32[2,1,2048]{2,1,0:T(1,128)S(1)} %get-tuple-element.42), channel_id=1, source_target_pairs={{24,0},{28,4},{25,1},{29,5},{26,2},{30,6},{27,3},{31,7}} | collective-permute-start | bytes 49160 | tf_op jit(solution)/shard_map/ppermute | solution.py:25
  37.2 6.5 %collective-permute-start.8 = (f32[2,1,2048]{2,1,0:T(1,128)S(1)}, f32[2,1,2048]{2,1,0:T(1,128)S(1)}, u32[]{:S(2)}, u32[]{:S(2)}) collective-permute-start(f32[2,1,2048]{2,1,0:T(1,128)S(1)} %get-tuple-element.43), channel_id=1, source_target_pairs={{16,0},{20,4},{24,8},{28,12},{17,1},{21,5},{25,9},{29,13},{18,2},{... | collective-permute-start | bytes 49160 | tf_op jit(solution)/shard_map/ppermute | solution.py:25
  39.4 7.8 %copy-start.4 = (bf16[8,2048]{1,0:T(8,128)(2,1)S(1)}, bf16[8,2048]{1,0:T(8,128)(2,1)}, u32[]{:S(2)}) copy-start(bf16[8,2048]{1,0:T(8,128)(2,1)} %get-tuple-element.25.own_ref) | copy-start | bytes 98308

commit v6 on v5

--- a/solution.py
+++ b/solution.py
@@ -163,7 +163,7 @@
         grad_v = dot(low_ref[h, B:, :], g_ref[:B, cols], ((1,), (0,)))
         for i, grad in enumerate((grad_k, grad_v)):
             same_ref[i, :, cols] = grad[:pairs]
-            other_ref[i, :, cols] = grad[pairs : 2 * pairs]
+            other_ref[i, :, cols] = grad[pairs : 2 * pairs].astype(BF16)
 
 
 def cross_queries_kernel(heads, padded, k_ref, summary_ref, grads_ref, stats_ref, gq_ref):
@@ -198,26 +198,31 @@
         grads[h] = (probs * (gp_ref[h] - inner)).astype(BF16)
 
     copies = []
-    for h in range(heads):
-        cols = head_columns(h)
-        grad_logits = grads[h]
-        grad_q = scale * dot(grad_logits, k_ref[:, cols], ((0,), (0,)))
-        grad_k = scale * dot(grad_logits, q_ref[:, cols], ((1,), (0,)))
-        grad_v = dot(low[h], g_ref[:, cols], ((1,), (0,)))
-        grad_k += gk_ref[:, cols] + jnp.where(last_row, gs_ref[0, :, cols], 0.0)
-        grad_v += gv_ref[:, cols] + jnp.where(last_row, gs_ref[1, :, cols], 0.0)
-        done_q[:, cols] = (grad_q + back_ref[:B, cols].astype(F32)).astype(BF16)
-        done_k[:, cols] = grad_k.astype(BF16)
-        done_v[:, cols] = grad_v.astype(BF16)
+
+    def put(done, out, h):
         if (h + 1) % group == 0:
             part = slice((h + 1 - group) * E, (h + 1) * E)
-            for done, out in (done_q, out_q_ref), (done_k, out_k_ref), (done_v, out_v_ref):
-                copies.append(
-                    pltpu.make_async_copy(
-                        done.at[:, part], out.at[:, part], sems.at[len(copies)]
-                    )
-                )
-                copies[-1].start()
+            sem = sems.at[len(copies)]
+            copies.append(pltpu.make_async_copy(done.at[:, part], out.at[:, part], sem))
+            copies[-1].start()
+
+    for h in range(heads):
+        cols = head_columns(h)
+        grad_q = scale * dot(grads[h], k_ref[:, cols], ((0,), (0,)))
+        done_q[:, cols] = (grad_q + back_ref[:B, cols].astype(F32)).astype(BF16)
+        put(done_q, out_q_ref, h)
+    for h in range(heads):
+        cols = head_columns(h)
+        grad_k = scale * dot(grads[h], q_ref[:, cols], ((1,), (0,)))
+        grad_k += gk_ref[:, cols] + jnp.where(last_row, gs_ref[0, :, cols], 0.0)
+        done_k[:, cols] = grad_k.astype(BF16)
+        put(done_k, out_k_ref, h)
+    for h in range(heads):
+        cols = head_columns(h)
+        grad_v = dot(low[h], g_ref[:, cols], ((1,), (0,)))
+        grad_v += gv_ref[:, cols] + jnp.where(last_row, gs_ref[1, :, cols], 0.0)
+        done_v[:, cols] = grad_v.astype(BF16)
+        put(done_v, out_v_ref, h)
     for copy in copies:
         copy.wait()
 
@@ -316,7 +321,7 @@
             (wide, BF16),
             ((STAT_ROWS, features), BF16),
             ((2, pairs, features), F32),
-            ((2, pairs, features), F32),
+            ((2, pairs, features), BF16),
         ],
     )
     other = lax.ppermute(other, "seq", across)
@@ -335,7 +340,7 @@
         (next_q, next_g, low, grads),
         [((B, features), F32)] * 2,
     )
-    grad_summary = same + other
+    grad_summary = same + other.astype(F32)
     while pairs > 1:
         ways = 4 if pairs % 4 == 0 else 2
         pairs //= ways

time: 49.3 us -> 49.3 us (level)
  no operation moved by 1% of the time
where the time goes in v6:
time: 49.3 us; the launch traced here: 48.9 us
  starting transfers between devices  21.1 us (43%)
  waiting for transfers between devices  17.1 us (35%)
  Pallas kernels  8.64 us (18%)
  local copies, waits for them, and re-layouts  0.9 us (2%)
  between operations  0.85 us (2%)
    ppermute x7, starting transfers between devices, passed_along(): return lax.ppermute(block, 'seq', route)  18.1 us
    ppermute x7, waiting for transfers between devices, passed_along(): return lax.ppermute(block, 'seq', route)  15 us
    pallas_call x7, Pallas kernels, kernel(): pl.pallas_call(function, in_specs=[smem] * scalar + [source] * (len(input...  8.64 us
    ppermute x1, waiting for transfers between devices, body(): swap = lax.ppermute(rows, 'seq', across)  2.1 us
    ppermute x1, starting transfers between devices, body(): swap = lax.ppermute(rows, 'seq', across)  1.58 us
    ppermute x1, starting transfers between devices, body(): other = lax.ppermute(other, 'seq', across)  1.46 us
  transfers between devices with their start and end apart: 10, of which 6 were waited for; matrix products, arithmetic and copies ran while one was open for 1% of the time, Pallas kernels for 12%

profile of v6, /device:TPU:8, one launch (start us, length us, event | category | flops | bytes accessed | tf_op | source)
XLA Modules:
  0.0 48.9 jit_solution(5515812805929936634)
XLA Ops:
  0.6 0.8 %slice_bitcast_fusion = (bf16[1,1,2048]{2,0,1:T(2,128)(2,1)S(1)}, bf16[1,1,2048]{2,0,1:T(2,128)(2,1)S(1)}) fusion(bf16[128,2048]{1,0:T(8,128)(2,1)} %v_ref.3, bf16[128,2048]{1,0:T(8,128)(2,1)} %k_ref.7), kind=kLoop, calls=%fused_computation.9 | loop fusion | bytes 16384 | tf_op jit(solution)/shard_map/stack | solution.py:269
  1.5 1.6 %collective-permute-start = (bf16[2,1,2048]{2,0,1:T(2,128)(2,1)S(1)}, bf16[2,1,2048]{2,0,1:T(2,128)(2,1)S(1)}, u32[]{:S(2)}, u32[]{:S(2)}) collective-permute-start(bf16[2,1,2048]{2,0,1:T(2,128)(2,1)S(1)} %pad_maximum_fusion.2), channel_id=1, source_target_pairs={{0,4},{4,0},{8,12},{12,8},{16,20},{20,16},{24,28},{28,24},{1,5},{5... | collective-permute-start | bytes 24584 | tf_op jit(solution)/shard_map/ppermute | solution.py:271
  3.0 0.0 collective-permute-start.1
  3.1 0.0 copy-start
  3.1 2.1 %collective-permute-done = bf16[2,1,2048]{2,0,1:T(2,128)(2,1)S(1)} collective-permute-done((bf16[2,1,2048]{2,0,1:T(2,128)(2,1)S(1)}, bf16[2,1,2048]{2,0,1:T(2,128)(2,1)S(1)}, u32[]{:S(2)}, u32[]{:S(2)}) %collective-permute-start) | collective-permute-done | bytes 8224 | tf_op jit(solution)/shard_map/ppermute | solution.py:271
  5.2 3.6 %own.1 = (bf16[136,2048]{1,0:T(8,128)(2,1)}, bf16[8,2048]{1,0:T(8,128)(2,1)}) custom-call(bf16[128,2048]{1,0:T(8,128)(2,1)} %q_ref.1, bf16[128,2048]{1,0:T(8,128)(2,1)} %k_ref.7, bf16[128,2048]{1,0:T(8,128)(2,1)} %v_ref.3, bf16[128,2048]{1,0:T(8,128)(2,1)} %g_ref.1), custom_call_target="tpu_custom_call" | custom-call | flops 134217728 | bytes 2686976 | tf_op jit(solution)/shard_map/own/pallas_call | solution.py:254
  8.8 0.0 copy-start.1
  8.8 3.4 %collective-permute-start.4 = (bf16[136,2048]{1,0:T(8,128)(2,1)}, bf16[136,2048]{1,0:T(8,128)(2,1)S(1)}, u32[]{:S(2)}, u32[]{:S(2)}) collective-permute-start(bf16[136,2048]{1,0:T(8,128)(2,1)} %get-tuple-element.31), channel_id=1, source_target_pairs={{4,0},{8,4},{12,8},{16,12},{20,16},{24,20},{28,24},{5,1},{9,5},{13... | collective-permute-start | bytes 1671176 | tf_op jit(solution)/shard_map/ppermute | solution.py:25
  12.3 3.5 %collective-permute-start.2 = (bf16[2,2,1,2048]{3,2,1,0:T(2,128)(2,1)S(1)}, bf16[2,2,1,2048]{3,2,1,0:T(2,128)(2,1)S(1)}, u32[]{:S(2)}, u32[]{:S(2)}) collective-permute-start(bf16[2,2,1,2048]{3,2,1,0:T(2,128)(2,1)S(1)} %copy_dynamic-update-slice_fusion), channel_id=1, source_target_pairs={{0,8},{4,12},{8,16},{12,20},{16,24},{20,28},{1,9},{5,13},{9,17},{1... | collective-permute-start | bytes 49160 | tf_op jit(solution)/shard_map/ppermute | solution.py:25
  15.8 3.6 %collective-permute-done.2 = bf16[2,2,1,2048]{3,2,1,0:T(2,128)(2,1)S(1)} collective-permute-done((bf16[2,2,1,2048]{3,2,1,0:T(2,128)(2,1)S(1)}, bf16[2,2,1,2048]{3,2,1,0:T(2,128)(2,1)S(1)}, u32[]{:S(2)}, u32[]{:S(2)}) %collective-permute-start.2) | collective-permute-done | bytes 16416 | tf_op jit(solution)/shard_map/ppermute | solution.py:25
  19.4 0.1 pad_maximum_fusion.1
  19.4 4.3 %collective-permute-start.3 = (bf16[2,2,2,2048]{3,2,1,0:T(2,128)(2,1)S(1)}, bf16[2,2,2,2048]{3,2,1,0:T(2,128)(2,1)S(1)}, u32[]{:S(2)}, u32[]{:S(2)}) collective-permute-start(bf16[2,2,2,2048]{3,2,1,0:T(2,128)(2,1)S(1)} %pad_maximum_fusion.1), channel_id=1, source_target_pairs={{0,16},{4,20},{8,24},{12,28},{1,17},{5,21},{9,25},{13,29},{2,18},{... | collective-permute-start | bytes 98312 | tf_op jit(solution)/shard_map/ppermute | solution.py:25
  23.7 1.8 %collective-permute-done.3 = bf16[2,2,2,2048]{3,2,1,0:T(2,128)(2,1)S(1)} collective-permute-done((bf16[2,2,2,2048]{3,2,1,0:T(2,128)(2,1)S(1)}, bf16[2,2,2,2048]{3,2,1,0:T(2,128)(2,1)S(1)}, u32[]{:S(2)}, u32[]{:S(2)}) %collective-permute-start.3) | collective-permute-done | bytes 32800 | tf_op jit(solution)/shard_map/ppermute | solution.py:25
  25.5 0.1 pad_maximum_fusion.summary_ref
  25.6 0.0 collective-permute-done.1.q_ref
  25.6 0.6 %cross_weights.1 = (f32[16,144,128]{2,1,0:T(8,128)S(1)}, f32[32,128]{1,0:T(8,128)S(1)}) custom-call(s32[1]{0:T(128)} %bitcast.place_ref, bf16[128,2048]{1,0:T(8,128)(2,1)S(1)} %collective-permute-done.1.q_ref, bf16[128,2048]{1,0:T(8,128)(2,1)S(1)} %copy-done, bf16[2,2,4,2048]{3,2,1,0:T(4,128)(2,1)S(1)} %pad_maximum_fusion.summary_ref), custom_call_target="tpu_custom_call" | custom-call | flops 67108864 | bytes 2310148 | tf_op jit(solution)/shard_map/cross_weights/pallas_call | solution.py:254
  26.2 2.4 %collective-permute-done.4.g_ref = bf16[136,2048]{1,0:T(8,128)(2,1)S(1)} collective-permute-done((bf16[136,2048]{1,0:T(8,128)(2,1)}, bf16[136,2048]{1,0:T(8,128)(2,1)S(1)}, u32[]{:S(2)}, u32[]{:S(2)}) %collective-permute-start.4) | collective-permute-done | bytes 557088 | tf_op jit(solution)/shard_map/ppermute | solution.py:25
  28.6 0.9 %cross_scores.1 = (bf16[16,144,128]{2,1,0:T(8,128)(2,1)S(1)}, bf16[16,144,128]{2,1,0:T(8,128)(2,1)S(1)}, bf16[8,2048]{1,0:T(8,128)(2,1)S(1)}, f32[2,4,2048]{2,1,0:T(4,128)S(1)}, bf16[2,4,2048]{2,1,0:T(4,128)(2,1)S(1)}) custom-call(bf16[128,2048]{1,0:T(8,128)(2,1)S(1)} %collective-permute-done.1.q_ref, bf16[136,2048]{1,0:T(8,128)(2,1)S(1)} %collective-permute-done.4.g_ref, ...), custom_call_target="tpu_custom_call" | custom-call | flops 134217728 | bytes 4177920 | tf_op jit(solution)/shard_map/cross_scores/pallas_call | solution.py:254
  29.5 1.5 %collective-permute-start.6 = (bf16[2,4,2048]{2,1,0:T(4,128)(2,1)S(1)}, bf16[2,4,2048]{2,1,0:T(4,128)(2,1)S(1)}, u32[]{:S(2)}, u32[]{:S(2)}) collective-permute-start(bf16[2,4,2048]{2,1,0:T(4,128)(2,1)S(1)} %get-tuple-element.40), channel_id=1, source_target_pairs={{0,4},{4,0},{8,12},{12,8},{16,20},{20,16},{24,28},{28,24},{1,5},{5... | collective-permute-start | bytes 98312 | tf_op jit(solution)/shard_map/ppermute | solution.py:327
  31.0 0.5 %cross_queries.1 = bf16[136,2048]{1,0:T(8,128)(2,1)S(1)} custom-call(bf16[128,2048]{1,0:T(8,128)(2,1)S(1)} %copy-done, bf16[2,2,4,2048]{3,2,1,0:T(4,128)(2,1)S(1)} %pad_maximum_fusion.summary_ref, bf16[16,144,128]{2,1,0:T(8,128)(2,1)S(1)} %get-tuple-element.34.grads_ref, bf16[8,2048]{1,0:T(8,128)(2,1)S(1)} %get-tuple-element.35.stats_ref), custom_call_target="tpu_custom_call" | custom-call | flops 67108864 | bytes 1769472 | tf_op jit(solution)/shard_map/cross_queries/pallas_call | solution.py:254
  31.5 2.5 %collective-permute-start.5 = (bf16[136,2048]{1,0:T(8,128)(2,1)S(1)}, bf16[136,2048]{1,0:T(8,128)(2,1)S(1)}, u32[]{:S(2)}, u32[]{:S(2)}) collective-permute-start(bf16[136,2048]{1,0:T(8,128)(2,1)S(1)} %cross_queries.1), channel_id=1, source_target_pairs={{0,4},{4,8},{8,12},{12,16},{16,20},{20,24},{24,28},{1,5},{5,9},{9,... | collective-permute-start | bytes 1671176 | tf_op jit(solution)/shard_map/ppermute | solution.py:25
  34.0 0.0 collective-permute-done.6
  34.1 2.4 %collective-permute-start.7 = (f32[2,1,2048]{2,1,0:T(1,128)S(1)}, f32[2,1,2048]{2,1,0:T(1,128)S(1)}, u32[]{:S(2)}, u32[]{:S(2)}) collective-permute-start(f32[2,1,2048]{2,1,0:T(1,128)S(1)} %get-tuple-element.41), channel_id=1, source_target_pairs={{8,0},{12,4},{16,8},{20,12},{24,16},{28,20},{9,1},{13,5},{17,9},{2... | collective-permute-start | bytes 49160 | tf_op jit(solution)/shard_map/ppermute | solution.py:25
  36.5 0.7 %collective-permute-start.9 = (f32[2,1,2048]{2,1,0:T(1,128)S(1)}, f32[2,1,2048]{2,1,0:T(1,128)S(1)}, u32[]{:S(2)}, u32[]{:S(2)}) collective-permute-start(f32[2,1,2048]{2,1,0:T(1,128)S(1)} %get-tuple-element.42), channel_id=1, source_target_pairs={{24,0},{28,4},{25,1},{29,5},{26,2},{30,6},{27,3},{31,7}} | collective-permute-start | bytes 49160 | tf_op jit(solution)/shard_map/ppermute | solution.py:25
  37.2 1.3 %collective-permute-start.8 = (f32[2,1,2048]{2,1,0:T(1,128)S(1)}, f32[2,1,2048]{2,1,0:T(1,128)S(1)}, u32[]{:S(2)}, u32[]{:S(2)}) collective-permute-start(f32[2,1,2048]{2,1,0:T(1,128)S(1)} %get-tuple-element.43), channel_id=1, source_target_pairs={{16,0},{20,4},{24,8},{28,12},{17,1},{21,5},{25,9},{29,13},{18,2},{... | collective-permute-start | bytes 49160 | tf_op jit(solution)/shard_map/ppermute | solution.py:25
  38.5 0.9 %own_weights.1 = (f32[16,128,128]{2,1,0:T(8,128)S(1)}, f32[16,128,128]{2,1,0:T(8,128)S(1)}, f32[16,128]{1,0:T(8,128)S(1)}) custom-call(bf16[128,2048]{1,0:T(8,128)(2,1)S(1)} %copy-done.2, bf16[128,2048]{1,0:T(8,128)(2,1)S(1)} %copy-done, bf16[128,2048]{1,0:T(8,128)(2,1)S(1)} %copy-done.1, bf16[128,2048]{1,0:T(8,128)(2,1)S(1)} %copy-done.3), custom_call_target="tpu_custom_call" | custom-call | flops 134217728 | bytes 4202496 | tf_op jit(solution)/shard_map/own_weights/pallas_call | solution.py:254
  39.4 0.0 copy-start.4
  39.4 0.4 cross_keys.1
  39.8 0.0 collective-permute-done.7
  39.9 3.8 %collective-permute-done.8 = f32[2,1,2048]{2,1,0:T(1,128)S(1)} collective-permute-done((f32[2,1,2048]{2,1,0:T(1,128)S(1)}, f32[2,1,2048]{2,1,0:T(1,128)S(1)}, u32[]{:S(2)}, u32[]{:S(2)}) %collective-permute-start.8) | collective-permute-done | bytes 16416 | tf_op jit(solution)/shard_map/ppermute | solution.py:25
  43.7 3.4 %collective-permute-done.5.back_ref = bf16[136,2048]{1,0:T(8,128)(2,1)S(1)} collective-permute-done((bf16[136,2048]{1,0:T(8,128)(2,1)S(1)}, bf16[136,2048]{1,0:T(8,128)(2,1)S(1)}, u32[]{:S(2)}, u32[]{:S(2)}) %collective-permute-start.5) | collective-permute-done | bytes 557088 | tf_op jit(solution)/shard_map/ppermute | solution.py:25
  47.2 1.7 %final.1 = (bf16[128,2048]{1,0:T(8,128)(2,1)}, bf16[128,2048]{1,0:T(8,128)(2,1)}, bf16[128,2048]{1,0:T(8,128)(2,1)}) custom-call(s32[1]{0:T(128)} %bitcast.place_ref, bf16[128,2048]{1,0:T(8,128)(2,1)S(1)} %copy-done.2, bf16[128,2048]{1,0:T(8,128)(2,1)S(1)} %copy-done.3, bf16[128,2048]{1,0:T(8,128)(2,1)S(1)} %copy-done, bf16[8,2048]{1,0:T(8,128)(2,1)S(1)} %copy-done.4, ...), custom_call_target="tpu_custom_call" | custom-call | flops 201326592 | bytes 7954436 | tf_op jit(solution)/shard_map/final/pallas_call | solution.py:254
  (14 shorter events, 0.2 us)
Async XLA Ops:
  1.5 3.7 %collective-permute-start = (bf16[2,1,2048]{2,0,1:T(2,128)(2,1)S(1)}, bf16[2,1,2048]{2,0,1:T(2,128)(2,1)S(1)}, u32[]{:S(2)}, u32[]{:S(2)}) collective-permute-start(bf16[2,1,2048]{2,0,1:T(2,128)(2,1)S(1)} %pad_maximum_fusion.2), channel_id=1, source_target_pairs={{0,4},{4,0},{8,12},{12,8},{16,20},{20,16},{24,28},{28,24},{1,5},{5... | collective-permute-start | bytes 24584 | tf_op jit(solution)/shard_map/ppermute | solution.py:271
  3.0 22.6 %collective-permute-start.1 = (bf16[128,2048]{1,0:T(8,128)(2,1)}, bf16[128,2048]{1,0:T(8,128)(2,1)S(1)}, u32[]{:S(2)}, u32[]{:S(2)}) collective-permute-start(bf16[128,2048]{1,0:T(8,128)(2,1)} %q_ref.1), channel_id=1, source_target_pairs={{0,28},{4,0},{8,4},{12,8},{16,12},{20,16},{24,20},{28,24},{1,29},{... | collective-permute-start | bytes 1572872 | tf_op jit(solution)/shard_map/ppermute | solution.py:30
  3.1 22.5 %copy-start = (bf16[128,2048]{1,0:T(8,128)(2,1)S(1)}, bf16[128,2048]{1,0:T(8,128)(2,1)}, u32[]{:S(2)}) copy-start(bf16[128,2048]{1,0:T(8,128)(2,1)} %k_ref.7) | copy-start | bytes 1572868
  8.8 19.8 %copy-start.1 = (bf16[128,2048]{1,0:T(8,128)(2,1)S(1)}, bf16[128,2048]{1,0:T(8,128)(2,1)}, u32[]{:S(2)}) copy-start(bf16[128,2048]{1,0:T(8,128)(2,1)} %v_ref.3) | copy-start | bytes 1572868
  8.8 19.8 %collective-permute-start.4 = (bf16[136,2048]{1,0:T(8,128)(2,1)}, bf16[136,2048]{1,0:T(8,128)(2,1)S(1)}, u32[]{:S(2)}, u32[]{:S(2)}) collective-permute-start(bf16[136,2048]{1,0:T(8,128)(2,1)} %get-tuple-element.31), channel_id=1, source_target_pairs={{4,0},{8,4},{12,8},{16,12},{20,16},{24,20},{28,24},{5,1},{9,5},{13... | collective-permute-start | bytes 1671176 | tf_op jit(solution)/shard_map/ppermute | solution.py:25
  12.3 7.1 %collective-permute-start.2 = (bf16[2,2,1,2048]{3,2,1,0:T(2,128)(2,1)S(1)}, bf16[2,2,1,2048]{3,2,1,0:T(2,128)(2,1)S(1)}, u32[]{:S(2)}, u32[]{:S(2)}) collective-permute-start(bf16[2,2,1,2048]{3,2,1,0:T(2,128)(2,1)S(1)} %copy_dynamic-update-slice_fusion), channel_id=1, source_target_pairs={{0,8},{4,12},{8,16},{12,20},{16,24},{20,28},{1,9},{5,13},{9,17},{1... | collective-permute-start | bytes 49160 | tf_op jit(solution)/shard_map/ppermute | solution.py:25
  19.4 6.0 %collective-permute-start.3 = (bf16[2,2,2,2048]{3,2,1,0:T(2,128)(2,1)S(1)}, bf16[2,2,2,2048]{3,2,1,0:T(2,128)(2,1)S(1)}, u32[]{:S(2)}, u32[]{:S(2)}) collective-permute-start(bf16[2,2,2,2048]{3,2,1,0:T(2,128)(2,1)S(1)} %pad_maximum_fusion.1), channel_id=1, source_target_pairs={{0,16},{4,20},{8,24},{12,28},{1,17},{5,21},{9,25},{13,29},{2,18},{... | collective-permute-start | bytes 98312 | tf_op jit(solution)/shard_map/ppermute | solution.py:25
  29.5 9.0 %copy-start.2 = (bf16[128,2048]{1,0:T(8,128)(2,1)S(1)}, bf16[128,2048]{1,0:T(8,128)(2,1)}, u32[]{:S(2)}) copy-start(bf16[128,2048]{1,0:T(8,128)(2,1)} %q_ref.1) | copy-start | bytes 1572868
  29.5 9.0 %copy-start.3 = (bf16[128,2048]{1,0:T(8,128)(2,1)S(1)}, bf16[128,2048]{1,0:T(8,128)(2,1)}, u32[]{:S(2)}) copy-start(bf16[128,2048]{1,0:T(8,128)(2,1)} %g_ref.1) | copy-start | bytes 1572868
  29.5 4.5 %collective-permute-start.6 = (bf16[2,4,2048]{2,1,0:T(4,128)(2,1)S(1)}, bf16[2,4,2048]{2,1,0:T(4,128)(2,1)S(1)}, u32[]{:S(2)}, u32[]{:S(2)}) collective-permute-start(bf16[2,4,2048]{2,1,0:T(4,128)(2,1)S(1)} %get-tuple-element.40), channel_id=1, source_target_pairs={{0,4},{4,0},{8,12},{12,8},{16,20},{20,16},{24,28},{28,24},{1,5},{5... | collective-permute-start | bytes 98312 | tf_op jit(solution)/shard_map/ppermute | solution.py:327
  31.5 15.7 %collective-permute-start.5 = (bf16[136,2048]{1,0:T(8,128)(2,1)S(1)}, bf16[136,2048]{1,0:T(8,128)(2,1)S(1)}, u32[]{:S(2)}, u32[]{:S(2)}) collective-permute-start(bf16[136,2048]{1,0:T(8,128)(2,1)S(1)} %cross_queries.1), channel_id=1, source_target_pairs={{0,4},{4,8},{8,12},{12,16},{16,20},{20,24},{24,28},{1,5},{5,9},{9,... | collective-permute-start | bytes 1671176 | tf_op jit(solution)/shard_map/ppermute | solution.py:25
  34.1 5.7 %collective-permute-start.7 = (f32[2,1,2048]{2,1,0:T(1,128)S(1)}, f32[2,1,2048]{2,1,0:T(1,128)S(1)}, u32[]{:S(2)}, u32[]{:S(2)}) collective-permute-start(f32[2,1,2048]{2,1,0:T(1,128)S(1)} %get-tuple-element.41), channel_id=1, source_target_pairs={{8,0},{12,4},{16,8},{20,12},{24,16},{28,20},{9,1},{13,5},{17,9},{2... | collective-permute-start | bytes 49160 | tf_op jit(solution)/shard_map/ppermute | solution.py:25
  36.5 3.3 %collective-permute-start.9 = (f32[2,1,2048]{2,1,0:T(1,128)S(1)}, f32[2,1,2048]{2,1,0:T(1,128)S(1)}, u32[]{:S(2)}, u32[]{:S(2)}) collective-permute-start(f32[2,1,2048]{2,1,0:T(1,128)S(1)} %get-tuple-element.42), channel_id=1, source_target_pairs={{24,0},{28,4},{25,1},{29,5},{26,2},{30,6},{27,3},{31,7}} | collective-permute-start | bytes 49160 | tf_op jit(solution)/shard_map/ppermute | solution.py:25
  37.2 6.5 %collective-permute-start.8 = (f32[2,1,2048]{2,1,0:T(1,128)S(1)}, f32[2,1,2048]{2,1,0:T(1,128)S(1)}, u32[]{:S(2)}, u32[]{:S(2)}) collective-permute-start(f32[2,1,2048]{2,1,0:T(1,128)S(1)} %get-tuple-element.43), channel_id=1, source_target_pairs={{16,0},{20,4},{24,8},{28,12},{17,1},{21,5},{25,9},{29,13},{18,2},{... | collective-permute-start | bytes 49160 | tf_op jit(solution)/shard_map/ppermute | solution.py:25
  39.4 7.8 %copy-start.4 = (bf16[8,2048]{1,0:T(8,128)(2,1)S(1)}, bf16[8,2048]{1,0:T(8,128)(2,1)}, u32[]{:S(2)}) copy-start(bf16[8,2048]{1,0:T(8,128)(2,1)} %get-tuple-element.25.own_ref) | copy-start | bytes 98308

commit v7 on v6

--- a/solution.py
+++ b/solution.py
@@ -132,8 +132,8 @@
 
 
 def cross_scores_kernel(
-    heads, padded, q_ref, g_ref, v_ref, summary_ref, weight_ref, sums_ref,
-    low_ref, grads_ref, stats_ref, same_ref, other_ref
+    heads, padded, q_ref, g_ref, k_ref, v_ref, summary_ref, weight_ref, sums_ref,
+    low_ref, grads_ref, same_ref, other_ref, gq_ref
 ):
     pairs = summary_ref.shape[2]
     scale = E**-0.5
@@ -156,7 +156,7 @@
         probs = weight * cross_part
         low_ref[h] = probs.astype(BF16)
         grads_ref[h] = (probs * (grad_probs - inner)).astype(BF16)
-        stats_ref[:, cols] = stat_rows(top + jnp.log(total), inner)
+        gq_ref[B:, cols] = stat_rows(top + jnp.log(total), inner)
     for h in range(heads):
         cols = head_columns(h)
         grad_k = scale * dot(grads_ref[h, B:, :], q_ref[:, cols], ((1,), (0,)))
@@ -164,14 +164,10 @@
         for i, grad in enumerate((grad_k, grad_v)):
             same_ref[i, :, cols] = grad[:pairs]
             other_ref[i, :, cols] = grad[pairs : 2 * pairs].astype(BF16)
-
-
-def cross_queries_kernel(heads, padded, k_ref, summary_ref, grads_ref, stats_ref, gq_ref):
-    gq_ref[B:, :] = stats_ref[...]
     for h in range(heads):
         cols = head_columns(h)
         k = with_summary(k_ref[:, cols], summary_ref, 0, cols, padded)
-        gq_ref[:B, cols] = (E**-0.5 * dot(grads_ref[h], k, ((0,), (0,)))).astype(BF16)
+        gq_ref[:B, cols] = (scale * dot(grads_ref[h], k, ((0,), (0,)))).astype(BF16)
 
 
 def cross_keys_kernel(heads, q_ref, g_ref, low_ref, grads_ref, gk_ref, gv_ref):
@@ -311,27 +307,16 @@
         [(wide, F32), ((2 * heads, B), F32)],
         scalar=True,
     )
-    low, grads, stats, same, other = kernel(
+    low, grads, same, other, grad_q_next = kernel(
         functools.partial(cross_scores_kernel, heads, padded),
         "cross_scores",
-        2,
-        (next_q, next_g, value_vectors, summary, cross_weight, cross_sums),
-        [
-            (wide, BF16),
-            (wide, BF16),
-            ((STAT_ROWS, features), BF16),
-            ((2, pairs, features), F32),
-            ((2, pairs, features), BF16),
-        ],
+        3,
+        (next_q, next_g, key_vectors, value_vectors, summary, cross_weight, cross_sums),
+        [(wide, BF16)] * 2
+        + [((2, pairs, features), F32), ((2, pairs, features), BF16)]
+        + [((B + STAT_ROWS, features), BF16)],
     )
     other = lax.ppermute(other, "seq", across)
-    (grad_q_next,) = kernel(
-        functools.partial(cross_queries_kernel, heads, padded),
-        "cross_queries",
-        1,
-        (key_vectors, summary, grads, stats),
-        [((B + STAT_ROWS, features), BF16)],
-    )
     back = passed_along(grad_q_next, 1)
     grad_k, grad_v = kernel(
         functools.partial(cross_keys_kernel, heads),

time: 49.3 us -> 49.1 us (level)
    pallas_call x7 -> x6, Pallas kernels: 8.64 us -> 8.54 us  [kernel(): pl.pallas_call(function, in_specs=[smem] * scalar + [source] * (len(input...]
  transfers between devices with their start and end apart: 10 -> 10, of which waited for: 6 -> 6; matrix products, arithmetic and copies ran while one was open for 1% -> 1% of each run, Pallas kernels for 12% -> 11%
where the time goes in v7:
time: 49.1 us; the launch traced here: 48.8 us
  starting transfers between devices  21.1 us (43%)
  waiting for transfers between devices  17.1 us (35%)
  Pallas kernels  8.54 us (17%)
  local copies, waits for them, and re-layouts  0.9 us (2%)
  between operations  0.84 us (2%)
    ppermute x7, starting transfers between devices, passed_along(): return lax.ppermute(block, 'seq', route)  18 us
    ppermute x7, waiting for transfers between devices, passed_along(): return lax.ppermute(block, 'seq', route)  15 us
    pallas_call x6, Pallas kernels, kernel(): pl.pallas_call(function, in_specs=[smem] * scalar + [source] * (len(input...  8.54 us
    ppermute x1, waiting for transfers between devices, body(): swap = lax.ppermute(rows, 'seq', across)  2.1 us
    ppermute x1, starting transfers between devices, body(): swap = lax.ppermute(rows, 'seq', across)  1.58 us
    ppermute x1, starting transfers between devices, body(): other = lax.ppermute(other, 'seq', across)  1.47 us
  transfers between devices with their start and end apart: 10, of which 6 were waited for; matrix products, arithmetic and copies ran while one was open for 1% of the time, Pallas kernels for 11%

profile of v7, /device:TPU:8, one launch (start us, length us, event | category | flops | bytes accessed | tf_op | source)
XLA Modules:
  0.0 48.8 jit_solution(13505684565639856538)
XLA Ops:
  0.6 0.8 %slice_bitcast_fusion = (bf16[1,1,2048]{2,0,1:T(2,128)(2,1)S(1)}, bf16[1,1,2048]{2,0,1:T(2,128)(2,1)S(1)}) fusion(bf16[128,2048]{1,0:T(8,128)(2,1)} %v_ref.3, bf16[128,2048]{1,0:T(8,128)(2,1)} %k_ref.7), kind=kLoop, calls=%fused_computation.9 | loop fusion | bytes 16384 | tf_op jit(solution)/shard_map/stack | solution.py:265
  1.5 1.6 %collective-permute-start = (bf16[2,1,2048]{2,0,1:T(2,128)(2,1)S(1)}, bf16[2,1,2048]{2,0,1:T(2,128)(2,1)S(1)}, u32[]{:S(2)}, u32[]{:S(2)}) collective-permute-start(bf16[2,1,2048]{2,0,1:T(2,128)(2,1)S(1)} %pad_maximum_fusion.2), channel_id=1, source_target_pairs={{0,4},{4,0},{8,12},{12,8},{16,20},{20,16},{24,28},{28,24},{1,5},{5... | collective-permute-start | bytes 24584 | tf_op jit(solution)/shard_map/ppermute | solution.py:267
  3.0 0.0 collective-permute-start.1
  3.1 0.0 copy-start
  3.1 2.1 %collective-permute-done = bf16[2,1,2048]{2,0,1:T(2,128)(2,1)S(1)} collective-permute-done((bf16[2,1,2048]{2,0,1:T(2,128)(2,1)S(1)}, bf16[2,1,2048]{2,0,1:T(2,128)(2,1)S(1)}, u32[]{:S(2)}, u32[]{:S(2)}) %collective-permute-start) | collective-permute-done | bytes 8224 | tf_op jit(solution)/shard_map/ppermute | solution.py:267
  5.2 3.6 %own.1 = (bf16[136,2048]{1,0:T(8,128)(2,1)}, bf16[8,2048]{1,0:T(8,128)(2,1)}) custom-call(bf16[128,2048]{1,0:T(8,128)(2,1)} %q_ref.1, bf16[128,2048]{1,0:T(8,128)(2,1)} %k_ref.7, bf16[128,2048]{1,0:T(8,128)(2,1)} %v_ref.3, bf16[128,2048]{1,0:T(8,128)(2,1)} %g_ref.1), custom_call_target="tpu_custom_call" | custom-call | flops 134217728 | bytes 2686976 | tf_op jit(solution)/shard_map/own/pallas_call | solution.py:250
  8.8 0.0 copy-start.1
  8.8 3.4 %collective-permute-start.2 = (bf16[136,2048]{1,0:T(8,128)(2,1)}, bf16[136,2048]{1,0:T(8,128)(2,1)S(1)}, u32[]{:S(2)}, u32[]{:S(2)}) collective-permute-start(bf16[136,2048]{1,0:T(8,128)(2,1)} %get-tuple-element.30), channel_id=1, source_target_pairs={{4,0},{8,4},{12,8},{16,12},{20,16},{24,20},{28,24},{5,1},{9,5},{13... | collective-permute-start | bytes 1671176 | tf_op jit(solution)/shard_map/ppermute | solution.py:25
  12.3 3.5 %collective-permute-start.3 = (bf16[2,2,1,2048]{3,2,1,0:T(2,128)(2,1)S(1)}, bf16[2,2,1,2048]{3,2,1,0:T(2,128)(2,1)S(1)}, u32[]{:S(2)}, u32[]{:S(2)}) collective-permute-start(bf16[2,2,1,2048]{3,2,1,0:T(2,128)(2,1)S(1)} %copy_dynamic-update-slice_fusion), channel_id=1, source_target_pairs={{0,8},{4,12},{8,16},{12,20},{16,24},{20,28},{1,9},{5,13},{9,17},{1... | collective-permute-start | bytes 49160 | tf_op jit(solution)/shard_map/ppermute | solution.py:25
  15.8 3.6 %collective-permute-done.3 = bf16[2,2,1,2048]{3,2,1,0:T(2,128)(2,1)S(1)} collective-permute-done((bf16[2,2,1,2048]{3,2,1,0:T(2,128)(2,1)S(1)}, bf16[2,2,1,2048]{3,2,1,0:T(2,128)(2,1)S(1)}, u32[]{:S(2)}, u32[]{:S(2)}) %collective-permute-start.3) | collective-permute-done | bytes 16416 | tf_op jit(solution)/shard_map/ppermute | solution.py:25
  19.4 0.1 pad_maximum_fusion.1
  19.4 4.3 %collective-permute-start.4 = (bf16[2,2,2,2048]{3,2,1,0:T(2,128)(2,1)S(1)}, bf16[2,2,2,2048]{3,2,1,0:T(2,128)(2,1)S(1)}, u32[]{:S(2)}, u32[]{:S(2)}) collective-permute-start(bf16[2,2,2,2048]{3,2,1,0:T(2,128)(2,1)S(1)} %pad_maximum_fusion.1), channel_id=1, source_target_pairs={{0,16},{4,20},{8,24},{12,28},{1,17},{5,21},{9,25},{13,29},{2,18},{... | collective-permute-start | bytes 98312 | tf_op jit(solution)/shard_map/ppermute | solution.py:25
  23.7 1.8 %collective-permute-done.4 = bf16[2,2,2,2048]{3,2,1,0:T(2,128)(2,1)S(1)} collective-permute-done((bf16[2,2,2,2048]{3,2,1,0:T(2,128)(2,1)S(1)}, bf16[2,2,2,2048]{3,2,1,0:T(2,128)(2,1)S(1)}, u32[]{:S(2)}, u32[]{:S(2)}) %collective-permute-start.4) | collective-permute-done | bytes 32800 | tf_op jit(solution)/shard_map/ppermute | solution.py:25
  25.5 0.1 pad_maximum_fusion.summary_ref
  25.6 0.0 collective-permute-done.1.q_ref
  25.6 0.6 %cross_weights.1 = (f32[16,144,128]{2,1,0:T(8,128)S(1)}, f32[32,128]{1,0:T(8,128)S(1)}) custom-call(s32[1]{0:T(128)} %bitcast.place_ref, bf16[128,2048]{1,0:T(8,128)(2,1)S(1)} %collective-permute-done.1.q_ref, bf16[128,2048]{1,0:T(8,128)(2,1)S(1)} %copy-done, bf16[2,2,4,2048]{3,2,1,0:T(4,128)(2,1)S(1)} %pad_maximum_fusion.summary_ref), custom_call_target="tpu_custom_call" | custom-call | flops 67108864 | bytes 2310148 | tf_op jit(solution)/shard_map/cross_weights/pallas_call | solution.py:250
  26.2 2.4 %collective-permute-done.2.g_ref = bf16[136,2048]{1,0:T(8,128)(2,1)S(1)} collective-permute-done((bf16[136,2048]{1,0:T(8,128)(2,1)}, bf16[136,2048]{1,0:T(8,128)(2,1)S(1)}, u32[]{:S(2)}, u32[]{:S(2)}) %collective-permute-start.2) | collective-permute-done | bytes 557088 | tf_op jit(solution)/shard_map/ppermute | solution.py:25
  28.6 1.3 %cross_scores.1 = (bf16[16,144,128]{2,1,0:T(8,128)(2,1)S(1)}, bf16[16,144,128]{2,1,0:T(8,128)(2,1)S(1)}, f32[2,4,2048]{2,1,0:T(4,128)S(1)}, bf16[2,4,2048]{2,1,0:T(4,128)(2,1)S(1)}, bf16[136,2048]{1,0:T(8,128)(2,1)S(1)}) custom-call(bf16[128,2048]{1,0:T(8,128)(2,1)S(1)} %collective-permute-done.1.q_ref, bf16[136,2048]{1,0:T(8,128)(2,1)S(1)} %collective-permute-done.2.g_ref, ...), custom_call_target="tpu_custom_call" | custom-call | flops 201326592 | bytes 5226496 | tf_op jit(solution)/shard_map/cross_scores/pallas_call | solution.py:250
  29.9 1.5 %collective-permute-start.6 = (bf16[2,4,2048]{2,1,0:T(4,128)(2,1)S(1)}, bf16[2,4,2048]{2,1,0:T(4,128)(2,1)S(1)}, u32[]{:S(2)}, u32[]{:S(2)}) collective-permute-start(bf16[2,4,2048]{2,1,0:T(4,128)(2,1)S(1)} %get-tuple-element.40), channel_id=1, source_target_pairs={{0,4},{4,0},{8,12},{12,8},{16,20},{20,16},{24,28},{28,24},{1,5},{5... | collective-permute-start | bytes 98312 | tf_op jit(solution)/shard_map/ppermute | solution.py:319
  31.4 2.5 %collective-permute-start.5 = (bf16[136,2048]{1,0:T(8,128)(2,1)S(1)}, bf16[136,2048]{1,0:T(8,128)(2,1)S(1)}, u32[]{:S(2)}, u32[]{:S(2)}) collective-permute-start(bf16[136,2048]{1,0:T(8,128)(2,1)S(1)} %get-tuple-element.34), channel_id=1, source_target_pairs={{0,4},{4,8},{8,12},{12,16},{16,20},{20,24},{24,28},{1,5},{5,9},{9,... | collective-permute-start | bytes 1671176 | tf_op jit(solution)/shard_map/ppermute | solution.py:25
  33.9 0.0 collective-permute-done.6
  34.0 2.4 %collective-permute-start.7 = (f32[2,1,2048]{2,1,0:T(1,128)S(1)}, f32[2,1,2048]{2,1,0:T(1,128)S(1)}, u32[]{:S(2)}, u32[]{:S(2)}) collective-permute-start(f32[2,1,2048]{2,1,0:T(1,128)S(1)} %get-tuple-element.41), channel_id=1, source_target_pairs={{8,0},{12,4},{16,8},{20,12},{24,16},{28,20},{9,1},{13,5},{17,9},{2... | collective-permute-start | bytes 49160 | tf_op jit(solution)/shard_map/ppermute | solution.py:25
  36.4 0.7 %collective-permute-start.9 = (f32[2,1,2048]{2,1,0:T(1,128)S(1)}, f32[2,1,2048]{2,1,0:T(1,128)S(1)}, u32[]{:S(2)}, u32[]{:S(2)}) collective-permute-start(f32[2,1,2048]{2,1,0:T(1,128)S(1)} %get-tuple-element.42), channel_id=1, source_target_pairs={{24,0},{28,4},{25,1},{29,5},{26,2},{30,6},{27,3},{31,7}} | collective-permute-start | bytes 49160 | tf_op jit(solution)/shard_map/ppermute | solution.py:25
  37.0 1.3 %collective-permute-start.8 = (f32[2,1,2048]{2,1,0:T(1,128)S(1)}, f32[2,1,2048]{2,1,0:T(1,128)S(1)}, u32[]{:S(2)}, u32[]{:S(2)}) collective-permute-start(f32[2,1,2048]{2,1,0:T(1,128)S(1)} %get-tuple-element.43), channel_id=1, source_target_pairs={{16,0},{20,4},{24,8},{28,12},{17,1},{21,5},{25,9},{29,13},{18,2},{... | collective-permute-start | bytes 49160 | tf_op jit(solution)/shard_map/ppermute | solution.py:25
  38.4 0.9 %own_weights.1 = (f32[16,128,128]{2,1,0:T(8,128)S(1)}, f32[16,128,128]{2,1,0:T(8,128)S(1)}, f32[16,128]{1,0:T(8,128)S(1)}) custom-call(bf16[128,2048]{1,0:T(8,128)(2,1)S(1)} %copy-done.2, bf16[128,2048]{1,0:T(8,128)(2,1)S(1)} %copy-done, bf16[128,2048]{1,0:T(8,128)(2,1)S(1)} %copy-done.1, bf16[128,2048]{1,0:T(8,128)(2,1)S(1)} %copy-done.3), custom_call_target="tpu_custom_call" | custom-call | flops 134217728 | bytes 4202496 | tf_op jit(solution)/shard_map/own_weights/pallas_call | solution.py:250
  39.2 0.0 copy-start.4
  39.3 0.4 cross_keys.1
  39.7 0.0 collective-permute-done.7
  39.7 0.0 collective-permute-done.9
  39.7 3.9 %collective-permute-done.8 = f32[2,1,2048]{2,1,0:T(1,128)S(1)} collective-permute-done((f32[2,1,2048]{2,1,0:T(1,128)S(1)}, f32[2,1,2048]{2,1,0:T(1,128)S(1)}, u32[]{:S(2)}, u32[]{:S(2)}) %collective-permute-start.8) | collective-permute-done | bytes 16416 | tf_op jit(solution)/shard_map/ppermute | solution.py:25
  43.6 3.4 %collective-permute-done.5.back_ref = bf16[136,2048]{1,0:T(8,128)(2,1)S(1)} collective-permute-done((bf16[136,2048]{1,0:T(8,128)(2,1)S(1)}, bf16[136,2048]{1,0:T(8,128)(2,1)S(1)}, u32[]{:S(2)}, u32[]{:S(2)}) %collective-permute-start.5) | collective-permute-done | bytes 557088 | tf_op jit(solution)/shard_map/ppermute | solution.py:25
  47.0 1.7 %final.1 = (bf16[128,2048]{1,0:T(8,128)(2,1)}, bf16[128,2048]{1,0:T(8,128)(2,1)}, bf16[128,2048]{1,0:T(8,128)(2,1)}) custom-call(s32[1]{0:T(128)} %bitcast.place_ref, bf16[128,2048]{1,0:T(8,128)(2,1)S(1)} %copy-done.2, bf16[128,2048]{1,0:T(8,128)(2,1)S(1)} %copy-done.3, bf16[128,2048]{1,0:T(8,128)(2,1)S(1)} %copy-done, bf16[8,2048]{1,0:T(8,128)(2,1)S(1)} %copy-done.4, ...), custom_call_target="tpu_custom_call" | custom-call | flops 201326592 | bytes 7954436 | tf_op jit(solution)/shard_map/final/pallas_call | solution.py:250
  (13 shorter events, 0.2 us)
Async XLA Ops:
  1.5 3.7 %collective-permute-start = (bf16[2,1,2048]{2,0,1:T(2,128)(2,1)S(1)}, bf16[2,1,2048]{2,0,1:T(2,128)(2,1)S(1)}, u32[]{:S(2)}, u32[]{:S(2)}) collective-permute-start(bf16[2,1,2048]{2,0,1:T(2,128)(2,1)S(1)} %pad_maximum_fusion.2), channel_id=1, source_target_pairs={{0,4},{4,0},{8,12},{12,8},{16,20},{20,16},{24,28},{28,24},{1,5},{5... | collective-permute-start | bytes 24584 | tf_op jit(solution)/shard_map/ppermute | solution.py:267
  3.0 22.6 %collective-permute-start.1 = (bf16[128,2048]{1,0:T(8,128)(2,1)}, bf16[128,2048]{1,0:T(8,128)(2,1)S(1)}, u32[]{:S(2)}, u32[]{:S(2)}) collective-permute-start(bf16[128,2048]{1,0:T(8,128)(2,1)} %q_ref.1), channel_id=1, source_target_pairs={{0,28},{4,0},{8,4},{12,8},{16,12},{20,16},{24,20},{28,24},{1,29},{... | collective-permute-start | bytes 1572872 | tf_op jit(solution)/shard_map/ppermute | solution.py:30
  3.1 22.5 %copy-start = (bf16[128,2048]{1,0:T(8,128)(2,1)S(1)}, bf16[128,2048]{1,0:T(8,128)(2,1)}, u32[]{:S(2)}) copy-start(bf16[128,2048]{1,0:T(8,128)(2,1)} %k_ref.7) | copy-start | bytes 1572868
  8.8 19.8 %copy-start.1 = (bf16[128,2048]{1,0:T(8,128)(2,1)S(1)}, bf16[128,2048]{1,0:T(8,128)(2,1)}, u32[]{:S(2)}) copy-start(bf16[128,2048]{1,0:T(8,128)(2,1)} %v_ref.3) | copy-start | bytes 1572868
  8.8 19.8 %collective-permute-start.2 = (bf16[136,2048]{1,0:T(8,128)(2,1)}, bf16[136,2048]{1,0:T(8,128)(2,1)S(1)}, u32[]{:S(2)}, u32[]{:S(2)}) collective-permute-start(bf16[136,2048]{1,0:T(8,128)(2,1)} %get-tuple-element.30), channel_id=1, source_target_pairs={{4,0},{8,4},{12,8},{16,12},{20,16},{24,20},{28,24},{5,1},{9,5},{13... | collective-permute-start | bytes 1671176 | tf_op jit(solution)/shard_map/ppermute | solution.py:25
  12.3 7.1 %collective-permute-start.3 = (bf16[2,2,1,2048]{3,2,1,0:T(2,128)(2,1)S(1)}, bf16[2,2,1,2048]{3,2,1,0:T(2,128)(2,1)S(1)}, u32[]{:S(2)}, u32[]{:S(2)}) collective-permute-start(bf16[2,2,1,2048]{3,2,1,0:T(2,128)(2,1)S(1)} %copy_dynamic-update-slice_fusion), channel_id=1, source_target_pairs={{0,8},{4,12},{8,16},{12,20},{16,24},{20,28},{1,9},{5,13},{9,17},{1... | collective-permute-start | bytes 49160 | tf_op jit(solution)/shard_map/ppermute | solution.py:25
  19.4 6.0 %collective-permute-start.4 = (bf16[2,2,2,2048]{3,2,1,0:T(2,128)(2,1)S(1)}, bf16[2,2,2,2048]{3,2,1,0:T(2,128)(2,1)S(1)}, u32[]{:S(2)}, u32[]{:S(2)}) collective-permute-start(bf16[2,2,2,2048]{3,2,1,0:T(2,128)(2,1)S(1)} %pad_maximum_fusion.1), channel_id=1, source_target_pairs={{0,16},{4,20},{8,24},{12,28},{1,17},{5,21},{9,25},{13,29},{2,18},{... | collective-permute-start | bytes 98312 | tf_op jit(solution)/shard_map/ppermute | solution.py:25
  28.6 9.8 %copy-start.2 = (bf16[128,2048]{1,0:T(8,128)(2,1)S(1)}, bf16[128,2048]{1,0:T(8,128)(2,1)}, u32[]{:S(2)}) copy-start(bf16[128,2048]{1,0:T(8,128)(2,1)} %q_ref.1) | copy-start | bytes 1572868
  28.6 9.8 %copy-start.3 = (bf16[128,2048]{1,0:T(8,128)(2,1)S(1)}, bf16[128,2048]{1,0:T(8,128)(2,1)}, u32[]{:S(2)}) copy-start(bf16[128,2048]{1,0:T(8,128)(2,1)} %g_ref.1) | copy-start | bytes 1572868
  29.9 4.0 %collective-permute-start.6 = (bf16[2,4,2048]{2,1,0:T(4,128)(2,1)S(1)}, bf16[2,4,2048]{2,1,0:T(4,128)(2,1)S(1)}, u32[]{:S(2)}, u32[]{:S(2)}) collective-permute-start(bf16[2,4,2048]{2,1,0:T(4,128)(2,1)S(1)} %get-tuple-element.40), channel_id=1, source_target_pairs={{0,4},{4,0},{8,12},{12,8},{16,20},{20,16},{24,28},{28,24},{1,5},{5... | collective-permute-start | bytes 98312 | tf_op jit(solution)/shard_map/ppermute | solution.py:319
  31.4 15.7 %collective-permute-start.5 = (bf16[136,2048]{1,0:T(8,128)(2,1)S(1)}, bf16[136,2048]{1,0:T(8,128)(2,1)S(1)}, u32[]{:S(2)}, u32[]{:S(2)}) collective-permute-start(bf16[136,2048]{1,0:T(8,128)(2,1)S(1)} %get-tuple-element.34), channel_id=1, source_target_pairs={{0,4},{4,8},{8,12},{12,16},{16,20},{20,24},{24,28},{1,5},{5,9},{9,... | collective-permute-start | bytes 1671176 | tf_op jit(solution)/shard_map/ppermute | solution.py:25
  34.0 5.7 %collective-permute-start.7 = (f32[2,1,2048]{2,1,0:T(1,128)S(1)}, f32[2,1,2048]{2,1,0:T(1,128)S(1)}, u32[]{:S(2)}, u32[]{:S(2)}) collective-permute-start(f32[2,1,2048]{2,1,0:T(1,128)S(1)} %get-tuple-element.41), channel_id=1, source_target_pairs={{8,0},{12,4},{16,8},{20,12},{24,16},{28,20},{9,1},{13,5},{17,9},{2... | collective-permute-start | bytes 49160 | tf_op jit(solution)/shard_map/ppermute | solution.py:25
  36.4 3.3 %collective-permute-start.9 = (f32[2,1,2048]{2,1,0:T(1,128)S(1)}, f32[2,1,2048]{2,1,0:T(1,128)S(1)}, u32[]{:S(2)}, u32[]{:S(2)}) collective-permute-start(f32[2,1,2048]{2,1,0:T(1,128)S(1)} %get-tuple-element.42), channel_id=1, source_target_pairs={{24,0},{28,4},{25,1},{29,5},{26,2},{30,6},{27,3},{31,7}} | collective-permute-start | bytes 49160 | tf_op jit(solution)/shard_map/ppermute | solution.py:25
  37.0 6.5 %collective-permute-start.8 = (f32[2,1,2048]{2,1,0:T(1,128)S(1)}, f32[2,1,2048]{2,1,0:T(1,128)S(1)}, u32[]{:S(2)}, u32[]{:S(2)}) collective-permute-start(f32[2,1,2048]{2,1,0:T(1,128)S(1)} %get-tuple-element.43), channel_id=1, source_target_pairs={{16,0},{20,4},{24,8},{28,12},{17,1},{21,5},{25,9},{29,13},{18,2},{... | collective-permute-start | bytes 49160 | tf_op jit(solution)/shard_map/ppermute | solution.py:25
  39.2 7.8 %copy-start.4 = (bf16[8,2048]{1,0:T(8,128)(2,1)S(1)}, bf16[8,2048]{1,0:T(8,128)(2,1)}, u32[]{:S(2)}) copy-start(bf16[8,2048]{1,0:T(8,128)(2,1)} %get-tuple-element.25.own_ref) | copy-start | bytes 98308

commit v8 on v7

--- a/solution.py
+++ b/solution.py
@@ -184,7 +184,7 @@
 ):
     first = place_ref[0] == 0
     scale = E**-0.5
-    group = heads // 4 if heads % 4 == 0 else heads
+    group = heads // 8 if heads % 8 == 0 else heads
     last_row = lax.broadcasted_iota(jnp.int32, (B, B), 0) == B - 1
     for h in range(heads):
         cols = head_columns(h)
@@ -359,7 +359,7 @@
             pltpu.VMEM((B, features), BF16),
             pltpu.VMEM((B, features), BF16),
             pltpu.VMEM((B, features), BF16),
-            pltpu.SemaphoreType.DMA((12,)),
+            pltpu.SemaphoreType.DMA((24,)),
         ],
         scalar=True,
     )

time: 49.1 us -> 49.2 us (level)
  no operation moved by 1% of the time
where the time goes in v8:
time: 49.2 us; the launch traced here: 48.9 us
  starting transfers between devices  21.1 us (43%)
  waiting for transfers between devices  17.1 us (35%)
  Pallas kernels  8.62 us (18%)
  local copies, waits for them, and re-layouts  0.9 us (2%)
  between operations  0.84 us (2%)
    ppermute x7, starting transfers between devices, passed_along(): return lax.ppermute(block, 'seq', route)  18 us
    ppermute x7, waiting for transfers between devices, passed_along(): return lax.ppermute(block, 'seq', route)  15 us
    pallas_call x6, Pallas kernels, kernel(): pl.pallas_call(function, in_specs=[smem] * scalar + [source] * (len(input...  8.62 us
    ppermute x1, waiting for transfers between devices, body(): swap = lax.ppermute(rows, 'seq', across)  2.1 us
    ppermute x1, starting transfers between devices, body(): swap = lax.ppermute(rows, 'seq', across)  1.58 us
    ppermute x1, starting transfers between devices, body(): other = lax.ppermute(other, 'seq', across)  1.47 us
  transfers between devices with their start and end apart: 10, of which 6 were waited for; matrix products, arithmetic and copies ran while one was open for 1% of the time, Pallas kernels for 11%

profile of v8, /device:TPU:8, one launch (start us, length us, event | category | flops | bytes accessed | tf_op | source)
XLA Modules:
  0.0 48.9 jit_solution(11948507567182819496)
XLA Ops:
  0.6 0.8 %slice_bitcast_fusion = (bf16[1,1,2048]{2,0,1:T(2,128)(2,1)S(1)}, bf16[1,1,2048]{2,0,1:T(2,128)(2,1)S(1)}) fusion(bf16[128,2048]{1,0:T(8,128)(2,1)} %v_ref.3, bf16[128,2048]{1,0:T(8,128)(2,1)} %k_ref.7), kind=kLoop, calls=%fused_computation.9 | loop fusion | bytes 16384 | tf_op jit(solution)/shard_map/stack | solution.py:265
  1.5 1.6 %collective-permute-start = (bf16[2,1,2048]{2,0,1:T(2,128)(2,1)S(1)}, bf16[2,1,2048]{2,0,1:T(2,128)(2,1)S(1)}, u32[]{:S(2)}, u32[]{:S(2)}) collective-permute-start(bf16[2,1,2048]{2,0,1:T(2,128)(2,1)S(1)} %pad_maximum_fusion.2), channel_id=1, source_target_pairs={{0,4},{4,0},{8,12},{12,8},{16,20},{20,16},{24,28},{28,24},{1,5},{5... | collective-permute-start | bytes 24584 | tf_op jit(solution)/shard_map/ppermute | solution.py:267
  3.0 0.0 collective-permute-start.1
  3.1 0.0 copy-start
  3.1 2.1 %collective-permute-done = bf16[2,1,2048]{2,0,1:T(2,128)(2,1)S(1)} collective-permute-done((bf16[2,1,2048]{2,0,1:T(2,128)(2,1)S(1)}, bf16[2,1,2048]{2,0,1:T(2,128)(2,1)S(1)}, u32[]{:S(2)}, u32[]{:S(2)}) %collective-permute-start) | collective-permute-done | bytes 8224 | tf_op jit(solution)/shard_map/ppermute | solution.py:267
  5.2 3.6 %own.1 = (bf16[136,2048]{1,0:T(8,128)(2,1)}, bf16[8,2048]{1,0:T(8,128)(2,1)}) custom-call(bf16[128,2048]{1,0:T(8,128)(2,1)} %q_ref.1, bf16[128,2048]{1,0:T(8,128)(2,1)} %k_ref.7, bf16[128,2048]{1,0:T(8,128)(2,1)} %v_ref.3, bf16[128,2048]{1,0:T(8,128)(2,1)} %g_ref.1), custom_call_target="tpu_custom_call" | custom-call | flops 134217728 | bytes 2686976 | tf_op jit(solution)/shard_map/own/pallas_call | solution.py:250
  8.8 0.0 copy-start.1
  8.8 3.4 %collective-permute-start.2 = (bf16[136,2048]{1,0:T(8,128)(2,1)}, bf16[136,2048]{1,0:T(8,128)(2,1)S(1)}, u32[]{:S(2)}, u32[]{:S(2)}) collective-permute-start(bf16[136,2048]{1,0:T(8,128)(2,1)} %get-tuple-element.30), channel_id=1, source_target_pairs={{4,0},{8,4},{12,8},{16,12},{20,16},{24,20},{28,24},{5,1},{9,5},{13... | collective-permute-start | bytes 1671176 | tf_op jit(solution)/shard_map/ppermute | solution.py:25
  12.3 3.5 %collective-permute-start.3 = (bf16[2,2,1,2048]{3,2,1,0:T(2,128)(2,1)S(1)}, bf16[2,2,1,2048]{3,2,1,0:T(2,128)(2,1)S(1)}, u32[]{:S(2)}, u32[]{:S(2)}) collective-permute-start(bf16[2,2,1,2048]{3,2,1,0:T(2,128)(2,1)S(1)} %copy_dynamic-update-slice_fusion), channel_id=1, source_target_pairs={{0,8},{4,12},{8,16},{12,20},{16,24},{20,28},{1,9},{5,13},{9,17},{1... | collective-permute-start | bytes 49160 | tf_op jit(solution)/shard_map/ppermute | solution.py:25
  15.8 3.6 %collective-permute-done.3 = bf16[2,2,1,2048]{3,2,1,0:T(2,128)(2,1)S(1)} collective-permute-done((bf16[2,2,1,2048]{3,2,1,0:T(2,128)(2,1)S(1)}, bf16[2,2,1,2048]{3,2,1,0:T(2,128)(2,1)S(1)}, u32[]{:S(2)}, u32[]{:S(2)}) %collective-permute-start.3) | collective-permute-done | bytes 16416 | tf_op jit(solution)/shard_map/ppermute | solution.py:25
  19.4 0.1 pad_maximum_fusion.1
  19.4 4.3 %collective-permute-start.4 = (bf16[2,2,2,2048]{3,2,1,0:T(2,128)(2,1)S(1)}, bf16[2,2,2,2048]{3,2,1,0:T(2,128)(2,1)S(1)}, u32[]{:S(2)}, u32[]{:S(2)}) collective-permute-start(bf16[2,2,2,2048]{3,2,1,0:T(2,128)(2,1)S(1)} %pad_maximum_fusion.1), channel_id=1, source_target_pairs={{0,16},{4,20},{8,24},{12,28},{1,17},{5,21},{9,25},{13,29},{2,18},{... | collective-permute-start | bytes 98312 | tf_op jit(solution)/shard_map/ppermute | solution.py:25
  23.7 1.8 %collective-permute-done.4 = bf16[2,2,2,2048]{3,2,1,0:T(2,128)(2,1)S(1)} collective-permute-done((bf16[2,2,2,2048]{3,2,1,0:T(2,128)(2,1)S(1)}, bf16[2,2,2,2048]{3,2,1,0:T(2,128)(2,1)S(1)}, u32[]{:S(2)}, u32[]{:S(2)}) %collective-permute-start.4) | collective-permute-done | bytes 32800 | tf_op jit(solution)/shard_map/ppermute | solution.py:25
  25.5 0.1 pad_maximum_fusion.summary_ref
  25.6 0.0 collective-permute-done.1.q_ref
  25.6 0.6 %cross_weights.1 = (f32[16,144,128]{2,1,0:T(8,128)S(1)}, f32[32,128]{1,0:T(8,128)S(1)}) custom-call(s32[1]{0:T(128)} %bitcast.place_ref, bf16[128,2048]{1,0:T(8,128)(2,1)S(1)} %collective-permute-done.1.q_ref, bf16[128,2048]{1,0:T(8,128)(2,1)S(1)} %copy-done, bf16[2,2,4,2048]{3,2,1,0:T(4,128)(2,1)S(1)} %pad_maximum_fusion.summary_ref), custom_call_target="tpu_custom_call" | custom-call | flops 67108864 | bytes 2310148 | tf_op jit(solution)/shard_map/cross_weights/pallas_call | solution.py:250
  26.2 2.4 %collective-permute-done.2.g_ref = bf16[136,2048]{1,0:T(8,128)(2,1)S(1)} collective-permute-done((bf16[136,2048]{1,0:T(8,128)(2,1)}, bf16[136,2048]{1,0:T(8,128)(2,1)S(1)}, u32[]{:S(2)}, u32[]{:S(2)}) %collective-permute-start.2) | collective-permute-done | bytes 557088 | tf_op jit(solution)/shard_map/ppermute | solution.py:25
  28.6 1.3 %cross_scores.1 = (bf16[16,144,128]{2,1,0:T(8,128)(2,1)S(1)}, bf16[16,144,128]{2,1,0:T(8,128)(2,1)S(1)}, f32[2,4,2048]{2,1,0:T(4,128)S(1)}, bf16[2,4,2048]{2,1,0:T(4,128)(2,1)S(1)}, bf16[136,2048]{1,0:T(8,128)(2,1)S(1)}) custom-call(bf16[128,2048]{1,0:T(8,128)(2,1)S(1)} %collective-permute-done.1.q_ref, bf16[136,2048]{1,0:T(8,128)(2,1)S(1)} %collective-permute-done.2.g_ref, ...), custom_call_target="tpu_custom_call" | custom-call | flops 201326592 | bytes 5226496 | tf_op jit(solution)/shard_map/cross_scores/pallas_call | solution.py:250
  29.9 1.5 %collective-permute-start.6 = (bf16[2,4,2048]{2,1,0:T(4,128)(2,1)S(1)}, bf16[2,4,2048]{2,1,0:T(4,128)(2,1)S(1)}, u32[]{:S(2)}, u32[]{:S(2)}) collective-permute-start(bf16[2,4,2048]{2,1,0:T(4,128)(2,1)S(1)} %get-tuple-element.40), channel_id=1, source_target_pairs={{0,4},{4,0},{8,12},{12,8},{16,20},{20,16},{24,28},{28,24},{1,5},{5... | collective-permute-start | bytes 98312 | tf_op jit(solution)/shard_map/ppermute | solution.py:319
  31.4 2.5 %collective-permute-start.5 = (bf16[136,2048]{1,0:T(8,128)(2,1)S(1)}, bf16[136,2048]{1,0:T(8,128)(2,1)S(1)}, u32[]{:S(2)}, u32[]{:S(2)}) collective-permute-start(bf16[136,2048]{1,0:T(8,128)(2,1)S(1)} %get-tuple-element.34), channel_id=1, source_target_pairs={{0,4},{4,8},{8,12},{12,16},{16,20},{20,24},{24,28},{1,5},{5,9},{9,... | collective-permute-start | bytes 1671176 | tf_op jit(solution)/shard_map/ppermute | solution.py:25
  33.9 0.0 collective-permute-done.6
  34.0 2.4 %collective-permute-start.7 = (f32[2,1,2048]{2,1,0:T(1,128)S(1)}, f32[2,1,2048]{2,1,0:T(1,128)S(1)}, u32[]{:S(2)}, u32[]{:S(2)}) collective-permute-start(f32[2,1,2048]{2,1,0:T(1,128)S(1)} %get-tuple-element.41), channel_id=1, source_target_pairs={{8,0},{12,4},{16,8},{20,12},{24,16},{28,20},{9,1},{13,5},{17,9},{2... | collective-permute-start | bytes 49160 | tf_op jit(solution)/shard_map/ppermute | solution.py:25
  36.4 0.7 %collective-permute-start.9 = (f32[2,1,2048]{2,1,0:T(1,128)S(1)}, f32[2,1,2048]{2,1,0:T(1,128)S(1)}, u32[]{:S(2)}, u32[]{:S(2)}) collective-permute-start(f32[2,1,2048]{2,1,0:T(1,128)S(1)} %get-tuple-element.42), channel_id=1, source_target_pairs={{24,0},{28,4},{25,1},{29,5},{26,2},{30,6},{27,3},{31,7}} | collective-permute-start | bytes 49160 | tf_op jit(solution)/shard_map/ppermute | solution.py:25
  37.0 1.3 %collective-permute-start.8 = (f32[2,1,2048]{2,1,0:T(1,128)S(1)}, f32[2,1,2048]{2,1,0:T(1,128)S(1)}, u32[]{:S(2)}, u32[]{:S(2)}) collective-permute-start(f32[2,1,2048]{2,1,0:T(1,128)S(1)} %get-tuple-element.43), channel_id=1, source_target_pairs={{16,0},{20,4},{24,8},{28,12},{17,1},{21,5},{25,9},{29,13},{18,2},{... | collective-permute-start | bytes 49160 | tf_op jit(solution)/shard_map/ppermute | solution.py:25
  38.4 0.9 %own_weights.1 = (f32[16,128,128]{2,1,0:T(8,128)S(1)}, f32[16,128,128]{2,1,0:T(8,128)S(1)}, f32[16,128]{1,0:T(8,128)S(1)}) custom-call(bf16[128,2048]{1,0:T(8,128)(2,1)S(1)} %copy-done.2, bf16[128,2048]{1,0:T(8,128)(2,1)S(1)} %copy-done, bf16[128,2048]{1,0:T(8,128)(2,1)S(1)} %copy-done.1, bf16[128,2048]{1,0:T(8,128)(2,1)S(1)} %copy-done.3), custom_call_target="tpu_custom_call" | custom-call | flops 134217728 | bytes 4202496 | tf_op jit(solution)/shard_map/own_weights/pallas_call | solution.py:250
  39.2 0.0 copy-start.4
  39.3 0.4 cross_keys.1
  39.7 0.0 collective-permute-done.7
  39.7 0.0 collective-permute-done.9
  39.7 3.9 %collective-permute-done.8 = f32[2,1,2048]{2,1,0:T(1,128)S(1)} collective-permute-done((f32[2,1,2048]{2,1,0:T(1,128)S(1)}, f32[2,1,2048]{2,1,0:T(1,128)S(1)}, u32[]{:S(2)}, u32[]{:S(2)}) %collective-permute-start.8) | collective-permute-done | bytes 16416 | tf_op jit(solution)/shard_map/ppermute | solution.py:25
  43.6 3.4 %collective-permute-done.5.back_ref = bf16[136,2048]{1,0:T(8,128)(2,1)S(1)} collective-permute-done((bf16[136,2048]{1,0:T(8,128)(2,1)S(1)}, bf16[136,2048]{1,0:T(8,128)(2,1)S(1)}, u32[]{:S(2)}, u32[]{:S(2)}) %collective-permute-start.5) | collective-permute-done | bytes 557088 | tf_op jit(solution)/shard_map/ppermute | solution.py:25
  47.0 1.8 %final.1 = (bf16[128,2048]{1,0:T(8,128)(2,1)}, bf16[128,2048]{1,0:T(8,128)(2,1)}, bf16[128,2048]{1,0:T(8,128)(2,1)}) custom-call(s32[1]{0:T(128)} %bitcast.place_ref, bf16[128,2048]{1,0:T(8,128)(2,1)S(1)} %copy-done.2, bf16[128,2048]{1,0:T(8,128)(2,1)S(1)} %copy-done.3, bf16[128,2048]{1,0:T(8,128)(2,1)S(1)} %copy-done, bf16[8,2048]{1,0:T(8,128)(2,1)S(1)} %copy-done.4, ...), custom_call_target="tpu_custom_call" | custom-call | flops 201326592 | bytes 7954436 | tf_op jit(solution)/shard_map/final/pallas_call | solution.py:250
  (13 shorter events, 0.2 us)
Async XLA Ops:
  1.5 3.7 %collective-permute-start = (bf16[2,1,2048]{2,0,1:T(2,128)(2,1)S(1)}, bf16[2,1,2048]{2,0,1:T(2,128)(2,1)S(1)}, u32[]{:S(2)}, u32[]{:S(2)}) collective-permute-start(bf16[2,1,2048]{2,0,1:T(2,128)(2,1)S(1)} %pad_maximum_fusion.2), channel_id=1, source_target_pairs={{0,4},{4,0},{8,12},{12,8},{16,20},{20,16},{24,28},{28,24},{1,5},{5... | collective-permute-start | bytes 24584 | tf_op jit(solution)/shard_map/ppermute | solution.py:267
  3.0 22.6 %collective-permute-start.1 = (bf16[128,2048]{1,0:T(8,128)(2,1)}, bf16[128,2048]{1,0:T(8,128)(2,1)S(1)}, u32[]{:S(2)}, u32[]{:S(2)}) collective-permute-start(bf16[128,2048]{1,0:T(8,128)(2,1)} %q_ref.1), channel_id=1, source_target_pairs={{0,28},{4,0},{8,4},{12,8},{16,12},{20,16},{24,20},{28,24},{1,29},{... | collective-permute-start | bytes 1572872 | tf_op jit(solution)/shard_map/ppermute | solution.py:30
  3.1 22.5 %copy-start = (bf16[128,2048]{1,0:T(8,128)(2,1)S(1)}, bf16[128,2048]{1,0:T(8,128)(2,1)}, u32[]{:S(2)}) copy-start(bf16[128,2048]{1,0:T(8,128)(2,1)} %k_ref.7) | copy-start | bytes 1572868
  8.8 19.8 %copy-start.1 = (bf16[128,2048]{1,0:T(8,128)(2,1)S(1)}, bf16[128,2048]{1,0:T(8,128)(2,1)}, u32[]{:S(2)}) copy-start(bf16[128,2048]{1,0:T(8,128)(2,1)} %v_ref.3) | copy-start | bytes 1572868
  8.8 19.8 %collective-permute-start.2 = (bf16[136,2048]{1,0:T(8,128)(2,1)}, bf16[136,2048]{1,0:T(8,128)(2,1)S(1)}, u32[]{:S(2)}, u32[]{:S(2)}) collective-permute-start(bf16[136,2048]{1,0:T(8,128)(2,1)} %get-tuple-element.30), channel_id=1, source_target_pairs={{4,0},{8,4},{12,8},{16,12},{20,16},{24,20},{28,24},{5,1},{9,5},{13... | collective-permute-start | bytes 1671176 | tf_op jit(solution)/shard_map/ppermute | solution.py:25
  12.3 7.1 %collective-permute-start.3 = (bf16[2,2,1,2048]{3,2,1,0:T(2,128)(2,1)S(1)}, bf16[2,2,1,2048]{3,2,1,0:T(2,128)(2,1)S(1)}, u32[]{:S(2)}, u32[]{:S(2)}) collective-permute-start(bf16[2,2,1,2048]{3,2,1,0:T(2,128)(2,1)S(1)} %copy_dynamic-update-slice_fusion), channel_id=1, source_target_pairs={{0,8},{4,12},{8,16},{12,20},{16,24},{20,28},{1,9},{5,13},{9,17},{1... | collective-permute-start | bytes 49160 | tf_op jit(solution)/shard_map/ppermute | solution.py:25
  19.4 6.0 %collective-permute-start.4 = (bf16[2,2,2,2048]{3,2,1,0:T(2,128)(2,1)S(1)}, bf16[2,2,2,2048]{3,2,1,0:T(2,128)(2,1)S(1)}, u32[]{:S(2)}, u32[]{:S(2)}) collective-permute-start(bf16[2,2,2,2048]{3,2,1,0:T(2,128)(2,1)S(1)} %pad_maximum_fusion.1), channel_id=1, source_target_pairs={{0,16},{4,20},{8,24},{12,28},{1,17},{5,21},{9,25},{13,29},{2,18},{... | collective-permute-start | bytes 98312 | tf_op jit(solution)/shard_map/ppermute | solution.py:25
  28.6 9.8 %copy-start.2 = (bf16[128,2048]{1,0:T(8,128)(2,1)S(1)}, bf16[128,2048]{1,0:T(8,128)(2,1)}, u32[]{:S(2)}) copy-start(bf16[128,2048]{1,0:T(8,128)(2,1)} %q_ref.1) | copy-start | bytes 1572868
  28.6 9.8 %copy-start.3 = (bf16[128,2048]{1,0:T(8,128)(2,1)S(1)}, bf16[128,2048]{1,0:T(8,128)(2,1)}, u32[]{:S(2)}) copy-start(bf16[128,2048]{1,0:T(8,128)(2,1)} %g_ref.1) | copy-start | bytes 1572868
  29.9 4.0 %collective-permute-start.6 = (bf16[2,4,2048]{2,1,0:T(4,128)(2,1)S(1)}, bf16[2,4,2048]{2,1,0:T(4,128)(2,1)S(1)}, u32[]{:S(2)}, u32[]{:S(2)}) collective-permute-start(bf16[2,4,2048]{2,1,0:T(4,128)(2,1)S(1)} %get-tuple-element.40), channel_id=1, source_target_pairs={{0,4},{4,0},{8,12},{12,8},{16,20},{20,16},{24,28},{28,24},{1,5},{5... | collective-permute-start | bytes 98312 | tf_op jit(solution)/shard_map/ppermute | solution.py:319
  31.4 15.7 %collective-permute-start.5 = (bf16[136,2048]{1,0:T(8,128)(2,1)S(1)}, bf16[136,2048]{1,0:T(8,128)(2,1)S(1)}, u32[]{:S(2)}, u32[]{:S(2)}) collective-permute-start(bf16[136,2048]{1,0:T(8,128)(2,1)S(1)} %get-tuple-element.34), channel_id=1, source_target_pairs={{0,4},{4,8},{8,12},{12,16},{16,20},{20,24},{24,28},{1,5},{5,9},{9,... | collective-permute-start | bytes 1671176 | tf_op jit(solution)/shard_map/ppermute | solution.py:25
  34.0 5.7 %collective-permute-start.7 = (f32[2,1,2048]{2,1,0:T(1,128)S(1)}, f32[2,1,2048]{2,1,0:T(1,128)S(1)}, u32[]{:S(2)}, u32[]{:S(2)}) collective-permute-start(f32[2,1,2048]{2,1,0:T(1,128)S(1)} %get-tuple-element.41), channel_id=1, source_target_pairs={{8,0},{12,4},{16,8},{20,12},{24,16},{28,20},{9,1},{13,5},{17,9},{2... | collective-permute-start | bytes 49160 | tf_op jit(solution)/shard_map/ppermute | solution.py:25
  36.4 3.3 %collective-permute-start.9 = (f32[2,1,2048]{2,1,0:T(1,128)S(1)}, f32[2,1,2048]{2,1,0:T(1,128)S(1)}, u32[]{:S(2)}, u32[]{:S(2)}) collective-permute-start(f32[2,1,2048]{2,1,0:T(1,128)S(1)} %get-tuple-element.42), channel_id=1, source_target_pairs={{24,0},{28,4},{25,1},{29,5},{26,2},{30,6},{27,3},{31,7}} | collective-permute-start | bytes 49160 | tf_op jit(solution)/shard_map/ppermute | solution.py:25
  37.0 6.5 %collective-permute-start.8 = (f32[2,1,2048]{2,1,0:T(1,128)S(1)}, f32[2,1,2048]{2,1,0:T(1,128)S(1)}, u32[]{:S(2)}, u32[]{:S(2)}) collective-permute-start(f32[2,1,2048]{2,1,0:T(1,128)S(1)} %get-tuple-element.43), channel_id=1, source_target_pairs={{16,0},{20,4},{24,8},{28,12},{17,1},{21,5},{25,9},{29,13},{18,2},{... | collective-permute-start | bytes 49160 | tf_op jit(solution)/shard_map/ppermute | solution.py:25
  39.2 7.8 %copy-start.4 = (bf16[8,2048]{1,0:T(8,128)(2,1)S(1)}, bf16[8,2048]{1,0:T(8,128)(2,1)}, u32[]{:S(2)}) copy-start(bf16[8,2048]{1,0:T(8,128)(2,1)} %get-tuple-element.25.own_ref) | copy-start | bytes 98308
